TPU v7x, 512 devices: a whole 4x8x8 slice. The times are simulated.
512 devices in a mesh: ctx: 128 (over y, z, core), head: 4 (over x).
Axes of the slice: x: 4, y: 8, z: 8, core: 2. Of those that a mesh axis runs over, the one named last changes fastest.
Arguments:
- queries: bfloat16 [32768, 2048], P('ctx', 'head'), may hold values from -120 to 120
- keys: bfloat16 [32768, 128], P('ctx'), may hold values from -20 to 20
- values: bfloat16 [32768, 128], P('ctx'), may hold values from -6 to 6
- grad_out: bfloat16 [32768, 2048], P('ctx', 'head'), may hold values from -6 to 6
- doc_of_block: int32 [128], replicated, may hold values from 0 to 31, never falling along the last dimension, each value on 1 to 8 neighbouring positions
- pair_list: int32 [128, 7], P('ctx'), may hold values from 0 to 7, as said below
- knock: int32 [16, 128], P('head'), may hold values 0 or 1
Outputs:
- d_queries: bfloat16 [32768, 2048], P('ctx', 'head')
- d_keys: bfloat16 [32768, 128], P('ctx')
- d_values: bfloat16 [32768, 128], P('ctx')
Inputs may be any that keep to these rules, and one draw needn't show every extreme that they name: `pair_list`: row b holds distinct offsets from 1 to 7 in its first entries and 0 in the rest; some row holds all 7 offsets; an offset that reaches before block 0 names no block. `doc_of_block`: never falls along the blocks; each document covers 1 to 8 whole blocks, one exactly 8.
All inputs are finite; a program needn't handle non-finite values. No bound on the sum of `knock` on one device may be relied on, other than what follows from the above.
Results may differ from a plain program's by a relative error of at most 0.01.
Values may be sent and summed in bfloat16 or wider, within the bound.
No kernel may reach another device: no remote copies, remote signals or barrier semaphores. Data moves between devices by JAX's collectives and lax.ppermute only.
A program may use at most 128 MiB of HBM per device.

v0:
```python
import jax
import jax.numpy as jnp
from jax import lax
from jax.sharding import PartitionSpec as P

NEG = -1e30


def from_behind(array, axis, by):
    size = lax.axis_size(axis)
    pairs = [(i, i + by) for i in range(size) if 0 <= i + by < size]
    return lax.ppermute(array, axis, pairs)


def local(queries, keys, values, grad_out, doc_of_block, pair_list, knock):
    rows = keys.shape[0]
    width = keys.shape[1]
    local_heads = queries.shape[1] // width
    reach = pair_list.shape[1] + 1
    blocks = doc_of_block.shape[0]
    scale = width ** (-0.5)
    here = lax.axis_index("ctx")
    query_heads = queries.reshape(rows, local_heads, width)
    grad_heads = grad_out.reshape(rows, local_heads, width)
    packed = jnp.concatenate([keys, values], axis=1)
    lower = jnp.arange(rows)[:, None] >= jnp.arange(rows)[None, :]
    own_doc = lax.dynamic_index_in_dim(doc_of_block, here, 0, keepdims=False)

    def tile_mask(offset):
        if offset == 0:
            return jnp.broadcast_to(lower[None], (local_heads, rows, rows))
        source = here - offset
        clipped = jnp.clip(source, 0, blocks - 1)
        listed = jnp.any(pair_list[0] == offset)
        same_doc = lax.dynamic_index_in_dim(doc_of_block, clipped, 0, keepdims=False) == own_doc
        keeping = lax.dynamic_index_in_dim(knock, clipped, 1, keepdims=False) == 1
        allowed = (source >= 0) & listed & same_doc & keeping
        return jnp.broadcast_to(allowed[:, None, None], (local_heads, rows, rows))

    tiles = [packed]
    current = packed
    for offset in range(1, reach):
        current = from_behind(current, "ctx", 1)
        tiles.append(current)
    top = jnp.full((local_heads, rows, 1), NEG, jnp.float32)
    total = jnp.zeros((local_heads, rows, 1), jnp.float32)
    weighted = jnp.zeros((local_heads, rows, 1), jnp.float32)
    kept = []
    masks = []
    for offset in range(reach):
        mask = tile_mask(offset)
        masks.append(mask)
        first_tile = tiles[offset]
        raw = (
            jnp.einsum(
                "ihd,jd->hij",
                query_heads,
                first_tile[:, :width],
                preferred_element_type=jnp.float32,
            )
            * scale
        )
        scores = jnp.where(mask, raw, NEG)
        grad_probs = jnp.einsum(
            "ihd,jd->hij", grad_heads, first_tile[:, width:], preferred_element_type=jnp.float32
        )
        new_top = jnp.maximum(top, jnp.max(scores, axis=2, keepdims=True))
        factor = jnp.exp(top - new_top)
        shifted = jnp.exp(scores - new_top)
        new_total = total * factor + jnp.sum(shifted, axis=2, keepdims=True)
        new_weighted = weighted * factor + jnp.sum(shifted * grad_probs, axis=2, keepdims=True)
        scores, grad_probs, top, total, weighted = (
            scores,
            grad_probs,
            new_top,
            new_total,
            new_weighted,
        )
        kept.append((scores, grad_probs))
    log_total = top + jnp.log(total)
    delta = weighted / total

    def grad_step(tile, scores, grad_probs, query_sum):
        probs = jnp.exp(scores - log_total)
        grad_scores = probs * (grad_probs - delta)
        probs_low = probs.astype(jnp.bfloat16)
        grad_low = grad_scores.astype(jnp.bfloat16)
        query_add = jnp.einsum(
            "hij,jd->ihd", grad_low, tile[:, :width], preferred_element_type=jnp.float32
        )
        key_part = (
            jnp.einsum("hij,ihd->jd", grad_low, query_heads, preferred_element_type=jnp.float32)
            * scale
        )
        value_part = jnp.einsum(
            "hij,ihd->jd", probs_low, grad_heads, preferred_element_type=jnp.float32
        )
        return (query_sum + query_add, jnp.concatenate([key_part, value_part], axis=1))

    def grad_tile(offset, query_sum):
        scores, grad_probs = kept[offset]
        return grad_step(tiles[offset], scores, grad_probs, query_sum)

    query_sum = jnp.zeros((rows, local_heads, width), jnp.float32)
    carried = None
    for offset in reversed(range(reach)):
        query_sum, term = grad_tile(offset, query_sum)
        if carried is None:
            carried = term
        else:
            carried = (
                from_behind(carried.astype(jnp.bfloat16), "ctx", -1).astype(carried.dtype) + term
            )
    result = lax.psum(carried, "head").astype(jnp.bfloat16)
    d_queries = (query_sum * scale).reshape(rows, local_heads * width).astype(jnp.bfloat16)
    return (d_queries, result[:, :width], result[:, width:])


def solution(mesh):
    in_specs = (
        P("ctx", "head"),
        P("ctx", None),
        P("ctx", None),
        P("ctx", "head"),
        P(),
        P("ctx", None),
        P("head", None),
    )
    out_specs = (P("ctx", "head"), P("ctx", None), P("ctx", None))
    return jax.shard_map(local, mesh=mesh, in_specs=in_specs, out_specs=out_specs, check_vma=False)
```

profile of v0, /device:TPU:32, one launch (start us, length us, event | category | flops | bytes accessed | tf_op | source)
XLA Modules:
  0.0 178.6 jit_solution(8060086629659866876)
XLA Ops:
  0.6 0.9 pad_maximum_fusion
  1.6 1.9 %collective-permute-start = (bf16[256,256]{1,0:T(8,128)(2,1)S(1)}, bf16[256,256]{1,0:T(8,128)(2,1)S(1)}, u32[]{:S(2)}, u32[]{:S(2)}) collective-permute-start(bf16[256,256]{1,0:T(8,128)(2,1)S(1)} %pad_maximum_fusion), channel_id=1, source_target_pairs={{0,4},{4,8},{8,12},{12,16},{16,20},{20,24},{24,28},{28,32},{32,36}... | collective-permute-start | bytes 393224 | tf_op jit(solution)/shard_map/ppermute | solution.py:12
  3.6 0.6 copy-done.17
  4.2 0.7 fusion.100
  13.2 0.8 compare_reduce_fusion
  14.2 0.8 copy-done.14
  20.2 4.4 %collective-permute-start.1 = (bf16[256,256]{1,0:T(8,128)(2,1)S(1)}, bf16[256,256]{1,0:T(8,128)(2,1)S(1)}, u32[]{:S(2)}, u32[]{:S(2)}) collective-permute-start(bf16[256,256]{1,0:T(8,128)(2,1)S(1)} %collective-permute-done), channel_id=1, source_target_pairs={{0,4},{4,8},{8,12},{12,16},{16,20},{20,24},{24,28},{28,32},{32,36}... | collective-permute-start | bytes 393224 | tf_op jit(solution)/shard_map/ppermute | solution.py:12
  24.9 8.2 %collective-permute-done.1 = bf16[256,256]{1,0:T(8,128)(2,1)S(1)} collective-permute-done((bf16[256,256]{1,0:T(8,128)(2,1)S(1)}, bf16[256,256]{1,0:T(8,128)(2,1)S(1)}, u32[]{:S(2)}, u32[]{:S(2)}) %collective-permute-start.1) | collective-permute-done | bytes 131104 | tf_op jit(solution)/shard_map/ppermute | solution.py:12
  33.2 1.9 %collective-permute-start.2 = (bf16[256,256]{1,0:T(8,128)(2,1)S(1)}, bf16[256,256]{1,0:T(8,128)(2,1)S(1)}, u32[]{:S(2)}, u32[]{:S(2)}) collective-permute-start(bf16[256,256]{1,0:T(8,128)(2,1)S(1)} %collective-permute-done.1), channel_id=1, source_target_pairs={{0,4},{4,8},{8,12},{12,16},{16,20},{20,24},{24,28},{28,32},{32,36}... | collective-permute-start | bytes 393224 | tf_op jit(solution)/shard_map/ppermute | solution.py:12
  35.4 7.4 %collective-permute-done.2 = bf16[256,256]{1,0:T(8,128)(2,1)S(1)} collective-permute-done((bf16[256,256]{1,0:T(8,128)(2,1)S(1)}, bf16[256,256]{1,0:T(8,128)(2,1)S(1)}, u32[]{:S(2)}, u32[]{:S(2)}) %collective-permute-start.2) | collective-permute-done | bytes 131104 | tf_op jit(solution)/shard_map/ppermute | solution.py:12
  42.8 1.9 %collective-permute-start.3 = (bf16[256,256]{1,0:T(8,128)(2,1)S(1)}, bf16[256,256]{1,0:T(8,128)(2,1)S(1)}, u32[]{:S(2)}, u32[]{:S(2)}) collective-permute-start(bf16[256,256]{1,0:T(8,128)(2,1)S(1)} %collective-permute-done.2), channel_id=1, source_target_pairs={{0,4},{4,8},{8,12},{12,16},{16,20},{20,24},{24,28},{28,32},{32,36}... | collective-permute-start | bytes 393224 | tf_op jit(solution)/shard_map/ppermute | solution.py:12
  45.0 7.4 %collective-permute-done.3 = bf16[256,256]{1,0:T(8,128)(2,1)S(1)} collective-permute-done((bf16[256,256]{1,0:T(8,128)(2,1)S(1)}, bf16[256,256]{1,0:T(8,128)(2,1)S(1)}, u32[]{:S(2)}, u32[]{:S(2)}) %collective-permute-start.3) | collective-permute-done | bytes 131104 | tf_op jit(solution)/shard_map/ppermute | solution.py:12
  52.3 1.9 %collective-permute-start.4 = (bf16[256,256]{1,0:T(8,128)(2,1)S(1)}, bf16[256,256]{1,0:T(8,128)(2,1)S(1)}, u32[]{:S(2)}, u32[]{:S(2)}) collective-permute-start(bf16[256,256]{1,0:T(8,128)(2,1)S(1)} %collective-permute-done.3), channel_id=1, source_target_pairs={{0,4},{4,8},{8,12},{12,16},{16,20},{20,24},{24,28},{28,32},{32,36}... | collective-permute-start | bytes 393224 | tf_op jit(solution)/shard_map/ppermute | solution.py:12
  54.6 7.4 %collective-permute-done.4 = bf16[256,256]{1,0:T(8,128)(2,1)S(1)} collective-permute-done((bf16[256,256]{1,0:T(8,128)(2,1)S(1)}, bf16[256,256]{1,0:T(8,128)(2,1)S(1)}, u32[]{:S(2)}, u32[]{:S(2)}) %collective-permute-start.4) | collective-permute-done | bytes 131104 | tf_op jit(solution)/shard_map/ppermute | solution.py:12
  61.9 1.9 %collective-permute-start.5 = (bf16[256,256]{1,0:T(8,128)(2,1)S(1)}, bf16[256,256]{1,0:T(8,128)(2,1)S(1)}, u32[]{:S(2)}, u32[]{:S(2)}) collective-permute-start(bf16[256,256]{1,0:T(8,128)(2,1)S(1)} %collective-permute-done.4), channel_id=1, source_target_pairs={{0,4},{4,8},{8,12},{12,16},{16,20},{20,24},{24,28},{28,32},{32,36}... | collective-permute-start | bytes 393224 | tf_op jit(solution)/shard_map/ppermute | solution.py:12
  64.2 7.4 %collective-permute-done.5 = bf16[256,256]{1,0:T(8,128)(2,1)S(1)} collective-permute-done((bf16[256,256]{1,0:T(8,128)(2,1)S(1)}, bf16[256,256]{1,0:T(8,128)(2,1)S(1)}, u32[]{:S(2)}, u32[]{:S(2)}) %collective-permute-start.5) | collective-permute-done | bytes 131104 | tf_op jit(solution)/shard_map/ppermute | solution.py:12
  71.5 1.9 %collective-permute-start.6 = (bf16[256,256]{1,0:T(8,128)(2,1)S(1)}, bf16[256,256]{1,0:T(8,128)(2,1)S(1)}, u32[]{:S(2)}, u32[]{:S(2)}) collective-permute-start(bf16[256,256]{1,0:T(8,128)(2,1)S(1)} %collective-permute-done.5), channel_id=1, source_target_pairs={{0,4},{4,8},{8,12},{12,16},{16,20},{20,24},{24,28},{28,32},{32,36}... | collective-permute-start | bytes 393224 | tf_op jit(solution)/shard_map/ppermute | solution.py:12
  73.8 7.4 %collective-permute-done.6 = bf16[256,256]{1,0:T(8,128)(2,1)S(1)} collective-permute-done((bf16[256,256]{1,0:T(8,128)(2,1)S(1)}, bf16[256,256]{1,0:T(8,128)(2,1)S(1)}, u32[]{:S(2)}, u32[]{:S(2)}) %collective-permute-start.6) | collective-permute-done | bytes 131104 | tf_op jit(solution)/shard_map/ppermute | solution.py:12
  81.5 0.8 copy-done.15
  84.9 0.3 fusion.34
  85.3 1.9 %multiply_convert_fusion.7 = (bf16[4,256,256]{1,2,0:T(8,128)(2,1)S(1)}, bf16[4,256,256]{1,2,0:T(8,128)(2,1)S(1)}, bf16[4,256,256]{1,2,0:T(8,128)(2,1)S(1)}, bf16...) fusion(f32[4,256,256]{1,2,0:T(8,128)S(1)} %get-tuple-element.80, ...), kind=kLoop, calls=%fused_computation.83 | loop fusion | flops 8388608 | bytes 20979712 | tf_op jit(solution)/shard_map/convert_element_type | solution.py:87
  88.1 1.0 fusion.26
  91.9 0.6 copy-done.12
  92.8 0.4 fusion.24
  93.2 0.8 copy.74
  94.1 2.1 %collective-permute-start.7 = (bf16[256,256]{0,1:T(8,128)(2,1)S(1)}, bf16[256,256]{0,1:T(8,128)(2,1)S(1)}, u32[]{:S(2)}, u32[]{:S(2)}) collective-permute-start(bf16[256,256]{0,1:T(8,128)(2,1)S(1)} %pad_maximum_fusion.1), channel_id=1, source_target_pairs={{4,0},{8,4},{12,8},{16,12},{20,16},{24,20},{28,24},{32,28},{36,32}... | collective-permute-start | bytes 393224 | tf_op jit(solution)/shard_map/ppermute | solution.py:12
  96.1 1.5 convolution_bitcast_fusion.21
  97.7 0.9 collective-permute-done.7
  98.7 7.2 %collective-permute-start.8 = (bf16[256,256]{0,1:T(8,128)(2,1)S(1)}, bf16[256,256]{0,1:T(8,128)(2,1)S(1)}, u32[]{:S(2)}, u32[]{:S(2)}) collective-permute-start(bf16[256,256]{0,1:T(8,128)(2,1)S(1)} %fusion.67), channel_id=1, source_target_pairs={{4,0},{8,4},{12,8},{16,12},{20,16},{24,20},{28,24},{32,28},{36,32}... | collective-permute-start | bytes 393224 | tf_op jit(solution)/shard_map/ppermute | solution.py:12
  105.9 0.3 convolution_bitcast_fusion.19
  106.3 2.2 %collective-permute-done.8 = bf16[256,256]{0,1:T(8,128)(2,1)S(1)} collective-permute-done((bf16[256,256]{0,1:T(8,128)(2,1)S(1)}, bf16[256,256]{0,1:T(8,128)(2,1)S(1)}, u32[]{:S(2)}, u32[]{:S(2)}) %collective-permute-start.8) | collective-permute-done | bytes 131104 | tf_op jit(solution)/shard_map/ppermute | solution.py:12
  108.5 7.2 %collective-permute-start.9 = (bf16[256,256]{0,1:T(8,128)(2,1)S(1)}, bf16[256,256]{0,1:T(8,128)(2,1)S(1)}, u32[]{:S(2)}, u32[]{:S(2)}) collective-permute-start(bf16[256,256]{0,1:T(8,128)(2,1)S(1)} %fusion.68), channel_id=1, source_target_pairs={{4,0},{8,4},{12,8},{16,12},{20,16},{24,20},{28,24},{32,28},{36,32}... | collective-permute-start | bytes 393224 | tf_op jit(solution)/shard_map/ppermute | solution.py:12
  115.7 0.3 convolution_bitcast_fusion.17
  116.1 2.2 %collective-permute-done.9 = bf16[256,256]{0,1:T(8,128)(2,1)S(1)} collective-permute-done((bf16[256,256]{0,1:T(8,128)(2,1)S(1)}, bf16[256,256]{0,1:T(8,128)(2,1)S(1)}, u32[]{:S(2)}, u32[]{:S(2)}) %collective-permute-start.9) | collective-permute-done | bytes 131104 | tf_op jit(solution)/shard_map/ppermute | solution.py:12
  118.3 7.2 %collective-permute-start.10 = (bf16[256,256]{0,1:T(8,128)(2,1)S(1)}, bf16[256,256]{0,1:T(8,128)(2,1)S(1)}, u32[]{:S(2)}, u32[]{:S(2)}) collective-permute-start(bf16[256,256]{0,1:T(8,128)(2,1)S(1)} %fusion.69), channel_id=1, source_target_pairs={{4,0},{8,4},{12,8},{16,12},{20,16},{24,20},{28,24},{32,28},{36,32}... | collective-permute-start | bytes 393224 | tf_op jit(solution)/shard_map/ppermute | solution.py:12
  125.5 0.3 convolution_bitcast_fusion.15
  125.8 2.2 %collective-permute-done.10 = bf16[256,256]{0,1:T(8,128)(2,1)S(1)} collective-permute-done((bf16[256,256]{0,1:T(8,128)(2,1)S(1)}, bf16[256,256]{0,1:T(8,128)(2,1)S(1)}, u32[]{:S(2)}, u32[]{:S(2)}) %collective-permute-start.10) | collective-permute-done | bytes 131104 | tf_op jit(solution)/shard_map/ppermute | solution.py:12
  128.0 7.1 %collective-permute-start.11 = (bf16[256,256]{0,1:T(8,128)(2,1)S(1)}, bf16[256,256]{0,1:T(8,128)(2,1)S(1)}, u32[]{:S(2)}, u32[]{:S(2)}) collective-permute-start(bf16[256,256]{0,1:T(8,128)(2,1)S(1)} %fusion.70), channel_id=1, source_target_pairs={{4,0},{8,4},{12,8},{16,12},{20,16},{24,20},{28,24},{32,28},{36,32}... | collective-permute-start | bytes 393224 | tf_op jit(solution)/shard_map/ppermute | solution.py:12
  135.1 0.3 convolution_bitcast_fusion.13
  135.5 2.2 %collective-permute-done.11 = bf16[256,256]{0,1:T(8,128)(2,1)S(1)} collective-permute-done((bf16[256,256]{0,1:T(8,128)(2,1)S(1)}, bf16[256,256]{0,1:T(8,128)(2,1)S(1)}, u32[]{:S(2)}, u32[]{:S(2)}) %collective-permute-start.11) | collective-permute-done | bytes 131104 | tf_op jit(solution)/shard_map/ppermute | solution.py:12
  137.7 7.1 %collective-permute-start.12 = (bf16[256,256]{0,1:T(8,128)(2,1)S(1)}, bf16[256,256]{0,1:T(8,128)(2,1)S(1)}, u32[]{:S(2)}, u32[]{:S(2)}) collective-permute-start(bf16[256,256]{0,1:T(8,128)(2,1)S(1)} %fusion.71), channel_id=1, source_target_pairs={{4,0},{8,4},{12,8},{16,12},{20,16},{24,20},{28,24},{32,28},{36,32}... | collective-permute-start | bytes 393224 | tf_op jit(solution)/shard_map/ppermute | solution.py:12
  145.1 2.2 %collective-permute-done.12 = bf16[256,256]{0,1:T(8,128)(2,1)S(1)} collective-permute-done((bf16[256,256]{0,1:T(8,128)(2,1)S(1)}, bf16[256,256]{0,1:T(8,128)(2,1)S(1)}, u32[]{:S(2)}, u32[]{:S(2)}) %collective-permute-start.12) | collective-permute-done | bytes 131104 | tf_op jit(solution)/shard_map/ppermute | solution.py:12
  147.3 7.1 %collective-permute-start.13 = (bf16[256,256]{0,1:T(8,128)(2,1)S(1)}, bf16[256,256]{0,1:T(8,128)(2,1)S(1)}, u32[]{:S(2)}, u32[]{:S(2)}) collective-permute-start(bf16[256,256]{0,1:T(8,128)(2,1)S(1)} %fusion.72), channel_id=1, source_target_pairs={{4,0},{8,4},{12,8},{16,12},{20,16},{24,20},{28,24},{32,28},{36,32}... | collective-permute-start | bytes 393224 | tf_op jit(solution)/shard_map/ppermute | solution.py:12
  154.4 0.3 convolution_bitcast_fusion.9
  154.7 2.2 %collective-permute-done.13 = bf16[256,256]{0,1:T(8,128)(2,1)S(1)} collective-permute-done((bf16[256,256]{0,1:T(8,128)(2,1)S(1)}, bf16[256,256]{0,1:T(8,128)(2,1)S(1)}, u32[]{:S(2)}, u32[]{:S(2)}) %collective-permute-start.13) | collective-permute-done | bytes 131104 | tf_op jit(solution)/shard_map/ppermute | solution.py:12
  156.9 20.2 %all-reduce.1 = bf16[256,256]{0,1:T(8,128)(2,1)S(1)} all-reduce(f32[256,256]{0,1:T(8,128)S(1)} %maximum_add_fusion.6), channel_id=1, replica_groups=mesh['ctx'=128,'head'=4] {'head'}, use_global_device_ids=true, to_apply=%region_31.32 | all-reduce | flops 65536 | bytes 393216 | tf_op jit(solution)/shard_map/psum | solution.py:114
  177.1 0.7 copy.76
  177.9 0.7 copy.75
  (82 shorter events, 10.2 us)
Async XLA Ops:
  0.6 13.4 %copy-start.13 = (bf16[256,512]{1,0:T(8,128)(2,1)S(1)}, bf16[256,512]{1,0:T(8,128)(2,1)}, u32[]{:S(2)}) copy-start(bf16[256,512]{1,0:T(8,128)(2,1)} %param.7) | copy-start | bytes 786436
  1.6 18.6 %collective-permute-start = (bf16[256,256]{1,0:T(8,128)(2,1)S(1)}, bf16[256,256]{1,0:T(8,128)(2,1)S(1)}, u32[]{:S(2)}, u32[]{:S(2)}) collective-permute-start(bf16[256,256]{1,0:T(8,128)(2,1)S(1)} %pad_maximum_fusion), channel_id=1, source_target_pairs={{0,4},{4,8},{8,12},{12,16},{16,20},{20,24},{24,28},{28,32},{32,36}... | collective-permute-start | bytes 393224 | tf_op jit(solution)/shard_map/ppermute | solution.py:12
  3.6 0.7 copy-start.17
  12.0 1.2 copy-start.18
  14.0 1.0 copy-start.14
  15.0 4.6 %copy-start.16 = (s32[4,128]{1,0:T(4,128)S(1)}, s32[4,128]{1,0:T(4,128)}, u32[]{:S(2)}) copy-start(s32[4,128]{1,0:T(4,128)} %param.13) | copy-start | bytes 6148
  15.1 4.8 %copy-start.9 = (bf16[256,128]{1,0:T(8,128)(2,1)S(1)}, bf16[256,128]{1,0:T(8,128)(2,1)}, u32[]{:S(2)}) copy-start(bf16[256,128]{1,0:T(8,128)(2,1)} %param.8) | copy-start | bytes 196612
  20.2 64.3 %copy-start.11 = (bf16[256,256]{1,0:T(8,128)(2,1)}, bf16[256,256]{1,0:T(8,128)(2,1)S(1)}, u32[]{:S(2)}) copy-start(bf16[256,256]{1,0:T(8,128)(2,1)S(1)} %collective-permute-done) | copy-start | bytes 393220
  20.2 12.9 %collective-permute-start.1 = (bf16[256,256]{1,0:T(8,128)(2,1)S(1)}, bf16[256,256]{1,0:T(8,128)(2,1)S(1)}, u32[]{:S(2)}, u32[]{:S(2)}) collective-permute-start(bf16[256,256]{1,0:T(8,128)(2,1)S(1)} %collective-permute-done), channel_id=1, source_target_pairs={{0,4},{4,8},{8,12},{12,16},{16,20},{20,24},{24,28},{28,32},{32,36}... | collective-permute-start | bytes 393224 | tf_op jit(solution)/shard_map/ppermute | solution.py:12
  33.2 9.6 %collective-permute-start.2 = (bf16[256,256]{1,0:T(8,128)(2,1)S(1)}, bf16[256,256]{1,0:T(8,128)(2,1)S(1)}, u32[]{:S(2)}, u32[]{:S(2)}) collective-permute-start(bf16[256,256]{1,0:T(8,128)(2,1)S(1)} %collective-permute-done.1), channel_id=1, source_target_pairs={{0,4},{4,8},{8,12},{12,16},{16,20},{20,24},{24,28},{28,32},{32,36}... | collective-permute-start | bytes 393224 | tf_op jit(solution)/shard_map/ppermute | solution.py:12
  35.4 49.9 %copy-start = (f32[4,256,256]{1,2,0:T(8,128)}, f32[4,256,256]{1,2,0:T(8,128)S(1)}, u32[]{:S(2)}) copy-start(f32[4,256,256]{1,2,0:T(8,128)S(1)} %get-tuple-element.75) | copy-start | bytes 3145732
  42.8 9.6 %collective-permute-start.3 = (bf16[256,256]{1,0:T(8,128)(2,1)S(1)}, bf16[256,256]{1,0:T(8,128)(2,1)S(1)}, u32[]{:S(2)}, u32[]{:S(2)}) collective-permute-start(bf16[256,256]{1,0:T(8,128)(2,1)S(1)} %collective-permute-done.2), channel_id=1, source_target_pairs={{0,4},{4,8},{8,12},{12,16},{16,20},{20,24},{24,28},{28,32},{32,36}... | collective-permute-start | bytes 393224 | tf_op jit(solution)/shard_map/ppermute | solution.py:12
  45.0 40.3 %copy-start.2 = (f32[4,256,256]{1,2,0:T(8,128)}, f32[4,256,256]{1,2,0:T(8,128)S(1)}, u32[]{:S(2)}) copy-start(f32[4,256,256]{1,2,0:T(8,128)S(1)} %get-tuple-element.73) | copy-start | bytes 3145732
  52.3 9.6 %collective-permute-start.4 = (bf16[256,256]{1,0:T(8,128)(2,1)S(1)}, bf16[256,256]{1,0:T(8,128)(2,1)S(1)}, u32[]{:S(2)}, u32[]{:S(2)}) collective-permute-start(bf16[256,256]{1,0:T(8,128)(2,1)S(1)} %collective-permute-done.3), channel_id=1, source_target_pairs={{0,4},{4,8},{8,12},{12,16},{16,20},{20,24},{24,28},{28,32},{32,36}... | collective-permute-start | bytes 393224 | tf_op jit(solution)/shard_map/ppermute | solution.py:12
  54.6 30.7 %copy-start.4 = (f32[4,256,256]{1,2,0:T(8,128)}, f32[4,256,256]{1,2,0:T(8,128)S(1)}, u32[]{:S(2)}) copy-start(f32[4,256,256]{1,2,0:T(8,128)S(1)} %get-tuple-element.71) | copy-start | bytes 3145732
  61.9 9.6 %collective-permute-start.5 = (bf16[256,256]{1,0:T(8,128)(2,1)S(1)}, bf16[256,256]{1,0:T(8,128)(2,1)S(1)}, u32[]{:S(2)}, u32[]{:S(2)}) collective-permute-start(bf16[256,256]{1,0:T(8,128)(2,1)S(1)} %collective-permute-done.4), channel_id=1, source_target_pairs={{0,4},{4,8},{8,12},{12,16},{16,20},{20,24},{24,28},{28,32},{32,36}... | collective-permute-start | bytes 393224 | tf_op jit(solution)/shard_map/ppermute | solution.py:12
  64.2 21.1 %copy-start.6 = (f32[4,256,256]{1,2,0:T(8,128)}, f32[4,256,256]{1,2,0:T(8,128)S(1)}, u32[]{:S(2)}) copy-start(f32[4,256,256]{1,2,0:T(8,128)S(1)} %get-tuple-element.69) | copy-start | bytes 3145732
  71.5 9.6 %collective-permute-start.6 = (bf16[256,256]{1,0:T(8,128)(2,1)S(1)}, bf16[256,256]{1,0:T(8,128)(2,1)S(1)}, u32[]{:S(2)}, u32[]{:S(2)}) collective-permute-start(bf16[256,256]{1,0:T(8,128)(2,1)S(1)} %collective-permute-done.5), channel_id=1, source_target_pairs={{0,4},{4,8},{8,12},{12,16},{16,20},{20,24},{24,28},{28,32},{32,36}... | collective-permute-start | bytes 393224 | tf_op jit(solution)/shard_map/ppermute | solution.py:12
  73.8 11.6 %copy-start.8 = (f32[4,256,256]{1,2,0:T(8,128)}, f32[4,256,256]{1,2,0:T(8,128)S(1)}, u32[]{:S(2)}) copy-start(f32[4,256,256]{1,2,0:T(8,128)S(1)} %get-tuple-element.67) | copy-start | bytes 3145732
  81.4 0.8 copy-start.15
  91.7 0.9 copy-start.12
  94.1 4.6 %copy-start.10 = (f32[256,128]{0,1:T(8,128)S(1)}, f32[256,128]{0,1:T(8,128)}, u32[]{:S(2)}) copy-start(f32[256,128]{0,1:T(8,128)} %fusion.26) | copy-start | bytes 393220
  94.1 11.9 %copy-start.7 = (f32[4,256,256]{1,2,0:T(8,128)S(1)}, f32[4,256,256]{1,2,0:T(8,128)}, u32[]{:S(2)}) copy-start(f32[4,256,256]{1,2,0:T(8,128)} %copy-done.6) | copy-start | bytes 3145732
  94.1 4.6 %collective-permute-start.7 = (bf16[256,256]{0,1:T(8,128)(2,1)S(1)}, bf16[256,256]{0,1:T(8,128)(2,1)S(1)}, u32[]{:S(2)}, u32[]{:S(2)}) collective-permute-start(bf16[256,256]{0,1:T(8,128)(2,1)S(1)} %pad_maximum_fusion.1), channel_id=1, source_target_pairs={{4,0},{8,4},{12,8},{16,12},{20,16},{24,20},{28,24},{32,28},{36,32}... | collective-permute-start | bytes 393224 | tf_op jit(solution)/shard_map/ppermute | solution.py:12
  98.7 17.0 %copy-start.5 = (f32[4,256,256]{1,2,0:T(8,128)S(1)}, f32[4,256,256]{1,2,0:T(8,128)}, u32[]{:S(2)}) copy-start(f32[4,256,256]{1,2,0:T(8,128)} %copy-done.4) | copy-start | bytes 3145732
  98.7 9.7 %collective-permute-start.8 = (bf16[256,256]{0,1:T(8,128)(2,1)S(1)}, bf16[256,256]{0,1:T(8,128)(2,1)S(1)}, u32[]{:S(2)}, u32[]{:S(2)}) collective-permute-start(bf16[256,256]{0,1:T(8,128)(2,1)S(1)} %fusion.67), channel_id=1, source_target_pairs={{4,0},{8,4},{12,8},{16,12},{20,16},{24,20},{28,24},{32,28},{36,32}... | collective-permute-start | bytes 393224 | tf_op jit(solution)/shard_map/ppermute | solution.py:12
  108.5 17.0 %copy-start.3 = (f32[4,256,256]{1,2,0:T(8,128)S(1)}, f32[4,256,256]{1,2,0:T(8,128)}, u32[]{:S(2)}) copy-start(f32[4,256,256]{1,2,0:T(8,128)} %copy-done.2) | copy-start | bytes 3145732
  108.5 9.7 %collective-permute-start.9 = (bf16[256,256]{0,1:T(8,128)(2,1)S(1)}, bf16[256,256]{0,1:T(8,128)(2,1)S(1)}, u32[]{:S(2)}, u32[]{:S(2)}) collective-permute-start(bf16[256,256]{0,1:T(8,128)(2,1)S(1)} %fusion.68), channel_id=1, source_target_pairs={{4,0},{8,4},{12,8},{16,12},{20,16},{24,20},{28,24},{32,28},{36,32}... | collective-permute-start | bytes 393224 | tf_op jit(solution)/shard_map/ppermute | solution.py:12
  118.2 16.9 %copy-start.1 = (f32[4,256,256]{1,2,0:T(8,128)S(1)}, f32[4,256,256]{1,2,0:T(8,128)}, u32[]{:S(2)}) copy-start(f32[4,256,256]{1,2,0:T(8,128)} %copy-done) | copy-start | bytes 3145732
  118.3 9.7 %collective-permute-start.10 = (bf16[256,256]{0,1:T(8,128)(2,1)S(1)}, bf16[256,256]{0,1:T(8,128)(2,1)S(1)}, u32[]{:S(2)}, u32[]{:S(2)}) collective-permute-start(bf16[256,256]{0,1:T(8,128)(2,1)S(1)} %fusion.69), channel_id=1, source_target_pairs={{4,0},{8,4},{12,8},{16,12},{20,16},{24,20},{28,24},{32,28},{36,32}... | collective-permute-start | bytes 393224 | tf_op jit(solution)/shard_map/ppermute | solution.py:12
  128.0 9.6 %collective-permute-start.11 = (bf16[256,256]{0,1:T(8,128)(2,1)S(1)}, bf16[256,256]{0,1:T(8,128)(2,1)S(1)}, u32[]{:S(2)}, u32[]{:S(2)}) collective-permute-start(bf16[256,256]{0,1:T(8,128)(2,1)S(1)} %fusion.70), channel_id=1, source_target_pairs={{4,0},{8,4},{12,8},{16,12},{20,16},{24,20},{28,24},{32,28},{36,32}... | collective-permute-start | bytes 393224 | tf_op jit(solution)/shard_map/ppermute | solution.py:12
  137.7 9.6 %collective-permute-start.12 = (bf16[256,256]{0,1:T(8,128)(2,1)S(1)}, bf16[256,256]{0,1:T(8,128)(2,1)S(1)}, u32[]{:S(2)}, u32[]{:S(2)}) collective-permute-start(bf16[256,256]{0,1:T(8,128)(2,1)S(1)} %fusion.71), channel_id=1, source_target_pairs={{4,0},{8,4},{12,8},{16,12},{20,16},{24,20},{28,24},{32,28},{36,32}... | collective-permute-start | bytes 393224 | tf_op jit(solution)/shard_map/ppermute | solution.py:12
  147.3 9.6 %collective-permute-start.13 = (bf16[256,256]{0,1:T(8,128)(2,1)S(1)}, bf16[256,256]{0,1:T(8,128)(2,1)S(1)}, u32[]{:S(2)}, u32[]{:S(2)}) collective-permute-start(bf16[256,256]{0,1:T(8,128)(2,1)S(1)} %fusion.72), channel_id=1, source_target_pairs={{4,0},{8,4},{12,8},{16,12},{20,16},{24,20},{28,24},{32,28},{36,32}... | collective-permute-start | bytes 393224 | tf_op jit(solution)/shard_map/ppermute | solution.py:12
where the time goes:
time: 179 us
  starting transfers between devices  60.9 us (34%)
  waiting for transfers between devices  58.9 us (33%)
  blocking collectives  20.2 us (11%)
  between operations  14.1 us (8%)
  matrix products  14 us (8%)
  local copies, waits for them, and re-layouts  6.25 us (3%)
  other arithmetic  4.23 us (2%)
    ppermute x14, starting transfers between devices, from_behind(): return lax.ppermute(array, axis, pairs)  60.9 us
    ppermute x14, waiting for transfers between devices, from_behind(): return lax.ppermute(array, axis, pairs)  58.9 us
    psum x1, blocking collectives, local(): result = lax.psum(carried, 'head').astype(jnp.bfloat16)  20.2 us
    unnamed x41, local copies, waits for them, and re-layouts  5.3 us
    dot_general x8, matrix products, grad_step(): jnp.einsum('hij,ihd->jd', probs_low, grad_heads, preferred_element_type=j...  3.82 us
  transfers between devices with their start and end apart: 14, of which 13 were waited for; matrix products, arithmetic and copies ran while one was open for 4% of the time, Pallas kernels for 0%

commit v1 on v0

v1 whole, which is shorter than its diff:
```python
import functools

import jax
import jax.numpy as jnp
from jax import lax
from jax.experimental import pallas as pl
from jax.experimental.pallas import tpu as pltpu
from jax.sharding import PartitionSpec as P

NEG = -1e30
BOTH = ("ctx", "head")
NT = (((1,), (1,)), ((), ()))


def attention_kernel(
    info, docs, pairs, knock, q_ref, g_ref, own, same, other, dq_ref, cross_ref, plane_ref, near_ref,
    scores, gprobs, acc, key_t, dq_t, top, total, weighted, last,
):
    rows, width = own.shape[0], own.shape[1] // 2
    heads = q_ref.shape[1] // width
    reach = pairs.shape[1] + 1
    scale = width ** (-0.5)
    here, side = info[0], info[1]
    f32 = jnp.float32

    def block_live(o):
        source = jnp.maximum(here - o, 0)
        listed = functools.reduce(jnp.logical_or, [pairs[0, k] == o for k in range(reach - 1)])
        return (here - o >= 0) & listed & (docs[source] == docs[here])

    lives = [None] + [block_live(o) for o in range(1, reach)]

    def live(o, h):
        return lives[o] & (knock[h, jnp.maximum(here - o, 0)] == 1)

    def tile(o):
        if o == 0:
            return own[...]
        if o % 2 == 0:
            return same[o // 2]
        if o == reach - 1:
            return last[...]
        return other[(o - 1) // 2 + (1 - side)]

    @pl.when(side == 0)
    def _():
        last[...] = same[0]

    @pl.when(side == 1)
    def _():
        last[...] = other[reach // 2 - 1]

    def each(o, h, fn):
        if o == 0:
            fn()
        else:
            pl.when(live(o, h))(fn)

    acc[...] = jnp.zeros_like(acc)
    for o in range(reach):
        def prepare(o=o):
            key_t[o] = tile(o)[:, :width].T
        if o == 0:
            prepare()
        else:
            pl.when(lives[o])(prepare)
    below = lax.broadcasted_iota(jnp.int32, (rows, rows), 0) <= lax.broadcasted_iota(
        jnp.int32, (rows, rows), 1
    )

    for h in range(heads):
        cols = slice(h * width, (h + 1) * width)
        top[...] = jnp.full_like(top, NEG)
        for o in range(reach):
            def first(o=o):
                kv = tile(o)
                s = lax.dot_general(kv[:, :width], q_ref[:, cols], NT, preferred_element_type=f32) * scale
                if o == 0:
                    s = jnp.where(below, s, NEG)
                scores[o] = s
                gprobs[o] = lax.dot_general(kv[:, width:], g_ref[:, cols], NT, preferred_element_type=f32)
                top[...] = jnp.maximum(top[...], jnp.max(s, axis=0, keepdims=True))
            each(o, h, first)
        total[...] = jnp.zeros_like(total)
        weighted[...] = jnp.zeros_like(weighted)
        for o in range(reach):
            def second(o=o):
                e = jnp.exp(scores[o] - top[...])
                scores[o] = e
                total[...] += jnp.sum(e, axis=0, keepdims=True)
                weighted[...] += jnp.sum(e * gprobs[o], axis=0, keepdims=True)
            each(o, h, second)
        inverse = 1.0 / total[...]
        delta = weighted[...] * inverse
        dq_t[...] = jnp.zeros_like(dq_t)
        for o in range(reach):
            def third(o=o):
                p = scores[o] * inverse
                ds = (p * (gprobs[o] - delta)).astype(jnp.bfloat16)
                acc[o, :, :width] += jnp.dot(ds, q_ref[:, cols], preferred_element_type=f32)
                acc[o, :, width:] += jnp.dot(
                    p.astype(jnp.bfloat16), g_ref[:, cols], preferred_element_type=f32
                )
                dq_t[...] += jnp.dot(key_t[o], ds, preferred_element_type=f32)
            each(o, h, third)
        dq_ref[:, cols] = (dq_t[...].T * scale).astype(dq_ref.dtype)

    def term(o):
        return jnp.concatenate([acc[o, :, :width] * scale, acc[o, :, width:]], axis=1)

    near_ref[...] = term(0)
    for o in range(2, reach, 2):
        plane_ref[o // 2] = term(o).astype(plane_ref.dtype)
    for o in range(1, reach - 1, 2):
        cross_ref[(o - 1) // 2 + (1 - side)] = term(o).astype(cross_ref.dtype)

    @pl.when(side == 0)
    def _():
        plane_ref[0] = term(reach - 1).astype(plane_ref.dtype)
        cross_ref[0] = jnp.zeros(cross_ref.shape[1:], cross_ref.dtype)

    @pl.when(side == 1)
    def _():
        cross_ref[reach // 2 - 1] = term(reach - 1).astype(cross_ref.dtype)
        plane_ref[0] = jnp.zeros(plane_ref.shape[1:], plane_ref.dtype)


def plane_pairs(blocks, planes):
    pairs = []
    for block in range(blocks):
        chip, side = block // 2, block % 2
        for plane in range(planes):
            source = 2 * (chip - plane) + side
            if plane == 0:
                source = 2 * (chip - planes) + 1
                if side == 1:
                    continue
            if source >= 0:
                pairs.append((source * planes + plane, block * planes + plane))
    return pairs


def local(queries, keys, values, grad_out, doc_of_block, pair_list, knock):
    rows, width = keys.shape
    heads = queries.shape[1] // width
    reach = pair_list.shape[1] + 1
    blocks = doc_of_block.shape[0]
    planes = lax.axis_size("head")
    here = lax.axis_index("ctx")
    info = jnp.stack([here, here % 2])
    out = plane_pairs(blocks, planes)
    back = [(b, a) for a, b in out]
    swap = [(i, i ^ 1) for i in range(blocks)]
    bf16, f32 = jnp.bfloat16, jnp.float32

    own = jnp.concatenate([keys, values], axis=1)
    fetched = lax.ppermute(own, BOTH, out)
    same = lax.all_to_all(jnp.broadcast_to(fetched, (planes, rows, 2 * width)), "head", 0, 0)
    other = lax.ppermute(jnp.concatenate([own[None], same[1:]], axis=0), "ctx", swap)

    vmem = pl.BlockSpec(memory_space=pltpu.VMEM)
    smem = pl.BlockSpec(memory_space=pltpu.SMEM)
    four = jax.ShapeDtypeStruct((planes, rows, 2 * width), bf16)
    d_queries, cross, plane, near = pl.pallas_call(
        attention_kernel,
        out_shape=(
            jax.ShapeDtypeStruct(queries.shape, bf16),
            four,
            four,
            jax.ShapeDtypeStruct((rows, 2 * width), f32),
        ),
        in_specs=[smem] * 4 + [vmem] * 5,
        out_specs=(vmem,) * 4,
        scratch_shapes=[
            pltpu.VMEM((reach, rows, rows), f32),
            pltpu.VMEM((reach, rows, rows), f32),
            pltpu.VMEM((reach, rows, 2 * width), f32),
            pltpu.VMEM((reach, width, rows), bf16),
            pltpu.VMEM((width, rows), f32),
            pltpu.VMEM((1, rows), f32),
            pltpu.VMEM((1, rows), f32),
            pltpu.VMEM((1, rows), f32),
            pltpu.VMEM((rows, 2 * width), bf16),
        ],
        compiler_params=pltpu.CompilerParams(vmem_limit_bytes=40 << 20),
    )(info, doc_of_block, pair_list, knock, queries, grad_out, own, same, other)

    crossed = lax.ppermute(cross, "ctx", swap).astype(f32)
    summed = jnp.concatenate([plane[:1], (plane[1:] + crossed[1:]).astype(bf16)], axis=0)
    near = near + crossed[0]
    parts = lax.all_to_all(summed, "head", 0, 0)
    sent = jnp.sum(parts.astype(f32), axis=0).astype(bf16)
    landed = lax.ppermute(sent, BOTH, back)
    mine = (landed.astype(f32) + near).astype(bf16)
    every = lax.all_to_all(jnp.broadcast_to(mine, (planes, rows, 2 * width)), "head", 0, 0)
    result = jnp.sum(every.astype(f32), axis=0).astype(bf16)
    return d_queries, result[:, :width], result[:, width:]


def solution(mesh):
    in_specs = (
        P("ctx", "head"),
        P("ctx", None),
        P("ctx", None),
        P("ctx", "head"),
        P(),
        P("ctx", None),
        P("head", None),
    )
    out_specs = (P("ctx", "head"), P("ctx", None), P("ctx", None))
    return jax.shard_map(local, mesh=mesh, in_specs=in_specs, out_specs=out_specs, check_vma=False)
```

time: 179 us -> 93.2 us (0.52)
  the two profiles are of different devices: /device:TPU:32 before, /device:TPU:40 now
where the time goes in v1:
time: 93.2 us; the launch traced here: 92.9 us
  blocking collectives  50.3 us (54%)
  waiting for transfers between devices  18.9 us (20%)
  Pallas kernels  10.7 us (11%)
  starting transfers between devices  9.88 us (11%)
  local copies, waits for them, and re-layouts  1.71 us (2%)
    all_to_all x1, blocking collectives, local(): lax.all_to_all(jnp.broadcast_to(mine, (planes, rows, 2 * width)), 'head',...  19.5 us
    all_to_all x1, blocking collectives, local(): lax.all_to_all(jnp.broadcast_to(fetched, (planes, rows, 2 * width)), 'hea...  18.1 us
    ppermute x1, waiting for transfers between devices, local(): fetched = lax.ppermute(own, BOTH, out)  13.1 us
    all_to_all x1, blocking collectives, local(): parts = lax.all_to_all(summed, 'head', 0, 0)  12.8 us
    pallas_call x1, Pallas kernels, local(): pl.pallas_call(attention_kernel, out_shape=(jax.ShapeDtypeStruct(queries....  10.7 us
    ppermute x1, starting transfers between devices, local(): crossed = lax.ppermute(cross, 'ctx', swap).astype(f32)  4.17 us
    ppermute x1, waiting for transfers between devices, local(): landed = lax.ppermute(sent, BOTH, back)  2.5 us
    ppermute x1, starting transfers between devices, local(): landed = lax.ppermute(sent, BOTH, back)  2.37 us
  transfers between devices with their start and end apart: 4, of which 4 were waited for; matrix products, arithmetic and copies ran while one was open for 0% of the time, Pallas kernels for 0%

profile of v1, /device:TPU:40, one launch (start us, length us, event | category | flops | bytes accessed | tf_op | source)
XLA Modules:
  0.0 92.9 jit_solution(14190838210438982352)
XLA Ops:
  0.6 0.0 copy-start.5
  0.6 0.9 constant_dynamic-update-slice_fusion.1
  1.5 0.0 copy-done.5
  1.6 1.3 %collective-permute-start = (bf16[256,256]{1,0:T(8,128)(2,1)S(1)}, bf16[256,256]{1,0:T(8,128)(2,1)S(1)}, u32[]{:S(2)}, u32[]{:S(2)}) collective-permute-start(bf16[256,256]{1,0:T(8,128)(2,1)S(1)} %constant_dynamic-update-slice_fusion.own), channel_id=1, source_target_pairs={{1,9},{5,13},{9,17},{2,18},{13,21},{6,22},{17,25},{10,26},{3,27},{... | collective-permute-start | bytes 393224 | tf_op jit(solution)/shard_map/ppermute | solution.py:157
  2.9 13.1 %collective-permute-done = bf16[256,256]{1,0:T(8,128)(2,1)S(1)} collective-permute-done((bf16[256,256]{1,0:T(8,128)(2,1)S(1)}, bf16[256,256]{1,0:T(8,128)(2,1)S(1)}, u32[]{:S(2)}, u32[]{:S(2)}) %collective-permute-start) | collective-permute-done | bytes 131104 | tf_op jit(solution)/shard_map/ppermute | solution.py:157
  16.0 18.1 %all_to_all.15.same = bf16[4,256,256]{2,1,0:T(8,128)(2,1)S(1)} all-to-all(bf16[4,256,256]{2,1,0:T(8,128)(2,1)S(1)} %broadcast_in_dim.9), channel_id=1, replica_groups=mesh['ctx'=128,'head'=4] {'head'}, dimensions={0} | all-to-all | bytes 1048576 | tf_op jit(solution)/shard_map/all_to_all | solution.py:158
  34.1 0.0 copy-start
  34.2 0.0 copy-start.1
  34.2 2.1 %collective-permute-start.1 = (bf16[4,256,256]{2,1,0:T(8,128)(2,1)S(1)}, bf16[4,256,256]{2,1,0:T(8,128)(2,1)S(1)}, u32[]{:S(2)}, u32[]{:S(2)}) collective-permute-start(bf16[4,256,256]{2,1,0:T(8,128)(2,1)S(1)} %pad_maximum_fusion), channel_id=1, source_target_pairs={{0,4},{4,0},{8,12},{12,8},{16,20},{20,16},{24,28},{28,24},{32,36},... | collective-permute-start | bytes 1572872 | tf_op jit(solution)/shard_map/ppermute | solution.py:159
  36.3 0.0 copy-start.2
  36.3 0.0 copy-start.3
  36.3 0.0 copy-start.4
  36.3 0.1 pad_add_fusion.info
  36.4 1.8 %collective-permute-done.1.other = bf16[4,256,256]{2,1,0:T(8,128)(2,1)S(1)} collective-permute-done((bf16[4,256,256]{2,1,0:T(8,128)(2,1)S(1)}, bf16[4,256,256]{2,1,0:T(8,128)(2,1)S(1)}, u32[]{:S(2)}, u32[]{:S(2)}) %collective-permute-start.1) | collective-permute-done | bytes 524320 | tf_op jit(solution)/shard_map/ppermute | solution.py:159
  38.2 0.0 copy-done
  38.2 0.0 copy-done.1
  38.2 0.0 copy-done.2
  38.2 0.0 copy-done.3
  38.2 0.0 copy-done.4
  38.2 10.7 %shard_map.94 = (bf16[256,512]{1,0:T(8,128)(2,1)}, bf16[4,256,256]{2,1,0:T(8,128)(2,1)S(1)}, bf16[4,256,256]{2,1,0:T(8,128)(2,1)S(1)}, f32[256,256]{1,0:T(8,128)S(1)}) custom-call(s32[2]{0:T(128)S(1)} %pad_add_fusion.info, s32[128]{0:T(128)S(1)} %copy-done.3, s32[1,7]{1,0:T(1,128)S(1)} %copy-done.4, s32[4,128]{1,0:T(4,128)S(1)} %copy-done.2, ...), custom_call_target="tpu_custom_call" | custom-call | tf_op jit(solution)/shard_map/pallas_call | solution.py:164
  48.9 4.2 %collective-permute-start.2 = (bf16[4,256,256]{2,1,0:T(8,128)(2,1)S(1)}, bf16[4,256,256]{2,1,0:T(8,128)(2,1)S(1)}, u32[]{:S(2)}, u32[]{:S(2)}) collective-permute-start(bf16[4,256,256]{2,1,0:T(8,128)(2,1)S(1)} %get-tuple-element.9), channel_id=1, source_target_pairs={{0,4},{4,0},{8,12},{12,8},{16,20},{20,16},{24,28},{28,24},{32,36},... | collective-permute-start | bytes 1572872 | tf_op jit(solution)/shard_map/ppermute | solution.py:188
  53.1 1.5 %collective-permute-done.2 = bf16[4,256,256]{2,1,0:T(8,128)(2,1)S(1)} collective-permute-done((bf16[4,256,256]{2,1,0:T(8,128)(2,1)S(1)}, bf16[4,256,256]{2,1,0:T(8,128)(2,1)S(1)}, u32[]{:S(2)}, u32[]{:S(2)}) %collective-permute-start.2) | collective-permute-done | bytes 524320 | tf_op jit(solution)/shard_map/ppermute | solution.py:188
  54.6 0.1 convert_element_type.20
  54.7 0.1 fusion
  54.8 12.8 %all_to_all.16 = bf16[4,256,256]{2,1,0:T(8,128)(2,1)S(1)} all-to-all(bf16[4,256,256]{2,1,0:T(8,128)(2,1)S(1)} %pad_maximum_fusion.1), channel_id=1, replica_groups=mesh['ctx'=128,'head'=4] {'head'}, dimensions={0} | all-to-all | bytes 1048576 | tf_op jit(solution)/shard_map/all_to_all | solution.py:191
  67.6 0.1 reduce_sum.24
  67.7 2.4 %collective-permute-start.3 = (bf16[256,256]{1,0:T(8,128)(2,1)S(1)}, bf16[256,256]{1,0:T(8,128)(2,1)S(1)}, u32[]{:S(2)}, u32[]{:S(2)}) collective-permute-start(bf16[256,256]{1,0:T(8,128)(2,1)S(1)} %reduce_sum.24), channel_id=1, source_target_pairs={{9,1},{13,5},{17,9},{18,2},{21,13},{22,6},{25,17},{26,10},{27,3},{... | collective-permute-start | bytes 393224 | tf_op jit(solution)/shard_map/ppermute | solution.py:193
  70.1 2.5 %collective-permute-done.3 = bf16[256,256]{1,0:T(8,128)(2,1)S(1)} collective-permute-done((bf16[256,256]{1,0:T(8,128)(2,1)S(1)}, bf16[256,256]{1,0:T(8,128)(2,1)S(1)}, u32[]{:S(2)}, u32[]{:S(2)}) %collective-permute-start.3) | collective-permute-done | bytes 131104 | tf_op jit(solution)/shard_map/ppermute | solution.py:193
  72.7 19.5 %all_to_all.17 = bf16[4,256,256]{2,1,0:T(8,128)(2,1)S(1)} all-to-all(bf16[4,256,256]{2,1,0:T(8,128)(2,1)S(1)} %broadcast_in_dim.11), channel_id=1, replica_groups=mesh['ctx'=128,'head'=4] {'head'}, dimensions={0} | all-to-all | bytes 1048576 | tf_op jit(solution)/shard_map/all_to_all | solution.py:195
  92.2 0.1 reduce_sum.25
  92.2 0.7 fusion.4
  (8 shorter events, 0.3 us)
Async XLA Ops:
  0.6 0.9 copy-start.5
  1.6 14.4 %collective-permute-start = (bf16[256,256]{1,0:T(8,128)(2,1)S(1)}, bf16[256,256]{1,0:T(8,128)(2,1)S(1)}, u32[]{:S(2)}, u32[]{:S(2)}) collective-permute-start(bf16[256,256]{1,0:T(8,128)(2,1)S(1)} %constant_dynamic-update-slice_fusion.own), channel_id=1, source_target_pairs={{1,9},{5,13},{9,17},{2,18},{13,21},{6,22},{17,25},{10,26},{3,27},{... | collective-permute-start | bytes 393224 | tf_op jit(solution)/shard_map/ppermute | solution.py:157
  34.1 4.0 %copy-start = (bf16[256,512]{1,0:T(8,128)(2,1)S(1)}, bf16[256,512]{1,0:T(8,128)(2,1)}, u32[]{:S(2)}) copy-start(bf16[256,512]{1,0:T(8,128)(2,1)} %q_ref.1) | copy-start | bytes 786436
  34.2 4.0 %copy-start.1 = (bf16[256,512]{1,0:T(8,128)(2,1)S(1)}, bf16[256,512]{1,0:T(8,128)(2,1)}, u32[]{:S(2)}) copy-start(bf16[256,512]{1,0:T(8,128)(2,1)} %g_ref.1) | copy-start | bytes 786436
  34.2 3.9 %collective-permute-start.1 = (bf16[4,256,256]{2,1,0:T(8,128)(2,1)S(1)}, bf16[4,256,256]{2,1,0:T(8,128)(2,1)S(1)}, u32[]{:S(2)}, u32[]{:S(2)}) collective-permute-start(bf16[4,256,256]{2,1,0:T(8,128)(2,1)S(1)} %pad_maximum_fusion), channel_id=1, source_target_pairs={{0,4},{4,0},{8,12},{12,8},{16,20},{20,16},{24,28},{28,24},{32,36},... | collective-permute-start | bytes 1572872 | tf_op jit(solution)/shard_map/ppermute | solution.py:159
  36.3 1.9 %copy-start.2 = (s32[4,128]{1,0:T(4,128)S(1)}, s32[4,128]{1,0:T(4,128)}, u32[]{:S(2)}) copy-start(s32[4,128]{1,0:T(4,128)} %knock.1) | copy-start | bytes 6148
  36.3 1.9 %copy-start.3 = (s32[128]{0:T(128)S(1)}, s32[128]{0:T(128)}, u32[]{:S(2)}) copy-start(s32[128]{0:T(128)} %docs.1) | copy-start | bytes 1540
  36.3 1.9 %copy-start.4 = (s32[1,7]{1,0:T(1,128)S(1)}, s32[1,7]{1,0:T(1,128)}, u32[]{:S(2)}) copy-start(s32[1,7]{1,0:T(1,128)} %pairs.1) | copy-start | bytes 88
  48.9 5.7 %collective-permute-start.2 = (bf16[4,256,256]{2,1,0:T(8,128)(2,1)S(1)}, bf16[4,256,256]{2,1,0:T(8,128)(2,1)S(1)}, u32[]{:S(2)}, u32[]{:S(2)}) collective-permute-start(bf16[4,256,256]{2,1,0:T(8,128)(2,1)S(1)} %get-tuple-element.9), channel_id=1, source_target_pairs={{0,4},{4,0},{8,12},{12,8},{16,20},{20,16},{24,28},{28,24},{32,36},... | collective-permute-start | bytes 1572872 | tf_op jit(solution)/shard_map/ppermute | solution.py:188
  67.7 4.9 %collective-permute-start.3 = (bf16[256,256]{1,0:T(8,128)(2,1)S(1)}, bf16[256,256]{1,0:T(8,128)(2,1)S(1)}, u32[]{:S(2)}, u32[]{:S(2)}) collective-permute-start(bf16[256,256]{1,0:T(8,128)(2,1)S(1)} %reduce_sum.24), channel_id=1, source_target_pairs={{9,1},{13,5},{17,9},{18,2},{21,13},{22,6},{25,17},{26,10},{27,3},{... | collective-permute-start | bytes 393224 | tf_op jit(solution)/shard_map/ppermute | solution.py:193

commit v2 on v1

v2 whole, which is shorter than its diff:
```python
import functools

import jax
import jax.numpy as jnp
from jax import lax
from jax.experimental import pallas as pl
from jax.experimental.pallas import tpu as pltpu
from jax.sharding import PartitionSpec as P

NEG = -1e30
BOTH = ("ctx", "head")
NT = (((1,), (1,)), ((), ()))


def attention_kernel(
    info, docs, pairs, knock, q_ref, g_ref, own, same, other, dq_ref, cross_ref, plane_ref, near_ref,
    scores, gprobs, pool, key_t, dq_t, q_all, g_all, probs, grads, count, offset, bias,
):
    rows, width = own.shape[0], own.shape[1] // 2
    heads = q_ref.shape[1] // width
    reach = pairs.shape[1] + 1
    scale = width ** (-0.5)
    here, side = info[0], info[1]
    f32, bf16 = jnp.float32, jnp.bfloat16

    for h in range(heads):
        q_all[h * rows : (h + 1) * rows] = q_ref[:, h * width : (h + 1) * width]
        g_all[h * rows : (h + 1) * rows] = g_ref[:, h * width : (h + 1) * width]

    def admit(o, value):
        slot = count[0]
        pool[slot] = value
        key_t[slot] = value[:, :width].T
        offset[slot] = o
        for h in range(heads):
            kept = 1 if o == 0 else knock[h, jnp.maximum(here - o, 0)]
            bias[slot, h] = jnp.where(kept == 1, 0.0, NEG).astype(f32)
        count[0] = slot + 1

    count[0] = 0
    admit(0, own[...])
    for o in range(1, reach):
        source = jnp.maximum(here - o, 0)
        listed = functools.reduce(jnp.logical_or, [pairs[0, k] == o for k in range(reach - 1)])
        kept = functools.reduce(jnp.logical_or, [knock[h, source] == 1 for h in range(heads)])
        live = (here - o >= 0) & listed & (docs[source] == docs[here]) & kept
        if o % 2 == 0:
            pl.when(live)(lambda o=o: admit(o, same[o // 2]))
        elif o < reach - 1:
            pl.when(live)(lambda o=o: admit(o, other[(o - 1) // 2 + (1 - side)]))
        else:
            pl.when(live & (side == 0))(lambda o=o: admit(o, same[0]))
            pl.when(live & (side == 1))(lambda o=o: admit(o, other[reach // 2 - 1]))
    tiles = count[0]

    below = lax.broadcasted_iota(jnp.int32, (rows, rows), 0) <= lax.broadcasted_iota(
        jnp.int32, (rows, rows), 1
    )
    tops = []
    for h in range(heads):
        part = slice(h * rows, (h + 1) * rows)
        s = lax.dot_general(pool[0, :, :width], q_all[part], NT, preferred_element_type=f32) * scale
        s = jnp.where(below, s, NEG)
        scores[0, :, part] = s
        tops.append(jnp.max(s, axis=0, keepdims=True))

    def first(i, tops):
        fresh = []
        for h in range(heads):
            part = slice(h * rows, (h + 1) * rows)
            s = lax.dot_general(pool[i, :, :width], q_all[part], NT, preferred_element_type=f32)
            s = s * scale + bias[i, h]
            scores[i, :, part] = s
            fresh.append(jnp.maximum(tops[h], jnp.max(s, axis=0, keepdims=True)))
        return tuple(fresh)

    tops = lax.fori_loop(1, tiles, first, tuple(tops))

    def second(i, sums):
        fresh = []
        for h in range(heads):
            part = slice(h * rows, (h + 1) * rows)
            g = lax.dot_general(pool[i, :, width:], g_all[part], NT, preferred_element_type=f32)
            e = jnp.exp(scores[i, :, part] - tops[h])
            gprobs[i, :, part] = g
            scores[i, :, part] = e
            total, weighted = sums[h]
            fresh.append(
                (
                    total + jnp.sum(e, axis=0, keepdims=True),
                    weighted + jnp.sum(e * g, axis=0, keepdims=True),
                )
            )
        return tuple(fresh)

    zero = jnp.zeros((1, rows), f32)
    sums = lax.fori_loop(0, tiles, second, ((zero, zero),) * heads)
    inverse = [1.0 / total for total, _ in sums]
    delta = [weighted * inv for (_, weighted), inv in zip(sums, inverse)]

    def gradients(i):
        for h in range(heads):
            part = slice(h * rows, (h + 1) * rows)
            p = scores[i, :, part] * inverse[h]
            probs[:, part] = p.astype(bf16)
            grads[:, part] = (p * (gprobs[i, :, part] - delta[h])).astype(bf16)
        key_term = jnp.dot(grads[...], q_all[...], preferred_element_type=f32) * scale
        value_term = jnp.dot(probs[...], g_all[...], preferred_element_type=f32)
        query_term = jnp.dot(key_t[i], grads[...], preferred_element_type=f32)
        return key_term, value_term, query_term

    plane_ref[...] = jnp.zeros_like(plane_ref)
    cross_ref[...] = jnp.zeros_like(cross_ref)
    key_term, value_term, query_term = gradients(0)
    near_ref[:, :width] = key_term
    near_ref[:, width:] = value_term
    dq_t[...] = query_term

    def third(i, carry):
        key_term, value_term, query_term = gradients(i)
        dq_t[...] += query_term
        o = offset[i]
        in_plane = (o % 2 == 0) | ((o == reach - 1) & (side == 0))
        plane = jnp.where(o % 2 == 0, o // 2, 0)
        cross = jnp.clip((o - 1) // 2 + (1 - side), 0, reach // 2 - 1)

        @pl.when(in_plane)
        def _():
            plane_ref[plane, :, :width] = key_term.astype(bf16)
            plane_ref[plane, :, width:] = value_term.astype(bf16)

        @pl.when(jnp.logical_not(in_plane))
        def _():
            cross_ref[cross, :, :width] = key_term.astype(bf16)
            cross_ref[cross, :, width:] = value_term.astype(bf16)

        return carry

    lax.fori_loop(1, tiles, third, 0)
    for h in range(heads):
        part = slice(h * rows, (h + 1) * rows)
        dq_ref[:, h * width : (h + 1) * width] = (dq_t[:, part].T * scale).astype(bf16)


def plane_pairs(blocks, planes):
    pairs = []
    for block in range(blocks):
        chip, side = block // 2, block % 2
        for plane in range(planes):
            source = 2 * (chip - plane) + side
            if plane == 0:
                source = 2 * (chip - planes) + 1
                if side == 1:
                    continue
            if source >= 0:
                pairs.append((source * planes + plane, block * planes + plane))
    return pairs


def local(queries, keys, values, grad_out, doc_of_block, pair_list, knock):
    rows, width = keys.shape
    heads = queries.shape[1] // width
    reach = pair_list.shape[1] + 1
    blocks = doc_of_block.shape[0]
    planes = lax.axis_size("head")
    here = lax.axis_index("ctx")
    info = jnp.stack([here, here % 2])
    out = plane_pairs(blocks, planes)
    back = [(b, a) for a, b in out]
    swap = [(i, i ^ 1) for i in range(blocks)]
    bf16, f32 = jnp.bfloat16, jnp.float32

    own = jnp.concatenate([keys, values], axis=1)
    fetched = lax.ppermute(own, BOTH, out)
    same = lax.all_to_all(jnp.broadcast_to(fetched, (planes, rows, 2 * width)), "head", 0, 0)
    other = lax.ppermute(jnp.concatenate([own[None], same[1:]], axis=0), "ctx", swap)

    vmem = pl.BlockSpec(memory_space=pltpu.VMEM)
    smem = pl.BlockSpec(memory_space=pltpu.SMEM)
    four = jax.ShapeDtypeStruct((planes, rows, 2 * width), bf16)
    d_queries, cross, plane, near = pl.pallas_call(
        attention_kernel,
        out_shape=(
            jax.ShapeDtypeStruct(queries.shape, bf16),
            four,
            four,
            jax.ShapeDtypeStruct((rows, 2 * width), f32),
        ),
        in_specs=[smem] * 4 + [vmem] * 5,
        out_specs=(vmem,) * 4,
        scratch_shapes=[
            pltpu.VMEM((reach, rows, heads * rows), f32),
            pltpu.VMEM((reach, rows, heads * rows), f32),
            pltpu.VMEM((reach, rows, 2 * width), bf16),
            pltpu.VMEM((reach, width, rows), bf16),
            pltpu.VMEM((width, heads * rows), f32),
            pltpu.VMEM((heads * rows, width), bf16),
            pltpu.VMEM((heads * rows, width), bf16),
            pltpu.VMEM((rows, heads * rows), bf16),
            pltpu.VMEM((rows, heads * rows), bf16),
            pltpu.SMEM((1,), jnp.int32),
            pltpu.SMEM((reach,), jnp.int32),
            pltpu.SMEM((reach, heads), f32),
        ],
        compiler_params=pltpu.CompilerParams(vmem_limit_bytes=40 << 20),
    )(info, doc_of_block, pair_list, knock, queries, grad_out, own, same, other)

    crossed = lax.ppermute(cross, "ctx", swap).astype(f32)
    summed = jnp.concatenate([plane[:1], (plane[1:] + crossed[1:]).astype(bf16)], axis=0)
    near = near + crossed[0]
    parts = lax.all_to_all(summed, "head", 0, 0)
    sent = jnp.sum(parts.astype(f32), axis=0).astype(bf16)
    landed = lax.ppermute(sent, BOTH, back)
    mine = (landed.astype(f32) + near).astype(bf16)
    every = lax.all_to_all(jnp.broadcast_to(mine, (planes, rows, 2 * width)), "head", 0, 0)
    result = jnp.sum(every.astype(f32), axis=0).astype(bf16)
    return d_queries, result[:, :width], result[:, width:]


def solution(mesh):
    in_specs = (
        P("ctx", "head"),
        P("ctx", None),
        P("ctx", None),
        P("ctx", "head"),
        P(),
        P("ctx", None),
        P("head", None),
    )
    out_specs = (P("ctx", "head"), P("ctx", None), P("ctx", None))
    return jax.shard_map(local, mesh=mesh, in_specs=in_specs, out_specs=out_specs, check_vma=False)
```

time: 93.2 us -> 93.8 us (level)
  the two profiles are of different devices: /device:TPU:40 before, /device:TPU:24 now
where the time goes in v2:
time: 93.8 us; the launch traced here: 93.5 us
  blocking collectives  57.9 us (62%)
  waiting for transfers between devices  18.1 us (19%)
  starting transfers between devices  11.5 us (12%)
  Pallas kernels  2.97 us (3%)
  local copies, waits for them, and re-layouts  1.71 us (2%)
    all_to_all x1, blocking collectives, local(): lax.all_to_all(jnp.broadcast_to(mine, (planes, rows, 2 * width)), 'head',...  26.5 us
    all_to_all x1, blocking collectives, local(): lax.all_to_all(jnp.broadcast_to(fetched, (planes, rows, 2 * width)), 'hea...  19 us
    all_to_all x1, blocking collectives, local(): parts = lax.all_to_all(summed, 'head', 0, 0)  12.5 us
    ppermute x1, waiting for transfers between devices, local(): fetched = lax.ppermute(own, BOTH, out)  11.7 us
    ppermute x1, starting transfers between devices, local(): landed = lax.ppermute(sent, BOTH, back)  6.12 us
    pallas_call x1, Pallas kernels, local(): pl.pallas_call(attention_kernel, out_shape=(jax.ShapeDtypeStruct(queries....  2.97 us
    ppermute x1, waiting for transfers between devices, local(): landed = lax.ppermute(sent, BOTH, back)  2.85 us
    ppermute x1, starting transfers between devices, local(): lax.ppermute(jnp.concatenate([own[None], same[1:]], axis=0), 'ctx', swap)  2.05 us
  transfers between devices with their start and end apart: 4, of which 4 were waited for; matrix products, arithmetic and copies ran while one was open for 0% of the time, Pallas kernels for 0%

profile of v2, /device:TPU:24, one launch (start us, length us, event | category | flops | bytes accessed | tf_op | source)
XLA Modules:
  0.0 93.5 jit_solution(1249061962101038766)
XLA Ops:
  0.6 0.0 copy-start.5
  0.6 0.9 constant_dynamic-update-slice_fusion.1
  1.5 0.0 copy-done.5
  1.6 1.3 %collective-permute-start = (bf16[256,256]{1,0:T(8,128)(2,1)S(1)}, bf16[256,256]{1,0:T(8,128)(2,1)S(1)}, u32[]{:S(2)}, u32[]{:S(2)}) collective-permute-start(bf16[256,256]{1,0:T(8,128)(2,1)S(1)} %constant_dynamic-update-slice_fusion.own), channel_id=1, source_target_pairs={{1,9},{5,13},{9,17},{2,18},{13,21},{6,22},{17,25},{10,26},{3,27},{... | collective-permute-start | bytes 393224 | tf_op jit(solution)/shard_map/ppermute | solution.py:174
  2.9 11.7 %collective-permute-done = bf16[256,256]{1,0:T(8,128)(2,1)S(1)} collective-permute-done((bf16[256,256]{1,0:T(8,128)(2,1)S(1)}, bf16[256,256]{1,0:T(8,128)(2,1)S(1)}, u32[]{:S(2)}, u32[]{:S(2)}) %collective-permute-start) | collective-permute-done | bytes 131104 | tf_op jit(solution)/shard_map/ppermute | solution.py:174
  14.6 19.0 %all_to_all.15.same = bf16[4,256,256]{2,1,0:T(8,128)(2,1)S(1)} all-to-all(bf16[4,256,256]{2,1,0:T(8,128)(2,1)S(1)} %broadcast_in_dim.9), channel_id=1, replica_groups=mesh['ctx'=128,'head'=4] {'head'}, dimensions={0} | all-to-all | bytes 1048576 | tf_op jit(solution)/shard_map/all_to_all | solution.py:175
  33.6 0.0 copy-start
  33.6 0.0 copy-start.1
  33.7 2.1 %collective-permute-start.1 = (bf16[4,256,256]{2,1,0:T(8,128)(2,1)S(1)}, bf16[4,256,256]{2,1,0:T(8,128)(2,1)S(1)}, u32[]{:S(2)}, u32[]{:S(2)}) collective-permute-start(bf16[4,256,256]{2,1,0:T(8,128)(2,1)S(1)} %pad_maximum_fusion), channel_id=1, source_target_pairs={{0,4},{4,0},{8,12},{12,8},{16,20},{20,16},{24,28},{28,24},{32,36},... | collective-permute-start | bytes 1572872 | tf_op jit(solution)/shard_map/ppermute | solution.py:176
  35.8 0.0 copy-start.2
  35.8 0.0 copy-start.3
  35.8 0.0 copy-start.4
  35.8 0.1 pad_add_fusion.info
  35.9 1.8 %collective-permute-done.1.other = bf16[4,256,256]{2,1,0:T(8,128)(2,1)S(1)} collective-permute-done((bf16[4,256,256]{2,1,0:T(8,128)(2,1)S(1)}, bf16[4,256,256]{2,1,0:T(8,128)(2,1)S(1)}, u32[]{:S(2)}, u32[]{:S(2)}) %collective-permute-start.1) | collective-permute-done | bytes 524320 | tf_op jit(solution)/shard_map/ppermute | solution.py:176
  37.6 0.0 copy-done
  37.6 0.0 copy-done.1
  37.6 0.0 copy-done.2
  37.6 0.0 copy-done.3
  37.6 0.0 copy-done.4
  37.7 3.0 %shard_map.94 = (bf16[256,512]{1,0:T(8,128)(2,1)}, bf16[4,256,256]{2,1,0:T(8,128)(2,1)S(1)}, bf16[4,256,256]{2,1,0:T(8,128)(2,1)S(1)}, f32[256,256]{1,0:T(8,128)S(1)}) custom-call(s32[2]{0:T(128)S(1)} %pad_add_fusion.info, s32[128]{0:T(128)S(1)} %copy-done.3, s32[1,7]{1,0:T(1,128)S(1)} %copy-done.4, s32[4,128]{1,0:T(4,128)S(1)} %copy-done.2, ...), custom_call_target="tpu_custom_call" | custom-call | tf_op jit(solution)/shard_map/pallas_call | solution.py:181
  40.6 2.0 %collective-permute-start.2 = (bf16[4,256,256]{2,1,0:T(8,128)(2,1)S(1)}, bf16[4,256,256]{2,1,0:T(8,128)(2,1)S(1)}, u32[]{:S(2)}, u32[]{:S(2)}) collective-permute-start(bf16[4,256,256]{2,1,0:T(8,128)(2,1)S(1)} %get-tuple-element.9), channel_id=1, source_target_pairs={{0,4},{4,0},{8,12},{12,8},{16,20},{20,16},{24,28},{28,24},{32,36},... | collective-permute-start | bytes 1572872 | tf_op jit(solution)/shard_map/ppermute | solution.py:208
  42.7 1.7 %collective-permute-done.2 = bf16[4,256,256]{2,1,0:T(8,128)(2,1)S(1)} collective-permute-done((bf16[4,256,256]{2,1,0:T(8,128)(2,1)S(1)}, bf16[4,256,256]{2,1,0:T(8,128)(2,1)S(1)}, u32[]{:S(2)}, u32[]{:S(2)}) %collective-permute-start.2) | collective-permute-done | bytes 524320 | tf_op jit(solution)/shard_map/ppermute | solution.py:208
  44.4 0.1 convert_element_type.20
  44.5 0.1 fusion
  44.7 12.5 %all_to_all.16 = bf16[4,256,256]{2,1,0:T(8,128)(2,1)S(1)} all-to-all(bf16[4,256,256]{2,1,0:T(8,128)(2,1)S(1)} %pad_maximum_fusion.1), channel_id=1, replica_groups=mesh['ctx'=128,'head'=4] {'head'}, dimensions={0} | all-to-all | bytes 1048576 | tf_op jit(solution)/shard_map/all_to_all | solution.py:211
  57.1 0.1 reduce_sum.24
  57.2 6.1 %collective-permute-start.3 = (bf16[256,256]{1,0:T(8,128)(2,1)S(1)}, bf16[256,256]{1,0:T(8,128)(2,1)S(1)}, u32[]{:S(2)}, u32[]{:S(2)}) collective-permute-start(bf16[256,256]{1,0:T(8,128)(2,1)S(1)} %reduce_sum.24), channel_id=1, source_target_pairs={{9,1},{13,5},{17,9},{18,2},{21,13},{22,6},{25,17},{26,10},{27,3},{... | collective-permute-start | bytes 393224 | tf_op jit(solution)/shard_map/ppermute | solution.py:213
  63.3 2.9 %collective-permute-done.3 = bf16[256,256]{1,0:T(8,128)(2,1)S(1)} collective-permute-done((bf16[256,256]{1,0:T(8,128)(2,1)S(1)}, bf16[256,256]{1,0:T(8,128)(2,1)S(1)}, u32[]{:S(2)}, u32[]{:S(2)}) %collective-permute-start.3) | collective-permute-done | bytes 131104 | tf_op jit(solution)/shard_map/ppermute | solution.py:213
  66.3 26.5 %all_to_all.17 = bf16[4,256,256]{2,1,0:T(8,128)(2,1)S(1)} all-to-all(bf16[4,256,256]{2,1,0:T(8,128)(2,1)S(1)} %broadcast_in_dim.11), channel_id=1, replica_groups=mesh['ctx'=128,'head'=4] {'head'}, dimensions={0} | all-to-all | bytes 1048576 | tf_op jit(solution)/shard_map/all_to_all | solution.py:215
  92.8 0.1 reduce_sum.25
  92.8 0.7 fusion.4
  (8 shorter events, 0.3 us)
Async XLA Ops:
  0.6 0.9 copy-start.5
  1.6 13.0 %collective-permute-start = (bf16[256,256]{1,0:T(8,128)(2,1)S(1)}, bf16[256,256]{1,0:T(8,128)(2,1)S(1)}, u32[]{:S(2)}, u32[]{:S(2)}) collective-permute-start(bf16[256,256]{1,0:T(8,128)(2,1)S(1)} %constant_dynamic-update-slice_fusion.own), channel_id=1, source_target_pairs={{1,9},{5,13},{9,17},{2,18},{13,21},{6,22},{17,25},{10,26},{3,27},{... | collective-permute-start | bytes 393224 | tf_op jit(solution)/shard_map/ppermute | solution.py:174
  33.6 4.0 %copy-start = (bf16[256,512]{1,0:T(8,128)(2,1)S(1)}, bf16[256,512]{1,0:T(8,128)(2,1)}, u32[]{:S(2)}) copy-start(bf16[256,512]{1,0:T(8,128)(2,1)} %q_ref.1) | copy-start | bytes 786436
  33.6 4.0 %copy-start.1 = (bf16[256,512]{1,0:T(8,128)(2,1)S(1)}, bf16[256,512]{1,0:T(8,128)(2,1)}, u32[]{:S(2)}) copy-start(bf16[256,512]{1,0:T(8,128)(2,1)} %g_ref.1) | copy-start | bytes 786436
  33.7 3.9 %collective-permute-start.1 = (bf16[4,256,256]{2,1,0:T(8,128)(2,1)S(1)}, bf16[4,256,256]{2,1,0:T(8,128)(2,1)S(1)}, u32[]{:S(2)}, u32[]{:S(2)}) collective-permute-start(bf16[4,256,256]{2,1,0:T(8,128)(2,1)S(1)} %pad_maximum_fusion), channel_id=1, source_target_pairs={{0,4},{4,0},{8,12},{12,8},{16,20},{20,16},{24,28},{28,24},{32,36},... | collective-permute-start | bytes 1572872 | tf_op jit(solution)/shard_map/ppermute | solution.py:176
  35.8 1.9 %copy-start.2 = (s32[4,128]{1,0:T(4,128)S(1)}, s32[4,128]{1,0:T(4,128)}, u32[]{:S(2)}) copy-start(s32[4,128]{1,0:T(4,128)} %knock.1) | copy-start | bytes 6148
  35.8 1.9 %copy-start.3 = (s32[128]{0:T(128)S(1)}, s32[128]{0:T(128)}, u32[]{:S(2)}) copy-start(s32[128]{0:T(128)} %docs.1) | copy-start | bytes 1540
  35.8 1.9 %copy-start.4 = (s32[1,7]{1,0:T(1,128)S(1)}, s32[1,7]{1,0:T(1,128)}, u32[]{:S(2)}) copy-start(s32[1,7]{1,0:T(1,128)} %pairs.1) | copy-start | bytes 88
  40.6 3.8 %collective-permute-start.2 = (bf16[4,256,256]{2,1,0:T(8,128)(2,1)S(1)}, bf16[4,256,256]{2,1,0:T(8,128)(2,1)S(1)}, u32[]{:S(2)}, u32[]{:S(2)}) collective-permute-start(bf16[4,256,256]{2,1,0:T(8,128)(2,1)S(1)} %get-tuple-element.9), channel_id=1, source_target_pairs={{0,4},{4,0},{8,12},{12,8},{16,20},{20,16},{24,28},{28,24},{32,36},... | collective-permute-start | bytes 1572872 | tf_op jit(solution)/shard_map/ppermute | solution.py:208
  57.2 9.0 %collective-permute-start.3 = (bf16[256,256]{1,0:T(8,128)(2,1)S(1)}, bf16[256,256]{1,0:T(8,128)(2,1)S(1)}, u32[]{:S(2)}, u32[]{:S(2)}) collective-permute-start(bf16[256,256]{1,0:T(8,128)(2,1)S(1)} %reduce_sum.24), channel_id=1, source_target_pairs={{9,1},{13,5},{17,9},{18,2},{21,13},{22,6},{25,17},{26,10},{27,3},{... | collective-permute-start | bytes 393224 | tf_op jit(solution)/shard_map/ppermute | solution.py:213

commit v3 on v1

v3 whole, which is shorter than its diff:
```python
import functools

import jax
import jax.numpy as jnp
from jax import lax
from jax.experimental import pallas as pl
from jax.experimental.pallas import tpu as pltpu
from jax.sharding import PartitionSpec as P

NEG = -1e30
BOTH = ("ctx", "head")
NT = (((1,), (1,)), ((), ()))


def list_kernel(info, docs, pairs, pairs2, knock, meta):
    heads, slots = knock.shape[0], (pairs.shape[1] + 1) // 2
    here, side = info[0], info[1]
    for i in range(meta.shape[0]):
        meta[i] = 0
    for d in range(slots + 1):
        block = jnp.maximum(here - 2 * d, 0)
        slot = jnp.clip(jnp.where(side == 0, d, slots - d), 0, slots - 1)
        kept = functools.reduce(jnp.logical_or, [knock[h, block] == 1 for h in range(heads)])
        for which, table in ((0, pairs), (1, pairs2)):
            if which == 0 and d in (0, slots):
                continue
            back = 2 * d + which * (1 - 2 * side)
            query = here + which * (1 - 2 * side)
            listed = functools.reduce(
                jnp.logical_or, [table[0, k] == back for k in range(pairs.shape[1])]
            )
            live = (back > 0) & (here - 2 * d >= 0) & listed & (docs[block] == docs[query]) & kept

            @pl.when(live)
            def _(which=which, block=block, slot=slot):
                entry = (slots - 1) * which + meta[which]
                meta[8 + entry] = slot
                meta[24 + slot] = 1
                for h in range(heads):
                    meta[32 + heads * entry + h] = knock[h, block]
                meta[which] = meta[which] + 1


def first_kernel(q_ref, g_ref, own, exps, gprobs, key_t, stack, stats):
    rows, width = own.shape[0], own.shape[1] // 2
    heads = q_ref.shape[1] // width
    scale = width ** (-0.5)
    f32 = jnp.float32
    for h in range(heads):
        part, cols = slice(h * rows, (h + 1) * rows), slice(h * width, (h + 1) * width)
        stack[0, part], stack[1, part] = q_ref[:, cols], g_ref[:, cols]
    key_t[...] = own[:, :width].T
    stats[...] = jnp.zeros_like(stats)
    below = lax.broadcasted_iota(jnp.int32, (rows, rows), 0) <= lax.broadcasted_iota(
        jnp.int32, (rows, rows), 1
    )
    for h in range(heads):
        part = slice(h * rows, (h + 1) * rows)
        s = lax.dot_general(own[:, :width], stack[0, part], NT, preferred_element_type=f32) * scale
        g = lax.dot_general(own[:, width:], stack[1, part], NT, preferred_element_type=f32)
        s = jnp.where(below, s, NEG)
        top = jnp.max(s, axis=0, keepdims=True)
        e = jnp.exp(s - top)
        exps[:, part] = e
        gprobs[:, part] = g
        stats[0:1, part] = top
        stats[1:2, part] = jnp.sum(e, axis=0, keepdims=True)
        stats[2:3, part] = jnp.sum(e * g, axis=0, keepdims=True)


def scores_kernel(meta, stack, stack2, first_stats, same, exps, gprobs, key_t, stats):
    slots, rows, width = same.shape[0], same.shape[1], same.shape[2] // 2
    span = stack.shape[1]
    heads = span // rows
    scale = width ** (-0.5)
    f32 = jnp.float32

    for slot in range(slots):
        @pl.when(meta[24 + slot] == 1)
        def _(slot=slot):
            key_t[slot] = same[slot, :, :width].T

    stats[...] = jnp.zeros_like(stats)
    for which in range(2):
        stats[which, 0:1] = jnp.full((1, span), NEG, f32)
    stats[0, 3:6] = first_stats[0:3]

    for which, both in ((0, stack), (1, stack2)):
        base = (slots - 1) * which

        def first(i, carry, which=which, both=both, base=base):
            i = base + i
            slot = meta[8 + i]
            for h in range(heads):
                part = slice(h * rows, (h + 1) * rows)
                s = lax.dot_general(
                    same[slot, :, :width], both[0, part], NT, preferred_element_type=f32
                )
                s = s * scale + jnp.where(meta[32 + heads * i + h] == 1, 0.0, NEG).astype(f32)
                exps[i, :, part] = s
                stats[which, 0:1, part] = jnp.maximum(
                    stats[which, 0:1, part], jnp.max(s, axis=0, keepdims=True)
                )
            return carry

        def second(i, carry, which=which, both=both, base=base):
            i = base + i
            slot = meta[8 + i]
            for h in range(heads):
                part = slice(h * rows, (h + 1) * rows)
                g = lax.dot_general(
                    same[slot, :, width:], both[1, part], NT, preferred_element_type=f32
                )
                e = jnp.exp(exps[i, :, part] - stats[which, 0:1, part])
                gprobs[i, :, part] = g
                exps[i, :, part] = e
                stats[which, 1:2, part] += jnp.sum(e, axis=0, keepdims=True)
                stats[which, 2:3, part] += jnp.sum(e * g, axis=0, keepdims=True)
            return carry

        lax.fori_loop(0, meta[which], first, 0)
        lax.fori_loop(0, meta[which], second, 0)


def terms_kernel(
    info, meta, first_exps, first_gprobs, first_key_t, exps, gprobs, key_t, stack, stack2, mine, theirs,
    plane_ref, near_ref, dq_ref, factors, acc, probs, grads,
):
    rows, width = key_t.shape[2], key_t.shape[1]
    span = stack.shape[1]
    slots = plane_ref.shape[0]
    scale = width ** (-0.5)
    side = info[1]
    stacks = (stack, stack2)
    f32, bf16 = jnp.float32, jnp.bfloat16

    def three(ref, which, row):
        return ref[which, row : row + 1], ref[which, row + 1 : row + 2], ref[which, row + 2 : row + 3]

    groups = (
        (three(mine, 0, 0), three(mine, 0, 3), three(theirs, 1, 0)),
        (three(mine, 1, 0), three(theirs, 0, 0), three(theirs, 0, 3)),
    )
    for which, group in enumerate(groups):
        high = functools.reduce(jnp.maximum, [top for top, _, _ in group])
        shares = [jnp.exp(top - high) for top, _, _ in group]
        total = sum(share * part for share, (_, part, _) in zip(shares, group))
        weighted = sum(share * part for share, (_, _, part) in zip(shares, group))
        inverse = 1.0 / total
        factors[which, 0:1] = shares[0] * inverse
        factors[which, 1:2] = weighted * inverse
        factors[which, 2:3] = shares[1] * inverse

    def gradients(load_e, load_g, keys, which, row):
        for h in range(span // rows):
            part = slice(h * rows, (h + 1) * rows)
            p = load_e(part) * factors[which, row : row + 1, part]
            probs[:, part] = p.astype(bf16)
            grads[:, part] = (p * (load_g(part) - factors[which, 1:2, part])).astype(bf16)
        key_term = jnp.dot(grads[...], stacks[which][0], preferred_element_type=f32) * scale
        value_term = jnp.dot(probs[...], stacks[which][1], preferred_element_type=f32)
        query_term = jnp.dot(keys, grads[...], preferred_element_type=f32)
        return key_term, value_term, query_term

    acc[...] = jnp.zeros_like(acc)
    key_term, value_term, query_term = gradients(
        lambda part: first_exps[:, part], lambda part: first_gprobs[:, part], first_key_t[...], 0, 2
    )
    near_ref[:, :width] = key_term
    near_ref[:, width:] = value_term
    dq_ref[0] = query_term
    dq_ref[1] = jnp.zeros_like(query_term)

    for which in range(2):
        def step(i, carry, which=which):
            i = (slots - 1) * which + i
            slot = meta[8 + i]
            key_term, value_term, query_term = gradients(
                lambda part: exps[i, :, part], lambda part: gprobs[i, :, part], key_t[slot], which, 0
            )
            acc[slot, :, :width] += key_term
            acc[slot, :, width:] += value_term
            dq_ref[which] += query_term
            return carry

        lax.fori_loop(0, meta[which], step, 0)
    for slot in range(1, slots):
        plane_ref[slot] = acc[slot].astype(bf16)

    @pl.when(side == 0)
    def _():
        near_ref[...] += acc[0]
        plane_ref[0] = jnp.zeros(plane_ref.shape[1:], bf16)

    @pl.when(side == 1)
    def _():
        plane_ref[0] = acc[0].astype(bf16)


def queries_kernel(mine, theirs, dq_ref):
    width, rows = mine.shape[1], dq_ref.shape[0]
    scale = width ** (-0.5)
    for h in range(dq_ref.shape[1] // width):
        part = slice(h * rows, (h + 1) * rows)
        dq = (mine[0, :, part] + theirs[:, part]) * scale
        dq_ref[:, h * width : (h + 1) * width] = dq.T.astype(dq_ref.dtype)


def plane_pairs(blocks, planes):
    pairs = []
    for block in range(blocks):
        for plane in range(planes):
            source = block - 2 * (plane if block % 2 == 0 else planes - plane)
            if source >= 0:
                pairs.append((source * planes + plane, block * planes + plane))
    return pairs


def local(queries, keys, values, grad_out, doc_of_block, pair_list, knock):
    rows, width = keys.shape
    heads = queries.shape[1] // width
    reach = pair_list.shape[1] + 1
    blocks = doc_of_block.shape[0]
    planes = lax.axis_size("head")
    here = lax.axis_index("ctx")
    info = jnp.stack([here, here % 2])
    out = plane_pairs(blocks, planes)
    back = [(b, a) for a, b in out if a != b]
    swap = [(i, i ^ 1) for i in range(blocks)]
    bf16, f32 = jnp.bfloat16, jnp.float32
    span = heads * rows

    edge = jnp.zeros((), bf16)
    own = lax.pad(keys, edge, ((0, 0, 0), (0, width, 0))) + lax.pad(values, edge, ((0, 0, 0), (width, 0, 0)))
    fetched = lax.ppermute(own, BOTH, out)
    pairs2 = lax.ppermute(pair_list, "ctx", swap)

    vmem = pl.BlockSpec(memory_space=pltpu.VMEM)
    smem = pl.BlockSpec(memory_space=pltpu.SMEM)
    params = pltpu.CompilerParams(vmem_limit_bytes=20 << 20)
    meta = pl.pallas_call(
        list_kernel,
        out_shape=jax.ShapeDtypeStruct((32 + heads * reach,), jnp.int32),
        in_specs=[smem] * 5,
        out_specs=smem,
        compiler_params=params,
    )(info, doc_of_block, pair_list, pairs2, knock)
    exps0, gprobs0, key0_t, stack, stats0 = pl.pallas_call(
        first_kernel,
        out_shape=(
            pltpu.VMEM((rows, span), f32),
            pltpu.VMEM((rows, span), f32),
            pltpu.VMEM((width, rows), bf16),
            jax.ShapeDtypeStruct((2, span, width), bf16),
            jax.ShapeDtypeStruct((8, span), f32),
        ),
        in_specs=[vmem] * 3,
        out_specs=(vmem,) * 5,
        compiler_params=params,
    )(queries, grad_out, own)
    stack2 = lax.ppermute(stack, "ctx", swap)
    fetched, stats0, meta = lax.optimization_barrier((fetched, stats0, meta))
    same = lax.all_to_all(jnp.broadcast_to(fetched, (planes, rows, 2 * width)), "head", 0, 0)
    exps, gprobs, key_t, mine = pl.pallas_call(
        scores_kernel,
        out_shape=(
            pltpu.VMEM((reach - 1, rows, span), f32),
            pltpu.VMEM((reach - 1, rows, span), f32),
            pltpu.VMEM((planes, width, rows), bf16),
            jax.ShapeDtypeStruct((2, 8, span), f32),
        ),
        in_specs=[smem] + [vmem] * 4,
        out_specs=(vmem,) * 4,
        compiler_params=params,
    )(meta, stack, stack2, stats0, same)
    theirs = lax.ppermute(mine, "ctx", swap)
    plane, near, dq = pl.pallas_call(
        terms_kernel,
        out_shape=(
            jax.ShapeDtypeStruct((planes, rows, 2 * width), bf16),
            jax.ShapeDtypeStruct((rows, 2 * width), f32),
            jax.ShapeDtypeStruct((2, width, span), f32),
        ),
        in_specs=[smem] * 2 + [vmem] * 10,
        out_specs=(vmem,) * 3,
        scratch_shapes=[
            pltpu.VMEM((2, 8, span), f32),
            pltpu.VMEM((planes, rows, 2 * width), f32),
            pltpu.VMEM((rows, span), bf16),
            pltpu.VMEM((rows, span), bf16),
        ],
        compiler_params=params,
    )(info, meta, exps0, gprobs0, key0_t, exps, gprobs, key_t, stack, stack2, mine, theirs)

    parts = lax.all_to_all(plane, "head", 0, 0)
    sent = jnp.sum(parts.astype(f32), axis=0).astype(bf16)
    landed = lax.ppermute(sent, BOTH, back)
    dq2 = lax.ppermute(dq[1], "ctx", swap)
    d_queries = pl.pallas_call(
        queries_kernel,
        out_shape=jax.ShapeDtypeStruct(queries.shape, bf16),
        in_specs=[vmem] * 2,
        out_specs=vmem,
    )(dq, dq2)
    mine = (landed.astype(f32) + near).astype(bf16)
    every = lax.all_to_all(jnp.broadcast_to(mine, (planes, rows, 2 * width)), "head", 0, 0)
    result = jnp.sum(every.astype(f32), axis=0).astype(bf16)
    return d_queries, result[:, :width], result[:, width:]


def solution(mesh):
    in_specs = (
        P("ctx", "head"),
        P("ctx", None),
        P("ctx", None),
        P("ctx", "head"),
        P(),
        P("ctx", None),
        P("head", None),
    )
    out_specs = (P("ctx", "head"), P("ctx", None), P("ctx", None))
    return jax.shard_map(local, mesh=mesh, in_specs=in_specs, out_specs=out_specs, check_vma=False)
```

time: 93.2 us -> 85.7 us (0.920)
  the two profiles are of different devices: /device:TPU:40 before, /device:TPU:32 now
where the time goes in v3:
time: 85.7 us; the launch traced here: 85.1 us
  starting transfers between devices  34.8 us (41%)
  blocking collectives  25 us (29%)
  local copies, waits for them, and re-layouts  8.49 us (10%)
  Pallas kernels  7.44 us (9%)
  waiting for transfers between devices  7.43 us (9%)
  other arithmetic  1.15 us (1%)
    all_to_all x1, blocking collectives, local(): lax.all_to_all(jnp.broadcast_to(fetched, (planes, rows, 2 * width)), 'hea...  12.5 us
    all_to_all x1, blocking collectives, local(): parts = lax.all_to_all(plane, 'head', 0, 0)  12.4 us
    all_to_all x1, starting transfers between devices, local(): lax.all_to_all(jnp.broadcast_to(mine, (planes, rows, 2 * width)), 'head',...  11.9 us
    ppermute x1, starting transfers between devices, local(): stack2 = lax.ppermute(stack, 'ctx', swap)  11.7 us
    unnamed x18, local copies, waits for them, and re-layouts  6.89 us
    ppermute x1, starting transfers between devices, local(): dq2 = lax.ppermute(dq[1], 'ctx', swap)  5.96 us
    all_to_all x1, waiting for transfers between devices, local(): lax.all_to_all(jnp.broadcast_to(mine, (planes, rows, 2 * width)), 'head',...  5.06 us
    pallas_call x1, Pallas kernels, local(): pl.pallas_call(queries_kernel, out_shape=jax.ShapeDtypeStruct(queries.sha...  2.2 us
  transfers between devices with their start and end apart: 7, of which 3 were waited for; matrix products, arithmetic and copies ran while one was open for 1% of the time, Pallas kernels for 5%

profile of v3, /device:TPU:32, one launch (start us, length us, event | category | flops | bytes accessed | tf_op | source)
XLA Modules:
  0.0 85.1 jit_solution(3057989874501594365)
XLA Ops:
  0.6 0.9 %pad_add_fusion.own = bf16[256,256]{1,0:T(8,128)(2,1)S(1)} fusion(bf16[256,128]{1,0:T(8,128)(2,1)} %param.9, bf16[256,128]{1,0:T(8,128)(2,1)} %param.8), kind=kLoop, calls=%fused_computation.2 | loop fusion | flops 262144 | bytes 262144 | tf_op jit(solution)/shard_map/add | solution.py:234
  1.5 0.7 collective-permute-start
  2.2 0.0 copy-start.3
  2.2 0.9 %copy-done.3 = bf16[256,512]{1,0:T(8,128)(2,1)S(1)} copy-done((bf16[256,512]{1,0:T(8,128)(2,1)S(1)}, bf16[256,512]{1,0:T(8,128)(2,1)}, u32[]{:S(2)}) %copy-start.3) | copy-done | bytes 262168
  3.2 0.0 copy-start.4
  3.2 0.9 %copy-done.4 = bf16[256,512]{1,0:T(8,128)(2,1)S(1)} copy-done((bf16[256,512]{1,0:T(8,128)(2,1)S(1)}, bf16[256,512]{1,0:T(8,128)(2,1)}, u32[]{:S(2)}) %copy-start.4) | copy-done | bytes 262168
  4.1 0.6 shard_map.94
  4.8 0.0 copy-start.1
  4.8 1.0 %copy-done.1 = f32[256,1024]{1,0:T(8,128)} copy-done((f32[256,1024]{1,0:T(8,128)}, f32[256,1024]{1,0:T(8,128)S(1)}, u32[]{:S(2)}) %copy-start.1) | copy-done | bytes 1048600
  5.7 11.7 %collective-permute-start.2 = (bf16[2,1024,128]{2,1,0:T(8,128)(2,1)S(1)}, bf16[2,1024,128]{2,1,0:T(8,128)(2,1)S(1)}, u32[]{:S(2)}, u32[]{:S(2)}) collective-permute-start(bf16[2,1024,128]{2,1,0:T(8,128)(2,1)S(1)} %get-tuple-element.23.stack), channel_id=1, source_target_pairs={{0,4},{4,0},{8,12},{12,8},{16,20},{20,16},{24,28},{28,24},{32,36},... | collective-permute-start | bytes 1572872 | tf_op jit(solution)/shard_map/ppermute | solution.py:261
  17.4 1.9 %collective-permute-start.1 = (s32[1,7]{1,0:T(1,128)}, s32[1,7]{1,0:T(1,128)S(1)}, u32[]{:S(2)}, u32[]{:S(2)}) collective-permute-start(s32[1,7]{1,0:T(1,128)} %pairs.1), channel_id=1, source_target_pairs={{0,4},{4,0},{8,12},{12,8},{16,20},{20,16},{24,28},{28,24},{32,36},... | collective-permute-start | bytes 92 | tf_op jit(solution)/shard_map/ppermute | solution.py:236
  19.4 0.1 pad_add_fusion.1.info
  19.5 1.1 %collective-permute-done.1.pairs2 = s32[1,7]{1,0:T(1,128)S(1)} collective-permute-done((s32[1,7]{1,0:T(1,128)}, s32[1,7]{1,0:T(1,128)S(1)}, u32[]{:S(2)}, u32[]{:S(2)}) %collective-permute-start.1) | collective-permute-done | bytes 60 | tf_op jit(solution)/shard_map/ppermute | solution.py:236
  20.6 0.0 copy-start.5
  20.6 0.7 copy-done.5
  21.3 0.0 copy-start.6
  21.3 0.7 copy-done.6
  21.9 0.0 copy-start.7
  21.9 0.7 copy-done.7
  22.6 1.4 %shard_map.95.meta = s32[64]{0:T(128)S(1)} custom-call(s32[2]{0:T(128)S(1)} %pad_add_fusion.1.info, s32[128]{0:T(128)S(1)} %copy-done.6, s32[1,7]{1,0:T(1,128)S(1)} %copy-done.7, s32[1,7]{1,0:T(1,128)S(1)} %collective-permute-done.1.pairs2, s32[4,128]{1,0:T(4,128)S(1)} %copy-done.5), custom_call_target="tpu_custom_call" | custom-call | tf_op jit(solution)/shard_map/pallas_call | solution.py:241
  24.0 0.0 collective-permute-done
  24.1 12.5 %all_to_all.15.same = bf16[4,256,256]{2,1,0:T(8,128)(2,1)S(1)} all-to-all(bf16[4,256,256]{2,1,0:T(8,128)(2,1)S(1)} %broadcast_in_dim.6), channel_id=1, replica_groups=mesh['ctx'=128,'head'=4] {'head'}, dimensions={0} | all-to-all | bytes 1048576 | tf_op jit(solution)/shard_map/all_to_all | solution.py:263
  36.6 0.0 collective-permute-done.2.stack2
  36.6 1.3 %shard_map.96 = (f32[7,256,1024]{2,1,0:T(8,128)S(1)}, f32[7,256,1024]{2,1,0:T(8,128)S(1)}, bf16[4,128,256]{2,1,0:T(8,128)(2,1)S(1)}, f32[2,8,1024]{2,1,0:T(8,128)S(1)}) custom-call(s32[64]{0:T(128)S(1)} %shard_map.95.meta, bf16[2,1024,128]{2,1,0:T(8,128)(2,1)S(1)} %get-tuple-element.23.stack, bf16[2,1024,128]{2,1,0:T(8,128)(2,1)S(1)} %collective-permute-done.2.stack2, ...), custom_call_target="tpu_custom_call" | custom-call | tf_op jit(solution)/shard_map/pallas_call | solution.py:264
  37.9 1.9 %collective-permute-start.3 = (f32[2,8,1024]{2,1,0:T(8,128)S(1)}, f32[2,8,1024]{2,1,0:T(8,128)S(1)}, u32[]{:S(2)}, u32[]{:S(2)}) collective-permute-start(f32[2,8,1024]{2,1,0:T(8,128)S(1)} %get-tuple-element.29.mine), channel_id=1, source_target_pairs={{0,4},{4,0},{8,12},{12,8},{16,20},{20,16},{24,28},{28,24},{32,36},... | collective-permute-start | bytes 196616 | tf_op jit(solution)/shard_map/ppermute | solution.py:276
  39.8 1.2 %collective-permute-done.3.theirs = f32[2,8,1024]{2,1,0:T(8,128)S(1)} collective-permute-done((f32[2,8,1024]{2,1,0:T(8,128)S(1)}, f32[2,8,1024]{2,1,0:T(8,128)S(1)}, u32[]{:S(2)}, u32[]{:S(2)}) %collective-permute-start.3) | collective-permute-done | bytes 65568 | tf_op jit(solution)/shard_map/ppermute | solution.py:276
  41.0 0.0 copy-start.2
  41.0 1.2 %copy-done.2 = f32[256,1024]{1,0:T(8,128)S(1)} copy-done((f32[256,1024]{1,0:T(8,128)S(1)}, f32[256,1024]{1,0:T(8,128)}, u32[]{:S(2)}) %copy-start.2) | copy-done | bytes 1048600
  42.3 1.9 %shard_map.97 = (bf16[4,256,256]{2,1,0:T(8,128)(2,1)S(1)}, f32[256,256]{1,0:T(8,128)S(1)}, f32[2,128,1024]{2,1,0:T(8,128)S(1)}) custom-call(s32[2]{0:T(128)S(1)} %pad_add_fusion.1.info, s32[64]{0:T(128)S(1)} %shard_map.95.meta, f32[256,1024]{1,0:T(8,128)S(1)} %get-tuple-element.20.first_exps, f32[256,1024]{1,0:T(8,128)S(1)} %copy-done.2, ...), custom_call_target="tpu_custom_call" | custom-call | tf_op jit(solution)/shard_map/pallas_call | solution.py:277
  44.2 0.0 copy-start
  44.2 12.4 %all_to_all.16 = bf16[4,256,256]{2,1,0:T(8,128)(2,1)S(1)} all-to-all(bf16[4,256,256]{2,1,0:T(8,128)(2,1)S(1)} %get-tuple-element.31), channel_id=1, replica_groups=mesh['ctx'=128,'head'=4] {'head'}, dimensions={0} | all-to-all | bytes 1048576 | tf_op jit(solution)/shard_map/all_to_all | solution.py:295
  56.6 0.1 reduce_sum.24
  56.7 0.7 collective-permute-start.5
  57.4 6.0 %collective-permute-start.4 = (f32[128,1024]{1,0:T(8,128)S(1)}, f32[128,1024]{1,0:T(8,128)S(1)}, u32[]{:S(2)}, u32[]{:S(2)}) collective-permute-start(f32[128,1024]{1,0:T(8,128)S(1)} %slice_bitcast_fusion), channel_id=1, source_target_pairs={{0,4},{4,0},{8,12},{12,8},{16,20},{20,16},{24,28},{28,24},{32,36},... | collective-permute-start | bytes 1572872 | tf_op jit(solution)/shard_map/ppermute | solution.py:298
  63.4 0.0 collective-permute-done.5
  63.5 0.9 %broadcast_in_dim.7 = bf16[4,256,256]{2,1,0:T(8,128)(2,1)} broadcast(bf16[256,256]{1,0:T(8,128)(2,1)S(1)} %add_convert_fusion), dimensions={1,2} | broadcast | bytes 655360 | tf_op jit(solution)/shard_map/broadcast_in_dim | solution.py:306
  64.3 11.9 %all-to-all-start.2 = ((bf16[4,256,256]{2,1,0:T(8,128)(2,1)}), bf16[4,256,256]{2,1,0:T(8,128)(2,1)S(1)}, u32[]{:S(2)}, u32[]{:S(2)}) async-start(bf16[4,256,256]{2,1,0:T(8,128)(2,1)} %broadcast_in_dim.7), calls=%async_computation.2 | async-start | bytes 1048576 | tf_op jit(solution)/shard_map/all_to_all | solution.py:306
  76.3 0.0 collective-permute-done.4.theirs
  76.3 0.0 copy-done
  76.3 0.0 copy-start.8
  76.3 0.8 copy-done.8
  77.1 2.2 %shard_map.98 = bf16[256,512]{1,0:T(8,128)(2,1)} custom-call(f32[2,128,1024]{2,1,0:T(8,128)} %copy-done, f32[128,1024]{1,0:T(8,128)} %copy-done.8), custom_call_target="tpu_custom_call" | custom-call | tf_op jit(solution)/shard_map/pallas_call | solution.py:299
  79.3 5.1 %all-to-all-done.2 = bf16[4,256,256]{2,1,0:T(8,128)(2,1)S(1)} async-done(((bf16[4,256,256]{2,1,0:T(8,128)(2,1)}), bf16[4,256,256]{2,1,0:T(8,128)(2,1)S(1)}, u32[]{:S(2)}, u32[]{:S(2)}) %all-to-all-start.2) | async-done | bytes 524320 | tf_op jit(solution)/shard_map/all_to_all | solution.py:306
  84.3 0.1 reduce_sum.25
  84.4 0.7 fusion
  (3 shorter events, 0.1 us)
Async XLA Ops:
  1.5 22.5 %collective-permute-start = (bf16[256,256]{1,0:T(8,128)(2,1)S(1)}, bf16[256,256]{1,0:T(8,128)(2,1)S(1)}, u32[]{:S(2)}, u32[]{:S(2)}) collective-permute-start(bf16[256,256]{1,0:T(8,128)(2,1)S(1)} %pad_add_fusion.own), channel_id=1, source_target_pairs={{0,0},{8,8},{1,9},{7,15},{16,16},{9,17},{2,18},{6,22},{15,23},{24,... | collective-permute-start | bytes 393224 | tf_op jit(solution)/shard_map/ppermute | solution.py:235
  2.2 1.0 %copy-start.3 = (bf16[256,512]{1,0:T(8,128)(2,1)S(1)}, bf16[256,512]{1,0:T(8,128)(2,1)}, u32[]{:S(2)}) copy-start(bf16[256,512]{1,0:T(8,128)(2,1)} %q_ref.1) | copy-start | bytes 786436
  3.2 0.9 %copy-start.4 = (bf16[256,512]{1,0:T(8,128)(2,1)S(1)}, bf16[256,512]{1,0:T(8,128)(2,1)}, u32[]{:S(2)}) copy-start(bf16[256,512]{1,0:T(8,128)(2,1)} %g_ref.1) | copy-start | bytes 786436
  4.8 1.0 %copy-start.1 = (f32[256,1024]{1,0:T(8,128)}, f32[256,1024]{1,0:T(8,128)S(1)}, u32[]{:S(2)}) copy-start(f32[256,1024]{1,0:T(8,128)S(1)} %get-tuple-element.21.first_gprobs) | copy-start | bytes 3145732
  5.7 30.9 %collective-permute-start.2 = (bf16[2,1024,128]{2,1,0:T(8,128)(2,1)S(1)}, bf16[2,1024,128]{2,1,0:T(8,128)(2,1)S(1)}, u32[]{:S(2)}, u32[]{:S(2)}) collective-permute-start(bf16[2,1024,128]{2,1,0:T(8,128)(2,1)S(1)} %get-tuple-element.23.stack), channel_id=1, source_target_pairs={{0,4},{4,0},{8,12},{12,8},{16,20},{20,16},{24,28},{28,24},{32,36},... | collective-permute-start | bytes 1572872 | tf_op jit(solution)/shard_map/ppermute | solution.py:261
  17.4 3.2 %collective-permute-start.1 = (s32[1,7]{1,0:T(1,128)}, s32[1,7]{1,0:T(1,128)S(1)}, u32[]{:S(2)}, u32[]{:S(2)}) collective-permute-start(s32[1,7]{1,0:T(1,128)} %pairs.1), channel_id=1, source_target_pairs={{0,4},{4,0},{8,12},{12,8},{16,20},{20,16},{24,28},{28,24},{32,36},... | collective-permute-start | bytes 92 | tf_op jit(solution)/shard_map/ppermute | solution.py:236
  20.6 0.7 copy-start.5
  21.3 0.7 copy-start.6
  21.9 0.7 copy-start.7
  37.9 3.1 %collective-permute-start.3 = (f32[2,8,1024]{2,1,0:T(8,128)S(1)}, f32[2,8,1024]{2,1,0:T(8,128)S(1)}, u32[]{:S(2)}, u32[]{:S(2)}) collective-permute-start(f32[2,8,1024]{2,1,0:T(8,128)S(1)} %get-tuple-element.29.mine), channel_id=1, source_target_pairs={{0,4},{4,0},{8,12},{12,8},{16,20},{20,16},{24,28},{28,24},{32,36},... | collective-permute-start | bytes 196616 | tf_op jit(solution)/shard_map/ppermute | solution.py:276
  41.0 1.2 %copy-start.2 = (f32[256,1024]{1,0:T(8,128)S(1)}, f32[256,1024]{1,0:T(8,128)}, u32[]{:S(2)}) copy-start(f32[256,1024]{1,0:T(8,128)} %copy-done.1) | copy-start | bytes 3145732
  44.2 32.1 %copy-start = (f32[2,128,1024]{2,1,0:T(8,128)}, f32[2,128,1024]{2,1,0:T(8,128)S(1)}, u32[]{:S(2)}) copy-start(f32[2,128,1024]{2,1,0:T(8,128)S(1)} %get-tuple-element.30.mine) | copy-start | bytes 3145732
  56.7 6.7 %collective-permute-start.5 = (bf16[256,256]{1,0:T(8,128)(2,1)S(1)}, bf16[256,256]{1,0:T(8,128)(2,1)S(1)}, u32[]{:S(2)}, u32[]{:S(2)}) collective-permute-start(bf16[256,256]{1,0:T(8,128)(2,1)S(1)} %reduce_sum.24), channel_id=1, source_target_pairs={{9,1},{15,7},{17,9},{18,2},{22,6},{23,15},{25,17},{26,10},{27,3},{... | collective-permute-start | bytes 393224 | tf_op jit(solution)/shard_map/ppermute | solution.py:297
  57.4 18.8 %collective-permute-start.4 = (f32[128,1024]{1,0:T(8,128)S(1)}, f32[128,1024]{1,0:T(8,128)S(1)}, u32[]{:S(2)}, u32[]{:S(2)}) collective-permute-start(f32[128,1024]{1,0:T(8,128)S(1)} %slice_bitcast_fusion), channel_id=1, source_target_pairs={{0,4},{4,0},{8,12},{12,8},{16,20},{20,16},{24,28},{28,24},{32,36},... | collective-permute-start | bytes 1572872 | tf_op jit(solution)/shard_map/ppermute | solution.py:298
  64.3 20.0 %all-to-all-start.2 = ((bf16[4,256,256]{2,1,0:T(8,128)(2,1)}), bf16[4,256,256]{2,1,0:T(8,128)(2,1)S(1)}, u32[]{:S(2)}, u32[]{:S(2)}) async-start(bf16[4,256,256]{2,1,0:T(8,128)(2,1)} %broadcast_in_dim.7), calls=%async_computation.2 | async-start | bytes 1048576 | tf_op jit(solution)/shard_map/all_to_all | solution.py:306
  76.3 0.8 copy-start.8

commit v4 on v3

v4 whole, which is shorter than its diff:
```python
import functools

import jax
import jax.numpy as jnp
from jax import lax
from jax.experimental import pallas as pl
from jax.experimental.pallas import tpu as pltpu
from jax.sharding import PartitionSpec as P

NEG = -1e30
BOTH = ("ctx", "head")
NT = (((1,), (1,)), ((), ()))
GRANT = 12


KEEP, OTHER = 8, 24


def list_kernel(info, docs, pairs, knock, early):
    heads, slots = knock.shape[0], (pairs.shape[1] + 1) // 2
    here, side = info[0], info[1]
    early[0] = 0
    for d in range(slots + 1):
        block = jnp.maximum(here - 2 * d, 0)
        kept = functools.reduce(jnp.logical_or, [knock[h, block] == 1 for h in range(heads)])
        kept = kept & (here - 2 * d >= 0)
        back = 2 * d + 1 - 2 * side
        query = here + 1 - 2 * side
        candidate = (back > 0) & (back < 2 * slots) & kept & (docs[block] == docs[query])
        early[OTHER + d] = jnp.where(candidate, 1, 0)
        for h in range(heads):
            early[32 + heads * d + h] = knock[h, block]
        if 0 < d < slots:
            listed = functools.reduce(
                jnp.logical_or, [pairs[0, k] == 2 * d for k in range(pairs.shape[1])]
            )

            @pl.when(kept & listed & (docs[block] == docs[here]))
            def _(d=d, block=block):
                entry = early[0]
                early[1 + entry] = jnp.where(side == 0, d, slots - d)
                for h in range(heads):
                    early[KEEP + heads * entry + h] = knock[h, block]
                early[0] = entry + 1


def first_kernel(q_ref, g_ref, own, pairs, exps, gprobs, key_t, stack, stats):
    rows, width = own.shape[0], own.shape[1] // 2
    heads = q_ref.shape[1] // width
    span = heads * rows
    scale = width ** (-0.5)
    f32 = jnp.float32

    for h in range(heads):
        part, cols = slice(h * rows, (h + 1) * rows), slice(h * width, (h + 1) * width)
        stack[h * rows : (h + 1) * rows] = q_ref[:, cols]
        stack[span + h * rows : span + (h + 1) * rows] = g_ref[:, cols]
    stack[2 * span :] = jnp.zeros((16, width), stack.dtype)
    listed = jnp.broadcast_to(pairs[...].astype(f32), (16, pairs.shape[1]))
    stack[2 * span :, : pairs.shape[1]] = listed.astype(stack.dtype)
    key_t[...] = own[:, :width].T
    stats[...] = jnp.zeros_like(stats)
    below = lax.broadcasted_iota(jnp.int32, (rows, rows), 0) <= lax.broadcasted_iota(
        jnp.int32, (rows, rows), 1
    )
    for h in range(heads):
        part, cols = slice(h * rows, (h + 1) * rows), slice(h * width, (h + 1) * width)
        s = lax.dot_general(own[:, :width], q_ref[:, cols], NT, preferred_element_type=f32) * scale
        g = lax.dot_general(own[:, width:], g_ref[:, cols], NT, preferred_element_type=f32)
        s = jnp.where(below, s, NEG)
        top = jnp.max(s, axis=0, keepdims=True)
        e = jnp.exp(s - top)
        exps[:, part] = e
        gprobs[:, part] = g
        stats[0:1, part] = top
        stats[1:2, part] = jnp.sum(e, axis=0, keepdims=True)
        stats[2:3, part] = jnp.sum(e * g, axis=0, keepdims=True)


def scores_kernel(info, early, stack, stack2, first_stats, same, exps, gprobs, key_t, stats, late):
    slots, rows, width = same.shape[0], same.shape[1], same.shape[2] // 2
    span = (stack.shape[0] - 16) // 2
    heads = span // rows
    scale = width ** (-0.5)
    side = info[1]
    f32 = jnp.float32

    table = stack2[2 * span :].astype(f32)[0:1]
    bits = jnp.zeros_like(table)
    for d in range(slots + 1):
        back = 2 * d + 1 - 2 * side
        match = (table == back.astype(f32)) & (back > 0)
        bits = bits + jnp.where(match, float(1 << d), 0.0)
    bits = jnp.sum(bits).astype(jnp.int32)
    late[0] = 0
    for d in range(slots + 1):
        @pl.when((early[OTHER + d] == 1) & (((bits >> d) & 1) == 1))
        def _(d=d):
            entry = late[0]
            late[1 + entry] = jnp.where(side == 0, d, slots - d)
            for h in range(heads):
                late[KEEP + heads * entry + h] = early[32 + heads * d + h]
            late[0] = entry + 1

    stats[...] = jnp.zeros_like(stats)
    for which in range(2):
        stats[which, 0:1] = jnp.full((1, span), NEG, f32)
    stats[0, 3:6] = first_stats[0:3]

    for which, both, meta in ((0, stack, early), (1, stack2, late)):
        base = (slots - 1) * which

        def first(k, carry, which=which, both=both, base=base, meta=meta):
            i, slot = base + k, meta[1 + k]
            key_t[slot] = same[slot, :, :width].T
            for h in range(heads):
                part = slice(h * rows, (h + 1) * rows)
                s = lax.dot_general(
                    same[slot, :, :width], both[part], NT, preferred_element_type=f32
                )
                s = s * scale + jnp.where(meta[KEEP + heads * k + h] == 1, 0.0, NEG).astype(f32)
                exps[i, :, part] = s
                stats[which, 0:1, part] = jnp.maximum(
                    stats[which, 0:1, part], jnp.max(s, axis=0, keepdims=True)
                )
            return carry

        def second(k, carry, which=which, both=both, base=base, meta=meta):
            i, slot = base + k, meta[1 + k]
            for h in range(heads):
                part = slice(h * rows, (h + 1) * rows)
                g = lax.dot_general(
                    same[slot, :, width:], both[span + h * rows : span + (h + 1) * rows], NT, preferred_element_type=f32
                )
                e = jnp.exp(exps[i, :, part] - stats[which, 0:1, part])
                gprobs[i, :, part] = g
                exps[i, :, part] = e
                stats[which, 1:2, part] += jnp.sum(e, axis=0, keepdims=True)
                stats[which, 2:3, part] += jnp.sum(e * g, axis=0, keepdims=True)
            return carry

        lax.fori_loop(0, meta[0], first, 0)
        lax.fori_loop(0, meta[0], second, 0)


def terms_kernel(
    info, early, late, first_exps, first_gprobs, first_key_t, exps, gprobs, key_t, stack, stack2, mine, theirs,
    plane_ref, near_ref, dq_ref, factors, acc, probs, grads,
):
    rows, width = exps.shape[1], stack.shape[1]
    span = exps.shape[2]
    slots = plane_ref.shape[0]
    scale = width ** (-0.5)
    side = info[1]
    stacks = (stack, stack2)
    f32, bf16 = jnp.float32, jnp.bfloat16

    def three(ref, which, row):
        return ref[which, row : row + 1], ref[which, row + 1 : row + 2], ref[which, row + 2 : row + 3]

    groups = (
        (three(mine, 0, 0), three(mine, 0, 3), three(theirs, 1, 0)),
        (three(mine, 1, 0), three(theirs, 0, 0), three(theirs, 0, 3)),
    )
    for which, group in enumerate(groups):
        high = functools.reduce(jnp.maximum, [top for top, _, _ in group])
        shares = [jnp.exp(top - high) for top, _, _ in group]
        total = sum(share * part for share, (_, part, _) in zip(shares, group))
        weighted = sum(share * part for share, (_, _, part) in zip(shares, group))
        inverse = 1.0 / total
        factors[which, 0:1] = shares[0] * inverse
        factors[which, 1:2] = weighted * inverse
        factors[which, 2:3] = shares[1] * inverse

    def gradients(load_e, load_g, keys, which, row):
        for h in range(span // rows):
            part = slice(h * rows, (h + 1) * rows)
            p = load_e(part) * factors[which, row : row + 1, part]
            probs[:, part] = p.astype(bf16)
            grads[:, part] = (p * (load_g(part) - factors[which, 1:2, part])).astype(bf16)
        key_term = jnp.dot(grads[...], stacks[which][:span], preferred_element_type=f32) * scale
        value_term = jnp.dot(probs[...], stacks[which][span : 2 * span], preferred_element_type=f32)
        return key_term, value_term, jnp.dot(keys, grads[...], preferred_element_type=f32)

    acc[...] = jnp.zeros_like(acc)
    key_term, value_term, dq_ref[0] = gradients(
        lambda part: first_exps[:, part], lambda part: first_gprobs[:, part], first_key_t[...], 0, 2
    )
    dq_ref[1] = jnp.zeros(dq_ref.shape[1:], f32)
    near_ref[:, :width] = key_term
    near_ref[:, width:] = value_term

    for which, meta in ((0, early), (1, late)):
        def step(k, carry, which=which, meta=meta):
            i, slot = (slots - 1) * which + k, meta[1 + k]
            key_term, value_term, query_term = gradients(
                lambda part: exps[i, :, part], lambda part: gprobs[i, :, part], key_t[slot], which, 0
            )
            dq_ref[which] += query_term
            acc[slot, :, :width] += key_term
            acc[slot, :, width:] += value_term
            return carry

        lax.fori_loop(0, meta[0], step, 0)
    for slot in range(1, slots):
        plane_ref[slot] = acc[slot].astype(bf16)

    @pl.when(side == 0)
    def _():
        near_ref[...] += acc[0]
        plane_ref[0] = jnp.zeros(plane_ref.shape[1:], bf16)

    @pl.when(side == 1)
    def _():
        plane_ref[0] = acc[0].astype(bf16)


def queries_kernel(mine, theirs, dq_ref):
    width, rows = mine.shape[1], dq_ref.shape[0]
    scale = width ** (-0.5)
    for h in range(dq_ref.shape[1] // width):
        part = slice(h * rows, (h + 1) * rows)
        dq = (mine[0, :, part] + theirs[:, part]) * scale
        dq_ref[:, h * width : (h + 1) * width] = dq.T.astype(dq_ref.dtype)


def plane_pairs(blocks, planes):
    pairs = []
    for block in range(blocks):
        for plane in range(planes):
            source = block - 2 * (plane if block % 2 == 0 else planes - plane)
            if source >= 0:
                pairs.append((source * planes + plane, block * planes + plane))
    return pairs


def local(queries, keys, values, grad_out, doc_of_block, pair_list, knock):
    rows, width = keys.shape
    heads = queries.shape[1] // width
    reach = pair_list.shape[1] + 1
    blocks = doc_of_block.shape[0]
    planes = lax.axis_size("head")
    here = lax.axis_index("ctx")
    info = jnp.stack([here, here % 2])
    out = plane_pairs(blocks, planes)
    back = [(b, a) for a, b in out if a != b]
    swap = [(i, i ^ 1) for i in range(blocks)]
    bf16, f32 = jnp.bfloat16, jnp.float32
    span = heads * rows

    edge = jnp.zeros((), bf16)
    own = lax.pad(keys, edge, ((0, 0, 0), (0, width, 0))) + lax.pad(values, edge, ((0, 0, 0), (width, 0, 0)))
    fetched = lax.ppermute(own, BOTH, out)
    vmem = pl.BlockSpec(memory_space=pltpu.VMEM)
    smem = pl.BlockSpec(memory_space=pltpu.SMEM)

    def grant(mebibytes):
        return pltpu.CompilerParams(vmem_limit_bytes=mebibytes << 20)

    work = pl.CostEstimate(flops=10**10, bytes_accessed=1 << 22, transcendentals=0)
    lists = jax.ShapeDtypeStruct((32 + heads * (planes + 1),), jnp.int32)
    early = pl.pallas_call(
        list_kernel,
        out_shape=lists,
        in_specs=[smem] * 4,
        out_specs=smem,
        compiler_params=grant(GRANT),
        cost_estimate=work,
    )(info, doc_of_block, pair_list, knock)
    exps0, gprobs0, key0_t, stack, stats0 = pl.pallas_call(
        first_kernel,
        out_shape=(
            pltpu.VMEM((rows, span), f32),
            pltpu.VMEM((rows, span), f32),
            pltpu.VMEM((width, rows), bf16),
            jax.ShapeDtypeStruct((2 * span + 16, width), bf16),
            jax.ShapeDtypeStruct((8, span), f32),
        ),
        in_specs=[vmem] * 4,
        out_specs=(vmem,) * 5,
        compiler_params=grant(GRANT),
        cost_estimate=work,
    )(queries, grad_out, own, pair_list)
    stack2 = lax.ppermute(stack, "ctx", swap)
    fetched, stats0, early = lax.optimization_barrier((fetched, stats0, early))
    same = lax.all_to_all(jnp.broadcast_to(fetched, (planes, rows, 2 * width)), "head", 0, 0)
    exps, gprobs, key_t, mine, late = pl.pallas_call(
        scores_kernel,
        out_shape=(
            pltpu.VMEM((reach - 1, rows, span), f32),
            pltpu.VMEM((reach - 1, rows, span), f32),
            pltpu.VMEM((planes, width, rows), bf16),
            jax.ShapeDtypeStruct((2, 8, span), f32),
            lists,
        ),
        in_specs=[smem] * 2 + [vmem] * 4,
        out_specs=(vmem,) * 4 + (smem,),
        compiler_params=grant(GRANT),
    )(info, early, stack, stack2, stats0, same)
    theirs = lax.ppermute(mine, "ctx", swap)
    plane, near, dq = pl.pallas_call(
        terms_kernel,
        out_shape=(
            jax.ShapeDtypeStruct((planes, rows, 2 * width), bf16),
            jax.ShapeDtypeStruct((rows, 2 * width), f32),
            jax.ShapeDtypeStruct((2, width, span), f32),
        ),
        in_specs=[smem] * 3 + [vmem] * 10,
        out_specs=(vmem,) * 3,
        scratch_shapes=[
            pltpu.VMEM((2, 8, span), f32),
            pltpu.VMEM((planes, rows, 2 * width), f32),
            pltpu.VMEM((rows, span), bf16),
            pltpu.VMEM((rows, span), bf16),
        ],
        compiler_params=grant(GRANT),
    )(info, early, late, exps0, gprobs0, key0_t, exps, gprobs, key_t, stack, stack2, mine, theirs)

    parts = lax.all_to_all(plane, "head", 0, 0)
    sent = jnp.sum(parts.astype(f32), axis=0).astype(bf16)
    landed = lax.ppermute(sent, BOTH, back)
    dq2 = lax.ppermute(dq[1], "ctx", swap)
    d_queries = pl.pallas_call(
        queries_kernel,
        out_shape=jax.ShapeDtypeStruct(queries.shape, bf16),
        in_specs=[vmem] * 2,
        out_specs=vmem,
    )(dq, dq2)
    mine = (landed.astype(f32) + near).astype(bf16)
    every = lax.all_to_all(jnp.broadcast_to(mine, (planes, rows, 2 * width)), "head", 0, 0)
    d_keys = sum(every[i, :, :width].astype(f32) for i in range(planes)).astype(bf16)
    d_values = sum(every[i, :, width:].astype(f32) for i in range(planes)).astype(bf16)
    return d_queries, d_keys, d_values


def solution(mesh):
    in_specs = (
        P("ctx", "head"),
        P("ctx", None),
        P("ctx", None),
        P("ctx", "head"),
        P(),
        P("ctx", None),
        P("head", None),
    )
    out_specs = (P("ctx", "head"), P("ctx", None), P("ctx", None))
    return jax.shard_map(local, mesh=mesh, in_specs=in_specs, out_specs=out_specs, check_vma=False)
```

time: 85.7 us -> 80.1 us (0.935)
  the two profiles are of different devices: /device:TPU:32 before, /device:TPU:24 now
where the time goes in v4:
time: 80.1 us; the launch traced here: 79.7 us
  starting transfers between devices  33.7 us (42%)
  blocking collectives  24.8 us (31%)
  Pallas kernels  6.85 us (9%)
  waiting for transfers between devices  6.38 us (8%)
  local copies, waits for them, and re-layouts  5.28 us (7%)
  other arithmetic  1.8 us (2%)
    all_to_all x1, blocking collectives, local(): parts = lax.all_to_all(plane, 'head', 0, 0)  12.5 us
    all_to_all x1, blocking collectives, local(): lax.all_to_all(jnp.broadcast_to(fetched, (planes, rows, 2 * width)), 'hea...  12.3 us
    ppermute x1, starting transfers between devices, local(): stack2 = lax.ppermute(stack, 'ctx', swap)  11.7 us
    ppermute x1, starting transfers between devices, local(): dq2 = lax.ppermute(dq[1], 'ctx', swap)  9.75 us
    all_to_all x1, starting transfers between devices, local(): lax.all_to_all(jnp.broadcast_to(mine, (planes, rows, 2 * width)), 'head',...  9.04 us
    all_to_all x1, waiting for transfers between devices, local(): lax.all_to_all(jnp.broadcast_to(mine, (planes, rows, 2 * width)), 'head',...  5.15 us
    unnamed x20, local copies, waits for them, and re-layouts  4.35 us
    pallas_call x1, Pallas kernels, local(): pl.pallas_call(queries_kernel, out_shape=jax.ShapeDtypeStruct(queries.sha...  2.2 us
  transfers between devices with their start and end apart: 6, of which 2 were waited for; matrix products, arithmetic and copies ran while one was open for 1% of the time, Pallas kernels for 5%

profile of v4, /device:TPU:24, one launch (start us, length us, event | category | flops | bytes accessed | tf_op | source)
XLA Modules:
  0.0 79.7 jit_solution(7248898039182183849)
XLA Ops:
  0.6 0.9 %pad_add_fusion.own = bf16[256,256]{1,0:T(8,128)(2,1)S(1)} fusion(bf16[256,128]{1,0:T(8,128)(2,1)} %param.9, bf16[256,128]{1,0:T(8,128)(2,1)} %param.8), kind=kLoop, calls=%fused_computation.4 | loop fusion | flops 262144 | bytes 262144 | tf_op jit(solution)/shard_map/add | solution.py:252
  1.5 0.7 collective-permute-start
  2.2 0.0 copy-start.3
  2.2 0.9 %copy-done.3 = bf16[256,512]{1,0:T(8,128)(2,1)S(1)} copy-done((bf16[256,512]{1,0:T(8,128)(2,1)S(1)}, bf16[256,512]{1,0:T(8,128)(2,1)}, u32[]{:S(2)}) %copy-start.3) | copy-done | bytes 262168
  3.2 0.0 copy-start.4
  3.2 0.9 %copy-done.4 = bf16[256,512]{1,0:T(8,128)(2,1)S(1)} copy-done((bf16[256,512]{1,0:T(8,128)(2,1)S(1)}, bf16[256,512]{1,0:T(8,128)(2,1)}, u32[]{:S(2)}) %copy-start.4) | copy-done | bytes 262168
  4.1 0.0 copy-start.7
  4.1 0.7 copy-done.7
  4.8 0.0 copy-start.5
  4.8 0.0 copy-start.6
  4.8 0.0 copy-start.8
  4.8 0.7 shard_map.94
  5.5 0.0 copy-start.1
  5.5 1.0 %copy-done.1 = f32[256,1024]{1,0:T(8,128)} copy-done((f32[256,1024]{1,0:T(8,128)}, f32[256,1024]{1,0:T(8,128)S(1)}, u32[]{:S(2)}) %copy-start.1) | copy-done | bytes 1048600
  6.4 11.7 %collective-permute-start.1 = (bf16[2064,128]{1,0:T(8,128)(2,1)S(1)}, bf16[2064,128]{1,0:T(8,128)(2,1)S(1)}, u32[]{:S(2)}, u32[]{:S(2)}) collective-permute-start(bf16[2064,128]{1,0:T(8,128)(2,1)S(1)} %get-tuple-element.21.stack), channel_id=1, source_target_pairs={{0,4},{4,0},{8,12},{12,8},{16,20},{20,16},{24,28},{28,24},{32,36},... | collective-permute-start | bytes 1585160 | tf_op jit(solution)/shard_map/ppermute | solution.py:284
  18.2 0.1 pad_add_fusion.1.info
  18.2 0.0 copy-done.5
  18.2 0.0 copy-done.6
  18.2 0.0 copy-done.8
  18.2 0.0 copy-start.2
  18.3 1.3 %shard_map.95.early = s32[52]{0:T(128)S(1)} custom-call(s32[2]{0:T(128)S(1)} %pad_add_fusion.1.info, s32[128]{0:T(128)S(1)} %copy-done.6, s32[1,7]{1,0:T(1,128)S(1)} %copy-done.8, s32[4,128]{1,0:T(4,128)S(1)} %copy-done.5), custom_call_target="tpu_custom_call" | custom-call | flops 10000000000 | bytes 4194304 | tf_op jit(solution)/shard_map/pallas_call | solution.py:262
  19.6 0.0 collective-permute-done
  19.6 12.3 %all_to_all.15.same = bf16[4,256,256]{2,1,0:T(8,128)(2,1)S(1)} all-to-all(bf16[4,256,256]{2,1,0:T(8,128)(2,1)S(1)} %broadcast_in_dim.6), channel_id=1, replica_groups=mesh['ctx'=128,'head'=4] {'head'}, dimensions={0} | all-to-all | bytes 1048576 | tf_op jit(solution)/shard_map/all_to_all | solution.py:286
  31.9 0.0 collective-permute-done.1.stack2
  31.9 1.3 %shard_map.96 = (f32[7,256,1024]{2,1,0:T(8,128)S(1)}, f32[7,256,1024]{2,1,0:T(8,128)S(1)}, bf16[4,128,256]{2,1,0:T(8,128)(2,1)S(1)}, f32[2,8,1024]{2,1,0:T(8,128)S(1)}, s32[52]{0:T(128)S(1)}) custom-call(s32[2]{0:T(128)S(1)} %pad_add_fusion.1.info, s32[52]{0:T(128)S(1)} %shard_map.95.early, bf16[2064,128]{1,0:T(8,128)(2,1)S(1)} %get-tuple-element.21.stack, ...), custom_call_target="tpu_custom_call" | custom-call | tf_op jit(solution)/shard_map/pallas_call | solution.py:287
  33.3 1.9 %collective-permute-start.2 = (f32[2,8,1024]{2,1,0:T(8,128)S(1)}, f32[2,8,1024]{2,1,0:T(8,128)S(1)}, u32[]{:S(2)}, u32[]{:S(2)}) collective-permute-start(f32[2,8,1024]{2,1,0:T(8,128)S(1)} %get-tuple-element.31.mine), channel_id=1, source_target_pairs={{0,4},{4,0},{8,12},{12,8},{16,20},{20,16},{24,28},{28,24},{32,36},... | collective-permute-start | bytes 196616 | tf_op jit(solution)/shard_map/ppermute | solution.py:300
  35.2 1.2 %collective-permute-done.2.theirs = f32[2,8,1024]{2,1,0:T(8,128)S(1)} collective-permute-done((f32[2,8,1024]{2,1,0:T(8,128)S(1)}, f32[2,8,1024]{2,1,0:T(8,128)S(1)}, u32[]{:S(2)}, u32[]{:S(2)}) %collective-permute-start.2) | collective-permute-done | bytes 65568 | tf_op jit(solution)/shard_map/ppermute | solution.py:300
  36.4 0.0 copy-done.2
  36.4 1.3 %shard_map.97 = (bf16[4,256,256]{2,1,0:T(8,128)(2,1)S(1)}, f32[256,256]{1,0:T(8,128)S(1)}, f32[2,128,1024]{2,1,0:T(8,128)S(1)}) custom-call(s32[2]{0:T(128)S(1)} %pad_add_fusion.1.info, s32[52]{0:T(128)S(1)} %shard_map.95.early, s32[52]{0:T(128)S(1)} %get-tuple-element.24.late, f32[256,1024]{1,0:T(8,128)S(1)} %get-tuple-element.25.first_exps, ...), custom_call_target="tpu_custom_call" | custom-call | tf_op jit(solution)/shard_map/pallas_call | solution.py:301
  37.8 0.0 copy-start
  37.8 12.5 %all_to_all.16 = bf16[4,256,256]{2,1,0:T(8,128)(2,1)S(1)} all-to-all(bf16[4,256,256]{2,1,0:T(8,128)(2,1)S(1)} %get-tuple-element.33), channel_id=1, replica_groups=mesh['ctx'=128,'head'=4] {'head'}, dimensions={0} | all-to-all | bytes 1048576 | tf_op jit(solution)/shard_map/all_to_all | solution.py:319
  50.2 0.1 reduce_sum.12
  50.3 0.7 collective-permute-start.4
  51.1 9.7 %collective-permute-start.3 = (f32[128,1024]{1,0:T(8,128)S(1)}, f32[128,1024]{1,0:T(8,128)S(1)}, u32[]{:S(2)}, u32[]{:S(2)}) collective-permute-start(f32[128,1024]{1,0:T(8,128)S(1)} %slice_bitcast_fusion), channel_id=1, source_target_pairs={{0,4},{4,0},{8,12},{12,8},{16,20},{20,16},{24,28},{28,24},{32,36},... | collective-permute-start | bytes 1572872 | tf_op jit(solution)/shard_map/ppermute | solution.py:322
  60.8 0.0 collective-permute-done.4
  60.9 0.9 %broadcast_in_dim.7 = bf16[4,256,256]{2,1,0:T(8,128)(2,1)} broadcast(bf16[256,256]{1,0:T(8,128)(2,1)S(1)} %add_convert_fusion), dimensions={1,2} | broadcast | bytes 655360 | tf_op jit(solution)/shard_map/broadcast_in_dim | solution.py:330
  61.7 9.0 %all-to-all-start.2 = ((bf16[4,256,256]{2,1,0:T(8,128)(2,1)}), bf16[4,256,256]{2,1,0:T(8,128)(2,1)S(1)}, u32[]{:S(2)}, u32[]{:S(2)}) async-start(bf16[4,256,256]{2,1,0:T(8,128)(2,1)} %broadcast_in_dim.7), calls=%async_computation.2 | async-start | bytes 1048576 | tf_op jit(solution)/shard_map/all_to_all | solution.py:330
  70.8 0.0 collective-permute-done.3.theirs
  70.8 0.0 copy-done
  70.8 0.0 copy-start.9
  70.8 0.8 %copy-done.9 = f32[128,1024]{1,0:T(8,128)} copy-done((f32[128,1024]{1,0:T(8,128)}, f32[128,1024]{1,0:T(8,128)S(1)}, u32[]{:S(2)}) %copy-start.9) | copy-done | bytes 524312
  71.6 2.2 %shard_map.98 = bf16[256,512]{1,0:T(8,128)(2,1)} custom-call(f32[2,128,1024]{2,1,0:T(8,128)} %copy-done, f32[128,1024]{1,0:T(8,128)} %copy-done.9), custom_call_target="tpu_custom_call" | custom-call | tf_op jit(solution)/shard_map/pallas_call | solution.py:323
  73.8 5.1 %all-to-all-done.2 = bf16[4,256,256]{2,1,0:T(8,128)(2,1)S(1)} async-done(((bf16[4,256,256]{2,1,0:T(8,128)(2,1)}), bf16[4,256,256]{2,1,0:T(8,128)(2,1)S(1)}, u32[]{:S(2)}, u32[]{:S(2)}) %all-to-all-start.2) | async-done | bytes 524320 | tf_op jit(solution)/shard_map/all_to_all | solution.py:330
  78.9 0.7 fusion.1
  (3 shorter events, 0.1 us)
Async XLA Ops:
  1.5 18.0 %collective-permute-start = (bf16[256,256]{1,0:T(8,128)(2,1)S(1)}, bf16[256,256]{1,0:T(8,128)(2,1)S(1)}, u32[]{:S(2)}, u32[]{:S(2)}) collective-permute-start(bf16[256,256]{1,0:T(8,128)(2,1)S(1)} %pad_add_fusion.own), channel_id=1, source_target_pairs={{0,0},{8,8},{1,9},{7,15},{16,16},{9,17},{2,18},{6,22},{15,23},{24,... | collective-permute-start | bytes 393224 | tf_op jit(solution)/shard_map/ppermute | solution.py:253
  2.2 1.0 %copy-start.3 = (bf16[256,512]{1,0:T(8,128)(2,1)S(1)}, bf16[256,512]{1,0:T(8,128)(2,1)}, u32[]{:S(2)}) copy-start(bf16[256,512]{1,0:T(8,128)(2,1)} %q_ref.1) | copy-start | bytes 786436
  3.2 0.9 %copy-start.4 = (bf16[256,512]{1,0:T(8,128)(2,1)S(1)}, bf16[256,512]{1,0:T(8,128)(2,1)}, u32[]{:S(2)}) copy-start(bf16[256,512]{1,0:T(8,128)(2,1)} %g_ref.1) | copy-start | bytes 786436
  4.1 0.7 copy-start.7
  4.8 13.5 %copy-start.5 = (s32[4,128]{1,0:T(4,128)S(1)}, s32[4,128]{1,0:T(4,128)}, u32[]{:S(2)}) copy-start(s32[4,128]{1,0:T(4,128)} %knock.1) | copy-start | bytes 6148
  4.8 13.5 %copy-start.6 = (s32[128]{0:T(128)S(1)}, s32[128]{0:T(128)}, u32[]{:S(2)}) copy-start(s32[128]{0:T(128)} %docs.1) | copy-start | bytes 1540
  4.8 13.5 %copy-start.8 = (s32[1,7]{1,0:T(1,128)S(1)}, s32[1,7]{1,0:T(1,128)}, u32[]{:S(2)}) copy-start(s32[1,7]{1,0:T(1,128)} %pairs.3) | copy-start | bytes 88
  5.5 1.0 %copy-start.1 = (f32[256,1024]{1,0:T(8,128)}, f32[256,1024]{1,0:T(8,128)S(1)}, u32[]{:S(2)}) copy-start(f32[256,1024]{1,0:T(8,128)S(1)} %get-tuple-element.26.first_gprobs) | copy-start | bytes 3145732
  6.4 25.5 %collective-permute-start.1 = (bf16[2064,128]{1,0:T(8,128)(2,1)S(1)}, bf16[2064,128]{1,0:T(8,128)(2,1)S(1)}, u32[]{:S(2)}, u32[]{:S(2)}) collective-permute-start(bf16[2064,128]{1,0:T(8,128)(2,1)S(1)} %get-tuple-element.21.stack), channel_id=1, source_target_pairs={{0,4},{4,0},{8,12},{12,8},{16,20},{20,16},{24,28},{28,24},{32,36},... | collective-permute-start | bytes 1585160 | tf_op jit(solution)/shard_map/ppermute | solution.py:284
  18.2 18.2 %copy-start.2 = (f32[256,1024]{1,0:T(8,128)S(1)}, f32[256,1024]{1,0:T(8,128)}, u32[]{:S(2)}) copy-start(f32[256,1024]{1,0:T(8,128)} %copy-done.1) | copy-start | bytes 3145732
  33.3 3.1 %collective-permute-start.2 = (f32[2,8,1024]{2,1,0:T(8,128)S(1)}, f32[2,8,1024]{2,1,0:T(8,128)S(1)}, u32[]{:S(2)}, u32[]{:S(2)}) collective-permute-start(f32[2,8,1024]{2,1,0:T(8,128)S(1)} %get-tuple-element.31.mine), channel_id=1, source_target_pairs={{0,4},{4,0},{8,12},{12,8},{16,20},{20,16},{24,28},{28,24},{32,36},... | collective-permute-start | bytes 196616 | tf_op jit(solution)/shard_map/ppermute | solution.py:300
  37.8 33.0 %copy-start = (f32[2,128,1024]{2,1,0:T(8,128)}, f32[2,128,1024]{2,1,0:T(8,128)S(1)}, u32[]{:S(2)}) copy-start(f32[2,128,1024]{2,1,0:T(8,128)S(1)} %get-tuple-element.32.mine) | copy-start | bytes 3145732
  50.3 10.5 %collective-permute-start.4 = (bf16[256,256]{1,0:T(8,128)(2,1)S(1)}, bf16[256,256]{1,0:T(8,128)(2,1)S(1)}, u32[]{:S(2)}, u32[]{:S(2)}) collective-permute-start(bf16[256,256]{1,0:T(8,128)(2,1)S(1)} %reduce_sum.12), channel_id=1, source_target_pairs={{9,1},{15,7},{17,9},{18,2},{22,6},{23,15},{25,17},{26,10},{27,3},{... | collective-permute-start | bytes 393224 | tf_op jit(solution)/shard_map/ppermute | solution.py:321
  51.1 19.7 %collective-permute-start.3 = (f32[128,1024]{1,0:T(8,128)S(1)}, f32[128,1024]{1,0:T(8,128)S(1)}, u32[]{:S(2)}, u32[]{:S(2)}) collective-permute-start(f32[128,1024]{1,0:T(8,128)S(1)} %slice_bitcast_fusion), channel_id=1, source_target_pairs={{0,4},{4,0},{8,12},{12,8},{16,20},{20,16},{24,28},{28,24},{32,36},... | collective-permute-start | bytes 1572872 | tf_op jit(solution)/shard_map/ppermute | solution.py:322
  61.7 17.2 %all-to-all-start.2 = ((bf16[4,256,256]{2,1,0:T(8,128)(2,1)}), bf16[4,256,256]{2,1,0:T(8,128)(2,1)S(1)}, u32[]{:S(2)}, u32[]{:S(2)}) async-start(bf16[4,256,256]{2,1,0:T(8,128)(2,1)} %broadcast_in_dim.7), calls=%async_computation.2 | async-start | bytes 1048576 | tf_op jit(solution)/shard_map/all_to_all | solution.py:330
  70.8 0.8 %copy-start.9 = (f32[128,1024]{1,0:T(8,128)}, f32[128,1024]{1,0:T(8,128)S(1)}, u32[]{:S(2)}) copy-start(f32[128,1024]{1,0:T(8,128)S(1)} %collective-permute-done.3.theirs) | copy-start | bytes 1572868

commit v5 on v4

--- a/solution.py
+++ b/solution.py
@@ -13,13 +13,14 @@
 GRANT = 12
 
 
-KEEP, OTHER = 8, 24
+KEEP, OTHER, SIDE = 8, 24, 30
 
 
 def list_kernel(info, docs, pairs, knock, early):
     heads, slots = knock.shape[0], (pairs.shape[1] + 1) // 2
     here, side = info[0], info[1]
     early[0] = 0
+    early[SIDE] = side
     for d in range(slots + 1):
         block = jnp.maximum(here - 2 * d, 0)
         kept = functools.reduce(jnp.logical_or, [knock[h, block] == 1 for h in range(heads)])
@@ -44,17 +45,24 @@
                 early[0] = entry + 1
 
 
-def first_kernel(q_ref, g_ref, own, pairs, exps, gprobs, key_t, stack, stats):
+def first_kernel(q_ref, g_ref, own, pairs, both, key_t, stack, stats, arrivals):
     rows, width = own.shape[0], own.shape[1] // 2
     heads = q_ref.shape[1] // width
     span = heads * rows
     scale = width ** (-0.5)
     f32 = jnp.float32
 
-    for h in range(heads):
-        part, cols = slice(h * rows, (h + 1) * rows), slice(h * width, (h + 1) * width)
-        stack[h * rows : (h + 1) * rows] = q_ref[:, cols]
-        stack[span + h * rows : span + (h + 1) * rows] = g_ref[:, cols]
+    copies = []
+    for n, source in enumerate((q_ref, g_ref)):
+        for h in range(heads):
+            place = n * span + h * rows
+            copy = pltpu.make_async_copy(
+                source.at[:, pl.ds(h * width, width)],
+                stack.at[pl.ds(place, rows)],
+                arrivals.at[n * heads + h],
+            )
+            copy.start()
+            copies.append(copy)
     stack[2 * span :] = jnp.zeros((16, width), stack.dtype)
     listed = jnp.broadcast_to(pairs[...].astype(f32), (16, pairs.shape[1]))
     stack[2 * span :, : pairs.shape[1]] = listed.astype(stack.dtype)
@@ -63,33 +71,30 @@
     below = lax.broadcasted_iota(jnp.int32, (rows, rows), 0) <= lax.broadcasted_iota(
         jnp.int32, (rows, rows), 1
     )
+    for copy in copies:
+        copy.wait()
     for h in range(heads):
-        part, cols = slice(h * rows, (h + 1) * rows), slice(h * width, (h + 1) * width)
-        s = lax.dot_general(own[:, :width], q_ref[:, cols], NT, preferred_element_type=f32) * scale
-        g = lax.dot_general(own[:, width:], g_ref[:, cols], NT, preferred_element_type=f32)
+        part = slice(h * rows, (h + 1) * rows)
+        late_part = slice(span + h * rows, span + (h + 1) * rows)
+        s = lax.dot_general(own[:, :width], stack[part], NT, preferred_element_type=f32) * scale
+        g = lax.dot_general(own[:, width:], stack[late_part], NT, preferred_element_type=f32)
         s = jnp.where(below, s, NEG)
         top = jnp.max(s, axis=0, keepdims=True)
         e = jnp.exp(s - top)
-        exps[:, part] = e
-        gprobs[:, part] = g
+        both[0, :, part] = e
+        both[1, :, part] = g
         stats[0:1, part] = top
         stats[1:2, part] = jnp.sum(e, axis=0, keepdims=True)
         stats[2:3, part] = jnp.sum(e * g, axis=0, keepdims=True)
 
 
-def scores_kernel(info, early, stack, stack2, first_stats, same, exps, gprobs, key_t, stats, late):
-    slots, rows, width = same.shape[0], same.shape[1], same.shape[2] // 2
-    span = (stack.shape[0] - 16) // 2
-    heads = span // rows
-    scale = width ** (-0.5)
-    side = info[1]
-    f32 = jnp.float32
-
-    table = stack2[2 * span :].astype(f32)[0:1]
+def list_other(early, stack2, late, slots, heads):
+    side = early[SIDE]
+    table = stack2[stack2.shape[0] - 16 :].astype(jnp.float32)[0:1]
     bits = jnp.zeros_like(table)
     for d in range(slots + 1):
         back = 2 * d + 1 - 2 * side
-        match = (table == back.astype(f32)) & (back > 0)
+        match = (table == back.astype(jnp.float32)) & (back > 0)
         bits = bits + jnp.where(match, float(1 << d), 0.0)
     bits = jnp.sum(bits).astype(jnp.int32)
     late[0] = 0
@@ -102,6 +107,15 @@
                 late[KEEP + heads * entry + h] = early[32 + heads * d + h]
             late[0] = entry + 1
 
+
+def scores_kernel(early, stack, stack2, first_stats, same, exps, gprobs, key_t, stats, late):
+    slots, rows, width = same.shape[0], same.shape[1], same.shape[2] // 2
+    span = (stack.shape[0] - 16) // 2
+    heads = span // rows
+    scale = width ** (-0.5)
+    f32 = jnp.float32
+
+    list_other(early, stack2, late, slots, heads)
     stats[...] = jnp.zeros_like(stats)
     for which in range(2):
         stats[which, 0:1] = jnp.full((1, span), NEG, f32)
@@ -144,15 +158,16 @@
 
 
 def terms_kernel(
-    info, early, late, first_exps, first_gprobs, first_key_t, exps, gprobs, key_t, stack, stack2, mine, theirs,
-    plane_ref, near_ref, dq_ref, factors, acc, probs, grads,
+    early, first, first_key_t, exps, gprobs, key_t, stack, stack2, mine, theirs,
+    plane_ref, near_ref, dq_ref, factors, acc, probs, grads, late,
 ):
     rows, width = exps.shape[1], stack.shape[1]
     span = exps.shape[2]
     slots = plane_ref.shape[0]
     scale = width ** (-0.5)
-    side = info[1]
+    side = early[SIDE]
     stacks = (stack, stack2)
+    list_other(early, stack2, late, slots, span // rows)
     f32, bf16 = jnp.float32, jnp.bfloat16
 
     def three(ref, which, row):
@@ -184,7 +199,7 @@
 
     acc[...] = jnp.zeros_like(acc)
     key_term, value_term, dq_ref[0] = gradients(
-        lambda part: first_exps[:, part], lambda part: first_gprobs[:, part], first_key_t[...], 0, 2
+        lambda part: first[0, :, part], lambda part: first[1, :, part], first_key_t[...], 0, 2
     )
     dq_ref[1] = jnp.zeros(dq_ref.shape[1:], f32)
     near_ref[:, :width] = key_term
@@ -267,36 +282,37 @@
         compiler_params=grant(GRANT),
         cost_estimate=work,
     )(info, doc_of_block, pair_list, knock)
-    exps0, gprobs0, key0_t, stack, stats0 = pl.pallas_call(
+    far = pl.BlockSpec(memory_space=pltpu.HBM)
+    both0, key0_t, stack, stats0 = pl.pallas_call(
         first_kernel,
         out_shape=(
-            pltpu.VMEM((rows, span), f32),
-            pltpu.VMEM((rows, span), f32),
+            pltpu.VMEM((2, rows, span), f32),
             pltpu.VMEM((width, rows), bf16),
             jax.ShapeDtypeStruct((2 * span + 16, width), bf16),
             jax.ShapeDtypeStruct((8, span), f32),
         ),
-        in_specs=[vmem] * 4,
-        out_specs=(vmem,) * 5,
+        in_specs=[far, far, vmem, vmem],
+        out_specs=(vmem,) * 4,
+        scratch_shapes=[pltpu.SemaphoreType.DMA((2 * heads,))],
         compiler_params=grant(GRANT),
         cost_estimate=work,
-    )(queries, grad_out, own, pair_list)
+    )(*(pltpu.with_memory_space_constraint(x, pltpu.HBM) for x in (queries, grad_out)), own, pair_list)
     stack2 = lax.ppermute(stack, "ctx", swap)
     fetched, stats0, early = lax.optimization_barrier((fetched, stats0, early))
     same = lax.all_to_all(jnp.broadcast_to(fetched, (planes, rows, 2 * width)), "head", 0, 0)
-    exps, gprobs, key_t, mine, late = pl.pallas_call(
+    exps, gprobs, key_t, mine = pl.pallas_call(
         scores_kernel,
         out_shape=(
             pltpu.VMEM((reach - 1, rows, span), f32),
             pltpu.VMEM((reach - 1, rows, span), f32),
             pltpu.VMEM((planes, width, rows), bf16),
             jax.ShapeDtypeStruct((2, 8, span), f32),
-            lists,
         ),
-        in_specs=[smem] * 2 + [vmem] * 4,
-        out_specs=(vmem,) * 4 + (smem,),
+        in_specs=[smem] + [vmem] * 4,
+        out_specs=(vmem,) * 4,
+        scratch_shapes=[pltpu.SMEM((32,), jnp.int32)],
         compiler_params=grant(GRANT),
-    )(info, early, stack, stack2, stats0, same)
+    )(early, stack, stack2, stats0, same)
     theirs = lax.ppermute(mine, "ctx", swap)
     plane, near, dq = pl.pallas_call(
         terms_kernel,
@@ -305,16 +321,17 @@
             jax.ShapeDtypeStruct((rows, 2 * width), f32),
             jax.ShapeDtypeStruct((2, width, span), f32),
         ),
-        in_specs=[smem] * 3 + [vmem] * 10,
+        in_specs=[smem] + [vmem] * 9,
         out_specs=(vmem,) * 3,
         scratch_shapes=[
             pltpu.VMEM((2, 8, span), f32),
             pltpu.VMEM((planes, rows, 2 * width), f32),
             pltpu.VMEM((rows, span), bf16),
             pltpu.VMEM((rows, span), bf16),
+            pltpu.SMEM((32,), jnp.int32),
         ],
         compiler_params=grant(GRANT),
-    )(info, early, late, exps0, gprobs0, key0_t, exps, gprobs, key_t, stack, stack2, mine, theirs)
+    )(early, both0, key0_t, exps, gprobs, key_t, stack, stack2, mine, theirs)
 
     parts = lax.all_to_all(plane, "head", 0, 0)
     sent = jnp.sum(parts.astype(f32), axis=0).astype(bf16)

time: 80.1 us -> 78.5 us (0.980)
  the two profiles are of different devices: /device:TPU:24 before, /device:TPU:72 now
where the time goes in v5:
time: 78.5 us; the launch traced here: 78 us
  starting transfers between devices  27 us (34%)
  blocking collectives  26 us (33%)
  Pallas kernels  11.1 us (14%)
  waiting for transfers between devices  7.52 us (10%)
  local copies, waits for them, and re-layouts  3.74 us (5%)
  other arithmetic  1.8 us (2%)
  between operations  0.82 us (1%)
    all_to_all x1, blocking collectives, local(): lax.all_to_all(jnp.broadcast_to(fetched, (planes, rows, 2 * width)), 'hea...  13.5 us
    all_to_all x1, blocking collectives, local(): parts = lax.all_to_all(plane, 'head', 0, 0)  12.5 us
    ppermute x1, starting transfers between devices, local(): stack2 = lax.ppermute(stack, 'ctx', swap)  10.8 us
    all_to_all x1, starting transfers between devices, local(): lax.all_to_all(jnp.broadcast_to(mine, (planes, rows, 2 * width)), 'head',...  8.64 us
    all_to_all x1, waiting for transfers between devices, local(): lax.all_to_all(jnp.broadcast_to(mine, (planes, rows, 2 * width)), 'head',...  6.29 us
    ppermute x1, starting transfers between devices, local(): dq2 = lax.ppermute(dq[1], 'ctx', swap)  4.34 us
    pallas_call x1, Pallas kernels, local(): pl.pallas_call(terms_kernel, out_shape=(jax.ShapeDtypeStruct((planes, row...  3.12 us
    unnamed x16, local copies, waits for them, and re-layouts  2.81 us
  transfers between devices with their start and end apart: 6, of which 2 were waited for; matrix products, arithmetic and copies ran while one was open for 1% of the time, Pallas kernels for 7%

profile of v5, /device:TPU:72, one launch (start us, length us, event | category | flops | bytes accessed | tf_op | source)
XLA Modules:
  0.0 78.0 jit_solution(15000669767324428809)
XLA Ops:
  0.6 0.9 %pad_add_fusion.own = bf16[256,256]{1,0:T(8,128)(2,1)S(1)} fusion(bf16[256,128]{1,0:T(8,128)(2,1)} %param.9, bf16[256,128]{1,0:T(8,128)(2,1)} %param.8), kind=kLoop, calls=%fused_computation.4 | loop fusion | flops 262144 | bytes 262144 | tf_op jit(solution)/shard_map/add | solution.py:267
  1.5 0.0 copy-start.3
  1.5 0.0 copy-start.4
  1.5 0.7 collective-permute-start
  2.2 0.0 copy-start.5
  2.2 0.6 copy-done.5
  2.9 0.0 copy-start.6
  2.9 1.8 %shard_map.94 = (f32[2,256,1024]{2,1,0:T(8,128)S(1)}, bf16[128,256]{1,0:T(8,128)(2,1)S(1)}, bf16[2064,128]{1,0:T(8,128)(2,1)S(1)}, f32[8,1024]{1,0:T(8,128)S(1)}) custom-call(bf16[256,512]{1,0:T(8,128)(2,1)} %q_ref.1, bf16[256,512]{1,0:T(8,128)(2,1)} %g_ref.1, bf16[256,256]{1,0:T(8,128)(2,1)S(1)} %pad_add_fusion.own, s32[1,7]{1,0:T(1,128)S(1)} %copy-done.5), custom_call_target="tpu_custom_call" | custom-call | flops 10000000000 | bytes 4194304 | tf_op jit(solution)/shard_map/pallas_call | solution.py:286
  4.7 0.0 copy-start.1
  4.7 1.3 %copy-done.1 = f32[2,256,1024]{2,1,0:T(8,128)} copy-done((f32[2,256,1024]{2,1,0:T(8,128)}, f32[2,256,1024]{2,1,0:T(8,128)S(1)}, u32[]{:S(2)}) %copy-start.1) | copy-done | bytes 2097176
  6.0 10.8 %collective-permute-start.1 = (bf16[2064,128]{1,0:T(8,128)(2,1)S(1)}, bf16[2064,128]{1,0:T(8,128)(2,1)S(1)}, u32[]{:S(2)}, u32[]{:S(2)}) collective-permute-start(bf16[2064,128]{1,0:T(8,128)(2,1)S(1)} %get-tuple-element.21.stack), channel_id=1, source_target_pairs={{0,4},{4,0},{8,12},{12,8},{16,20},{20,16},{24,28},{28,24},{32,36},... | collective-permute-start | bytes 1585160 | tf_op jit(solution)/shard_map/ppermute | solution.py:300
  16.8 0.1 pad_add_fusion.1.info
  16.9 0.0 copy-done.3
  16.9 0.0 copy-done.4
  16.9 0.0 copy-done.6
  16.9 0.0 copy-start.2
  16.9 1.3 %shard_map.95.early = s32[52]{0:T(128)S(1)} custom-call(s32[2]{0:T(128)S(1)} %pad_add_fusion.1.info, s32[128]{0:T(128)S(1)} %copy-done.4, s32[1,7]{1,0:T(1,128)S(1)} %copy-done.6, s32[4,128]{1,0:T(4,128)S(1)} %copy-done.3), custom_call_target="tpu_custom_call" | custom-call | flops 10000000000 | bytes 4194304 | tf_op jit(solution)/shard_map/pallas_call | solution.py:277
  18.2 0.0 collective-permute-done
  18.3 13.5 %all_to_all.15.same = bf16[4,256,256]{2,1,0:T(8,128)(2,1)S(1)} all-to-all(bf16[4,256,256]{2,1,0:T(8,128)(2,1)S(1)} %broadcast_in_dim.6), channel_id=1, replica_groups=mesh['ctx'=128,'head'=4] {'head'}, dimensions={0} | all-to-all | bytes 1048576 | tf_op jit(solution)/shard_map/all_to_all | solution.py:302
  31.8 0.0 collective-permute-done.1.stack2
  31.8 2.7 %shard_map.96 = (f32[7,256,1024]{2,1,0:T(8,128)S(1)}, f32[7,256,1024]{2,1,0:T(8,128)S(1)}, bf16[4,128,256]{2,1,0:T(8,128)(2,1)S(1)}, f32[2,8,1024]{2,1,0:T(8,128)S(1)}) custom-call(s32[52]{0:T(128)S(1)} %shard_map.95.early, bf16[2064,128]{1,0:T(8,128)(2,1)S(1)} %get-tuple-element.21.stack, bf16[2064,128]{1,0:T(8,128)(2,1)S(1)} %collective-permute-done.1.stack2, ...), custom_call_target="tpu_custom_call" | custom-call | tf_op jit(solution)/shard_map/pallas_call | solution.py:303
  34.5 1.9 %collective-permute-start.2 = (f32[2,8,1024]{2,1,0:T(8,128)S(1)}, f32[2,8,1024]{2,1,0:T(8,128)S(1)}, u32[]{:S(2)}, u32[]{:S(2)}) collective-permute-start(f32[2,8,1024]{2,1,0:T(8,128)S(1)} %get-tuple-element.27.mine), channel_id=1, source_target_pairs={{0,4},{4,0},{8,12},{12,8},{16,20},{20,16},{24,28},{28,24},{32,36},... | collective-permute-start | bytes 196616 | tf_op jit(solution)/shard_map/ppermute | solution.py:316
  36.4 1.2 %collective-permute-done.2.theirs = f32[2,8,1024]{2,1,0:T(8,128)S(1)} collective-permute-done((f32[2,8,1024]{2,1,0:T(8,128)S(1)}, f32[2,8,1024]{2,1,0:T(8,128)S(1)}, u32[]{:S(2)}, u32[]{:S(2)}) %collective-permute-start.2) | collective-permute-done | bytes 65568 | tf_op jit(solution)/shard_map/ppermute | solution.py:316
  37.6 0.0 copy-done.2
  37.6 3.1 %shard_map.97 = (bf16[4,256,256]{2,1,0:T(8,128)(2,1)S(1)}, f32[256,256]{1,0:T(8,128)S(1)}, f32[2,128,1024]{2,1,0:T(8,128)S(1)}) custom-call(s32[52]{0:T(128)S(1)} %shard_map.95.early, f32[2,256,1024]{2,1,0:T(8,128)S(1)} %copy-done.2, bf16[128,256]{1,0:T(8,128)(2,1)S(1)} %get-tuple-element.20.first_key_t, f32[7,256,1024]{2,1,0:T(8,128)S(1)} %get-tuple-element.24.exps, ...), custom_call_target="tpu_custom_call" | custom-call | tf_op jit(solution)/shard_map/pallas_call | solution.py:317
  40.8 0.0 copy-start
  40.8 12.5 %all_to_all.16 = bf16[4,256,256]{2,1,0:T(8,128)(2,1)S(1)} all-to-all(bf16[4,256,256]{2,1,0:T(8,128)(2,1)S(1)} %get-tuple-element.29), channel_id=1, replica_groups=mesh['ctx'=128,'head'=4] {'head'}, dimensions={0} | all-to-all | bytes 1048576 | tf_op jit(solution)/shard_map/all_to_all | solution.py:336
  53.3 0.1 reduce_sum.12
  53.3 0.7 collective-permute-start.4
  54.1 4.3 %collective-permute-start.3 = (f32[128,1024]{1,0:T(8,128)S(1)}, f32[128,1024]{1,0:T(8,128)S(1)}, u32[]{:S(2)}, u32[]{:S(2)}) collective-permute-start(f32[128,1024]{1,0:T(8,128)S(1)} %slice_bitcast_fusion), channel_id=1, source_target_pairs={{0,4},{4,0},{8,12},{12,8},{16,20},{20,16},{24,28},{28,24},{32,36},... | collective-permute-start | bytes 1572872 | tf_op jit(solution)/shard_map/ppermute | solution.py:339
  58.4 0.0 collective-permute-done.4
  58.5 0.9 %broadcast_in_dim.7 = bf16[4,256,256]{2,1,0:T(8,128)(2,1)} broadcast(bf16[256,256]{1,0:T(8,128)(2,1)S(1)} %add_convert_fusion), dimensions={1,2} | broadcast | bytes 655360 | tf_op jit(solution)/shard_map/broadcast_in_dim | solution.py:347
  59.3 8.6 %all-to-all-start.2 = ((bf16[4,256,256]{2,1,0:T(8,128)(2,1)}), bf16[4,256,256]{2,1,0:T(8,128)(2,1)S(1)}, u32[]{:S(2)}, u32[]{:S(2)}) async-start(bf16[4,256,256]{2,1,0:T(8,128)(2,1)} %broadcast_in_dim.7), calls=%async_computation.2 | async-start | bytes 1048576 | tf_op jit(solution)/shard_map/all_to_all | solution.py:347
  67.9 0.0 collective-permute-done.3.theirs
  68.0 0.0 copy-done
  68.0 0.0 copy-start.7
  68.0 0.8 %copy-done.7 = f32[128,1024]{1,0:T(8,128)} copy-done((f32[128,1024]{1,0:T(8,128)}, f32[128,1024]{1,0:T(8,128)S(1)}, u32[]{:S(2)}) %copy-start.7) | copy-done | bytes 524312
  68.8 2.2 %shard_map.98 = bf16[256,512]{1,0:T(8,128)(2,1)} custom-call(f32[2,128,1024]{2,1,0:T(8,128)} %copy-done, f32[128,1024]{1,0:T(8,128)} %copy-done.7), custom_call_target="tpu_custom_call" | custom-call | tf_op jit(solution)/shard_map/pallas_call | solution.py:340
  71.0 6.3 %all-to-all-done.2 = bf16[4,256,256]{2,1,0:T(8,128)(2,1)S(1)} async-done(((bf16[4,256,256]{2,1,0:T(8,128)(2,1)}), bf16[4,256,256]{2,1,0:T(8,128)(2,1)S(1)}, u32[]{:S(2)}, u32[]{:S(2)}) %all-to-all-start.2) | async-done | bytes 524320 | tf_op jit(solution)/shard_map/all_to_all | solution.py:347
  77.3 0.7 fusion.1
  (3 shorter events, 0.1 us)
Async XLA Ops:
  1.5 15.4 %copy-start.3 = (s32[4,128]{1,0:T(4,128)S(1)}, s32[4,128]{1,0:T(4,128)}, u32[]{:S(2)}) copy-start(s32[4,128]{1,0:T(4,128)} %knock.1) | copy-start | bytes 6148
  1.5 15.4 %copy-start.4 = (s32[128]{0:T(128)S(1)}, s32[128]{0:T(128)}, u32[]{:S(2)}) copy-start(s32[128]{0:T(128)} %docs.1) | copy-start | bytes 1540
  1.5 16.7 %collective-permute-start = (bf16[256,256]{1,0:T(8,128)(2,1)S(1)}, bf16[256,256]{1,0:T(8,128)(2,1)S(1)}, u32[]{:S(2)}, u32[]{:S(2)}) collective-permute-start(bf16[256,256]{1,0:T(8,128)(2,1)S(1)} %pad_add_fusion.own), channel_id=1, source_target_pairs={{0,0},{8,8},{1,9},{7,15},{16,16},{9,17},{2,18},{6,22},{15,23},{24,... | collective-permute-start | bytes 393224 | tf_op jit(solution)/shard_map/ppermute | solution.py:268
  2.2 0.7 copy-start.5
  2.9 14.0 %copy-start.6 = (s32[1,7]{1,0:T(1,128)S(1)}, s32[1,7]{1,0:T(1,128)}, u32[]{:S(2)}) copy-start(s32[1,7]{1,0:T(1,128)} %pairs.3) | copy-start | bytes 88
  4.7 1.3 %copy-start.1 = (f32[2,256,1024]{2,1,0:T(8,128)}, f32[2,256,1024]{2,1,0:T(8,128)S(1)}, u32[]{:S(2)}) copy-start(f32[2,256,1024]{2,1,0:T(8,128)S(1)} %get-tuple-element.19.first) | copy-start | bytes 6291460
  6.0 25.8 %collective-permute-start.1 = (bf16[2064,128]{1,0:T(8,128)(2,1)S(1)}, bf16[2064,128]{1,0:T(8,128)(2,1)S(1)}, u32[]{:S(2)}, u32[]{:S(2)}) collective-permute-start(bf16[2064,128]{1,0:T(8,128)(2,1)S(1)} %get-tuple-element.21.stack), channel_id=1, source_target_pairs={{0,4},{4,0},{8,12},{12,8},{16,20},{20,16},{24,28},{28,24},{32,36},... | collective-permute-start | bytes 1585160 | tf_op jit(solution)/shard_map/ppermute | solution.py:300
  16.9 20.7 %copy-start.2 = (f32[2,256,1024]{2,1,0:T(8,128)S(1)}, f32[2,256,1024]{2,1,0:T(8,128)}, u32[]{:S(2)}) copy-start(f32[2,256,1024]{2,1,0:T(8,128)} %copy-done.1) | copy-start | bytes 6291460
  34.5 3.1 %collective-permute-start.2 = (f32[2,8,1024]{2,1,0:T(8,128)S(1)}, f32[2,8,1024]{2,1,0:T(8,128)S(1)}, u32[]{:S(2)}, u32[]{:S(2)}) collective-permute-start(f32[2,8,1024]{2,1,0:T(8,128)S(1)} %get-tuple-element.27.mine), channel_id=1, source_target_pairs={{0,4},{4,0},{8,12},{12,8},{16,20},{20,16},{24,28},{28,24},{32,36},... | collective-permute-start | bytes 196616 | tf_op jit(solution)/shard_map/ppermute | solution.py:316
  40.8 27.2 %copy-start = (f32[2,128,1024]{2,1,0:T(8,128)}, f32[2,128,1024]{2,1,0:T(8,128)S(1)}, u32[]{:S(2)}) copy-start(f32[2,128,1024]{2,1,0:T(8,128)S(1)} %get-tuple-element.28.mine) | copy-start | bytes 3145732
  53.3 5.1 %collective-permute-start.4 = (bf16[256,256]{1,0:T(8,128)(2,1)S(1)}, bf16[256,256]{1,0:T(8,128)(2,1)S(1)}, u32[]{:S(2)}, u32[]{:S(2)}) collective-permute-start(bf16[256,256]{1,0:T(8,128)(2,1)S(1)} %reduce_sum.12), channel_id=1, source_target_pairs={{9,1},{15,7},{17,9},{18,2},{22,6},{23,15},{25,17},{26,10},{27,3},{... | collective-permute-start | bytes 393224 | tf_op jit(solution)/shard_map/ppermute | solution.py:338
  54.1 13.9 %collective-permute-start.3 = (f32[128,1024]{1,0:T(8,128)S(1)}, f32[128,1024]{1,0:T(8,128)S(1)}, u32[]{:S(2)}, u32[]{:S(2)}) collective-permute-start(f32[128,1024]{1,0:T(8,128)S(1)} %slice_bitcast_fusion), channel_id=1, source_target_pairs={{0,4},{4,0},{8,12},{12,8},{16,20},{20,16},{24,28},{28,24},{32,36},... | collective-permute-start | bytes 1572872 | tf_op jit(solution)/shard_map/ppermute | solution.py:339
  59.3 18.0 %all-to-all-start.2 = ((bf16[4,256,256]{2,1,0:T(8,128)(2,1)}), bf16[4,256,256]{2,1,0:T(8,128)(2,1)S(1)}, u32[]{:S(2)}, u32[]{:S(2)}) async-start(bf16[4,256,256]{2,1,0:T(8,128)(2,1)} %broadcast_in_dim.7), calls=%async_computation.2 | async-start | bytes 1048576 | tf_op jit(solution)/shard_map/all_to_all | solution.py:347
  68.0 0.8 %copy-start.7 = (f32[128,1024]{1,0:T(8,128)}, f32[128,1024]{1,0:T(8,128)S(1)}, u32[]{:S(2)}) copy-start(f32[128,1024]{1,0:T(8,128)S(1)} %collective-permute-done.3.theirs) | copy-start | bytes 1572868

commit v6 on v5

--- a/solution.py
+++ b/solution.py
@@ -108,7 +108,7 @@
             late[0] = entry + 1
 
 
-def scores_kernel(early, stack, stack2, first_stats, same, exps, gprobs, key_t, stats, late):
+def scores_kernel(early, stack, stack2, first_stats, same, exps, gprobs, key_t, tops, stats, late):
     slots, rows, width = same.shape[0], same.shape[1], same.shape[2] // 2
     span = (stack.shape[0] - 16) // 2
     heads = span // rows
@@ -124,7 +124,7 @@
     for which, both, meta in ((0, stack, early), (1, stack2, late)):
         base = (slots - 1) * which
 
-        def first(k, carry, which=which, both=both, base=base, meta=meta):
+        def tile(k, carry, which=which, both=both, base=base, meta=meta):
             i, slot = base + k, meta[1 + k]
             key_t[slot] = same[slot, :, :width].T
             for h in range(heads):
@@ -132,33 +132,33 @@
                 s = lax.dot_general(
                     same[slot, :, :width], both[part], NT, preferred_element_type=f32
                 )
+                g = lax.dot_general(
+                    same[slot, :, width:],
+                    both[span + h * rows : span + (h + 1) * rows],
+                    NT,
+                    preferred_element_type=f32,
+                )
                 s = s * scale + jnp.where(meta[KEEP + heads * k + h] == 1, 0.0, NEG).astype(f32)
-                exps[i, :, part] = s
-                stats[which, 0:1, part] = jnp.maximum(
-                    stats[which, 0:1, part], jnp.max(s, axis=0, keepdims=True)
-                )
+                top = jnp.max(s, axis=0, keepdims=True)
+                e = jnp.exp(s - top)
+                exps[i, :, part] = e
+                gprobs[i, :, part] = g
+                tops[i, 0:1, part] = top
+                before = stats[which, 0:1, part]
+                high = jnp.maximum(before, top)
+                old, new = jnp.exp(before - high), jnp.exp(top - high)
+                total = jnp.sum(e, axis=0, keepdims=True)
+                weighted = jnp.sum(e * g, axis=0, keepdims=True)
+                stats[which, 0:1, part] = high
+                stats[which, 1:2, part] = stats[which, 1:2, part] * old + total * new
+                stats[which, 2:3, part] = stats[which, 2:3, part] * old + weighted * new
             return carry
 
-        def second(k, carry, which=which, both=both, base=base, meta=meta):
-            i, slot = base + k, meta[1 + k]
-            for h in range(heads):
-                part = slice(h * rows, (h + 1) * rows)
-                g = lax.dot_general(
-                    same[slot, :, width:], both[span + h * rows : span + (h + 1) * rows], NT, preferred_element_type=f32
-                )
-                e = jnp.exp(exps[i, :, part] - stats[which, 0:1, part])
-                gprobs[i, :, part] = g
-                exps[i, :, part] = e
-                stats[which, 1:2, part] += jnp.sum(e, axis=0, keepdims=True)
-                stats[which, 2:3, part] += jnp.sum(e * g, axis=0, keepdims=True)
-            return carry
-
-        lax.fori_loop(0, meta[0], first, 0)
-        lax.fori_loop(0, meta[0], second, 0)
+        lax.fori_loop(0, meta[0], tile, 0)
 
 
 def terms_kernel(
-    early, first, first_key_t, exps, gprobs, key_t, stack, stack2, mine, theirs,
+    early, first, first_key_t, exps, gprobs, key_t, tops, stack, stack2, mine, theirs,
     plane_ref, near_ref, dq_ref, factors, acc, probs, grads, late,
 ):
     rows, width = exps.shape[1], stack.shape[1]
@@ -183,14 +183,15 @@
         total = sum(share * part for share, (_, part, _) in zip(shares, group))
         weighted = sum(share * part for share, (_, _, part) in zip(shares, group))
         inverse = 1.0 / total
-        factors[which, 0:1] = shares[0] * inverse
+        factors[which, 0:1] = high
         factors[which, 1:2] = weighted * inverse
         factors[which, 2:3] = shares[1] * inverse
-
-    def gradients(load_e, load_g, keys, which, row):
+        factors[which, 3:4] = inverse
+
+    def gradients(load_e, load_g, keys, which, factor):
         for h in range(span // rows):
             part = slice(h * rows, (h + 1) * rows)
-            p = load_e(part) * factors[which, row : row + 1, part]
+            p = load_e(part) * factor(part)
             probs[:, part] = p.astype(bf16)
             grads[:, part] = (p * (load_g(part) - factors[which, 1:2, part])).astype(bf16)
         key_term = jnp.dot(grads[...], stacks[which][:span], preferred_element_type=f32) * scale
@@ -199,7 +200,8 @@
 
     acc[...] = jnp.zeros_like(acc)
     key_term, value_term, dq_ref[0] = gradients(
-        lambda part: first[0, :, part], lambda part: first[1, :, part], first_key_t[...], 0, 2
+        lambda part: first[0, :, part], lambda part: first[1, :, part], first_key_t[...], 0,
+        lambda part: factors[0, 2:3, part],
     )
     dq_ref[1] = jnp.zeros(dq_ref.shape[1:], f32)
     near_ref[:, :width] = key_term
@@ -209,7 +211,9 @@
         def step(k, carry, which=which, meta=meta):
             i, slot = (slots - 1) * which + k, meta[1 + k]
             key_term, value_term, query_term = gradients(
-                lambda part: exps[i, :, part], lambda part: gprobs[i, :, part], key_t[slot], which, 0
+                lambda part: exps[i, :, part], lambda part: gprobs[i, :, part], key_t[slot], which,
+                lambda part: jnp.exp(tops[i, 0:1, part] - factors[which, 0:1, part])
+                * factors[which, 3:4, part],
             )
             dq_ref[which] += query_term
             acc[slot, :, :width] += key_term
@@ -300,16 +304,17 @@
     stack2 = lax.ppermute(stack, "ctx", swap)
     fetched, stats0, early = lax.optimization_barrier((fetched, stats0, early))
     same = lax.all_to_all(jnp.broadcast_to(fetched, (planes, rows, 2 * width)), "head", 0, 0)
-    exps, gprobs, key_t, mine = pl.pallas_call(
+    exps, gprobs, key_t, tops, mine = pl.pallas_call(
         scores_kernel,
         out_shape=(
             pltpu.VMEM((reach - 1, rows, span), f32),
             pltpu.VMEM((reach - 1, rows, span), f32),
             pltpu.VMEM((planes, width, rows), bf16),
+            pltpu.VMEM((reach - 1, 8, span), f32),
             jax.ShapeDtypeStruct((2, 8, span), f32),
         ),
         in_specs=[smem] + [vmem] * 4,
-        out_specs=(vmem,) * 4,
+        out_specs=(vmem,) * 5,
         scratch_shapes=[pltpu.SMEM((32,), jnp.int32)],
         compiler_params=grant(GRANT),
     )(early, stack, stack2, stats0, same)
@@ -321,7 +326,7 @@
             jax.ShapeDtypeStruct((rows, 2 * width), f32),
             jax.ShapeDtypeStruct((2, width, span), f32),
         ),
-        in_specs=[smem] + [vmem] * 9,
+        in_specs=[smem] + [vmem] * 10,
         out_specs=(vmem,) * 3,
         scratch_shapes=[
             pltpu.VMEM((2, 8, span), f32),
@@ -331,7 +336,7 @@
             pltpu.SMEM((32,), jnp.int32),
         ],
         compiler_params=grant(GRANT),
-    )(early, both0, key0_t, exps, gprobs, key_t, stack, stack2, mine, theirs)
+    )(early, both0, key0_t, exps, gprobs, key_t, tops, stack, stack2, mine, theirs)
 
     parts = lax.all_to_all(plane, "head", 0, 0)
     sent = jnp.sum(parts.astype(f32), axis=0).astype(bf16)

time: 78.5 us -> 78.5 us (level)
  the two profiles are of different devices: /device:TPU:72 before, /device:TPU:48 now
where the time goes in v6:
time: 78.5 us; the launch traced here: 78 us
  starting transfers between devices  30.5 us (39%)
  blocking collectives  24.2 us (31%)
  Pallas kernels  8.52 us (11%)
  waiting for transfers between devices  8.39 us (11%)
  local copies, waits for them, and re-layouts  3.74 us (5%)
  other arithmetic  1.8 us (2%)
  between operations  0.82 us (1%)
    all_to_all x1, blocking collectives, local(): lax.all_to_all(jnp.broadcast_to(fetched, (planes, rows, 2 * width)), 'hea...  12.3 us
    all_to_all x1, blocking collectives, local(): parts = lax.all_to_all(plane, 'head', 0, 0)  11.9 us
    ppermute x1, starting transfers between devices, local(): stack2 = lax.ppermute(stack, 'ctx', swap)  11.7 us
    all_to_all x1, starting transfers between devices, local(): lax.all_to_all(jnp.broadcast_to(mine, (planes, rows, 2 * width)), 'head',...  7.78 us
    ppermute x1, starting transfers between devices, local(): dq2 = lax.ppermute(dq[1], 'ctx', swap)  7.76 us
    all_to_all x1, waiting for transfers between devices, local(): lax.all_to_all(jnp.broadcast_to(mine, (planes, rows, 2 * width)), 'head',...  7.16 us
    unnamed x16, local copies, waits for them, and re-layouts  2.81 us
    pallas_call x1, Pallas kernels, local(): pl.pallas_call(queries_kernel, out_shape=jax.ShapeDtypeStruct(queries.sha...  2.2 us
  transfers between devices with their start and end apart: 6, of which 2 were waited for; matrix products, arithmetic and copies ran while one was open for 1% of the time, Pallas kernels for 7%

profile of v6, /device:TPU:48, one launch (start us, length us, event | category | flops | bytes accessed | tf_op | source)
XLA Modules:
  0.0 78.0 jit_solution(14173497471797951850)
XLA Ops:
  0.6 0.9 %pad_add_fusion.own = bf16[256,256]{1,0:T(8,128)(2,1)S(1)} fusion(bf16[256,128]{1,0:T(8,128)(2,1)} %param.9, bf16[256,128]{1,0:T(8,128)(2,1)} %param.8), kind=kLoop, calls=%fused_computation.4 | loop fusion | flops 262144 | bytes 262144 | tf_op jit(solution)/shard_map/add | solution.py:271
  1.5 0.0 copy-start.3
  1.5 0.0 copy-start.4
  1.5 0.7 collective-permute-start
  2.2 0.0 copy-start.5
  2.2 0.6 copy-done.5
  2.9 0.0 copy-start.6
  2.9 1.8 %shard_map.94 = (f32[2,256,1024]{2,1,0:T(8,128)S(1)}, bf16[128,256]{1,0:T(8,128)(2,1)S(1)}, bf16[2064,128]{1,0:T(8,128)(2,1)S(1)}, f32[8,1024]{1,0:T(8,128)S(1)}) custom-call(bf16[256,512]{1,0:T(8,128)(2,1)} %q_ref.1, bf16[256,512]{1,0:T(8,128)(2,1)} %g_ref.1, bf16[256,256]{1,0:T(8,128)(2,1)S(1)} %pad_add_fusion.own, s32[1,7]{1,0:T(1,128)S(1)} %copy-done.5), custom_call_target="tpu_custom_call" | custom-call | flops 10000000000 | bytes 4194304 | tf_op jit(solution)/shard_map/pallas_call | solution.py:290
  4.7 0.0 copy-start.1
  4.7 1.3 %copy-done.1 = f32[2,256,1024]{2,1,0:T(8,128)} copy-done((f32[2,256,1024]{2,1,0:T(8,128)}, f32[2,256,1024]{2,1,0:T(8,128)S(1)}, u32[]{:S(2)}) %copy-start.1) | copy-done | bytes 2097176
  6.0 11.7 %collective-permute-start.1 = (bf16[2064,128]{1,0:T(8,128)(2,1)S(1)}, bf16[2064,128]{1,0:T(8,128)(2,1)S(1)}, u32[]{:S(2)}, u32[]{:S(2)}) collective-permute-start(bf16[2064,128]{1,0:T(8,128)(2,1)S(1)} %get-tuple-element.22.stack), channel_id=1, source_target_pairs={{0,4},{4,0},{8,12},{12,8},{16,20},{20,16},{24,28},{28,24},{32,36},... | collective-permute-start | bytes 1585160 | tf_op jit(solution)/shard_map/ppermute | solution.py:304
  17.7 0.1 pad_add_fusion.1.info
  17.8 0.0 copy-done.3
  17.8 0.0 copy-done.4
  17.8 0.0 copy-done.6
  17.8 0.0 copy-start.2
  17.8 1.3 %shard_map.95.early = s32[52]{0:T(128)S(1)} custom-call(s32[2]{0:T(128)S(1)} %pad_add_fusion.1.info, s32[128]{0:T(128)S(1)} %copy-done.4, s32[1,7]{1,0:T(1,128)S(1)} %copy-done.6, s32[4,128]{1,0:T(4,128)S(1)} %copy-done.3), custom_call_target="tpu_custom_call" | custom-call | flops 10000000000 | bytes 4194304 | tf_op jit(solution)/shard_map/pallas_call | solution.py:281
  19.1 0.0 collective-permute-done
  19.2 12.3 %all_to_all.15.same = bf16[4,256,256]{2,1,0:T(8,128)(2,1)S(1)} all-to-all(bf16[4,256,256]{2,1,0:T(8,128)(2,1)S(1)} %broadcast_in_dim.6), channel_id=1, replica_groups=mesh['ctx'=128,'head'=4] {'head'}, dimensions={0} | all-to-all | bytes 1048576 | tf_op jit(solution)/shard_map/all_to_all | solution.py:306
  31.5 0.0 collective-permute-done.1.stack2
  31.5 1.3 %shard_map.96 = (f32[7,256,1024]{2,1,0:T(8,128)S(1)}, f32[7,256,1024]{2,1,0:T(8,128)S(1)}, bf16[4,128,256]{2,1,0:T(8,128)(2,1)S(1)}, f32[7,8,1024]{2,1,0:T(8,128)S(1)}, f32[2,8,1024]{2,1,0:T(8,128)S(1)}) custom-call(s32[52]{0:T(128)S(1)} %shard_map.95.early, bf16[2064,128]{1,0:T(8,128)(2,1)S(1)} %get-tuple-element.22.stack, ...), custom_call_target="tpu_custom_call" | custom-call | tf_op jit(solution)/shard_map/pallas_call | solution.py:307
  32.9 1.9 %collective-permute-start.2 = (f32[2,8,1024]{2,1,0:T(8,128)S(1)}, f32[2,8,1024]{2,1,0:T(8,128)S(1)}, u32[]{:S(2)}, u32[]{:S(2)}) collective-permute-start(f32[2,8,1024]{2,1,0:T(8,128)S(1)} %get-tuple-element.29.mine), channel_id=1, source_target_pairs={{0,4},{4,0},{8,12},{12,8},{16,20},{20,16},{24,28},{28,24},{32,36},... | collective-permute-start | bytes 196616 | tf_op jit(solution)/shard_map/ppermute | solution.py:321
  34.8 1.2 %collective-permute-done.2.theirs = f32[2,8,1024]{2,1,0:T(8,128)S(1)} collective-permute-done((f32[2,8,1024]{2,1,0:T(8,128)S(1)}, f32[2,8,1024]{2,1,0:T(8,128)S(1)}, u32[]{:S(2)}, u32[]{:S(2)}) %collective-permute-start.2) | collective-permute-done | bytes 65568 | tf_op jit(solution)/shard_map/ppermute | solution.py:321
  36.0 0.0 copy-done.2
  36.0 1.9 %shard_map.97 = (bf16[4,256,256]{2,1,0:T(8,128)(2,1)S(1)}, f32[256,256]{1,0:T(8,128)S(1)}, f32[2,128,1024]{2,1,0:T(8,128)S(1)}) custom-call(s32[52]{0:T(128)S(1)} %shard_map.95.early, f32[2,256,1024]{2,1,0:T(8,128)S(1)} %copy-done.2, bf16[128,256]{1,0:T(8,128)(2,1)S(1)} %get-tuple-element.21.first_key_t, f32[7,256,1024]{2,1,0:T(8,128)S(1)} %get-tuple-element.25.exps, ...), custom_call_target="tpu_custom_call" | custom-call | tf_op jit(solution)/shard_map/pallas_call | solution.py:322
  37.9 0.0 copy-start
  37.9 11.9 %all_to_all.16 = bf16[4,256,256]{2,1,0:T(8,128)(2,1)S(1)} all-to-all(bf16[4,256,256]{2,1,0:T(8,128)(2,1)S(1)} %get-tuple-element.31), channel_id=1, replica_groups=mesh['ctx'=128,'head'=4] {'head'}, dimensions={0} | all-to-all | bytes 1048576 | tf_op jit(solution)/shard_map/all_to_all | solution.py:341
  49.8 0.1 reduce_sum.12
  49.9 0.7 collective-permute-start.4
  50.6 7.8 %collective-permute-start.3 = (f32[128,1024]{1,0:T(8,128)S(1)}, f32[128,1024]{1,0:T(8,128)S(1)}, u32[]{:S(2)}, u32[]{:S(2)}) collective-permute-start(f32[128,1024]{1,0:T(8,128)S(1)} %slice_bitcast_fusion), channel_id=1, source_target_pairs={{0,4},{4,0},{8,12},{12,8},{16,20},{20,16},{24,28},{28,24},{32,36},... | collective-permute-start | bytes 1572872 | tf_op jit(solution)/shard_map/ppermute | solution.py:344
  58.4 0.0 collective-permute-done.4
  58.5 0.9 %broadcast_in_dim.7 = bf16[4,256,256]{2,1,0:T(8,128)(2,1)} broadcast(bf16[256,256]{1,0:T(8,128)(2,1)S(1)} %add_convert_fusion), dimensions={1,2} | broadcast | bytes 655360 | tf_op jit(solution)/shard_map/broadcast_in_dim | solution.py:352
  59.3 7.8 %all-to-all-start.2 = ((bf16[4,256,256]{2,1,0:T(8,128)(2,1)}), bf16[4,256,256]{2,1,0:T(8,128)(2,1)S(1)}, u32[]{:S(2)}, u32[]{:S(2)}) async-start(bf16[4,256,256]{2,1,0:T(8,128)(2,1)} %broadcast_in_dim.7), calls=%async_computation.2 | async-start | bytes 1048576 | tf_op jit(solution)/shard_map/all_to_all | solution.py:352
  67.1 0.0 collective-permute-done.3.theirs
  67.1 0.0 copy-done
  67.1 0.0 copy-start.7
  67.1 0.8 %copy-done.7 = f32[128,1024]{1,0:T(8,128)} copy-done((f32[128,1024]{1,0:T(8,128)}, f32[128,1024]{1,0:T(8,128)S(1)}, u32[]{:S(2)}) %copy-start.7) | copy-done | bytes 524312
  67.9 2.2 %shard_map.98 = bf16[256,512]{1,0:T(8,128)(2,1)} custom-call(f32[2,128,1024]{2,1,0:T(8,128)} %copy-done, f32[128,1024]{1,0:T(8,128)} %copy-done.7), custom_call_target="tpu_custom_call" | custom-call | tf_op jit(solution)/shard_map/pallas_call | solution.py:345
  70.1 7.2 %all-to-all-done.2 = bf16[4,256,256]{2,1,0:T(8,128)(2,1)S(1)} async-done(((bf16[4,256,256]{2,1,0:T(8,128)(2,1)}), bf16[4,256,256]{2,1,0:T(8,128)(2,1)S(1)}, u32[]{:S(2)}, u32[]{:S(2)}) %all-to-all-start.2) | async-done | bytes 524320 | tf_op jit(solution)/shard_map/all_to_all | solution.py:352
  77.3 0.7 fusion.1
  (3 shorter events, 0.1 us)
Async XLA Ops:
  1.5 16.3 %copy-start.3 = (s32[4,128]{1,0:T(4,128)S(1)}, s32[4,128]{1,0:T(4,128)}, u32[]{:S(2)}) copy-start(s32[4,128]{1,0:T(4,128)} %knock.1) | copy-start | bytes 6148
  1.5 16.3 %copy-start.4 = (s32[128]{0:T(128)S(1)}, s32[128]{0:T(128)}, u32[]{:S(2)}) copy-start(s32[128]{0:T(128)} %docs.1) | copy-start | bytes 1540
  1.5 17.6 %collective-permute-start = (bf16[256,256]{1,0:T(8,128)(2,1)S(1)}, bf16[256,256]{1,0:T(8,128)(2,1)S(1)}, u32[]{:S(2)}, u32[]{:S(2)}) collective-permute-start(bf16[256,256]{1,0:T(8,128)(2,1)S(1)} %pad_add_fusion.own), channel_id=1, source_target_pairs={{0,0},{8,8},{1,9},{7,15},{16,16},{9,17},{2,18},{6,22},{15,23},{24,... | collective-permute-start | bytes 393224 | tf_op jit(solution)/shard_map/ppermute | solution.py:272
  2.2 0.7 copy-start.5
  2.9 14.9 %copy-start.6 = (s32[1,7]{1,0:T(1,128)S(1)}, s32[1,7]{1,0:T(1,128)}, u32[]{:S(2)}) copy-start(s32[1,7]{1,0:T(1,128)} %pairs.3) | copy-start | bytes 88
  4.7 1.3 %copy-start.1 = (f32[2,256,1024]{2,1,0:T(8,128)}, f32[2,256,1024]{2,1,0:T(8,128)S(1)}, u32[]{:S(2)}) copy-start(f32[2,256,1024]{2,1,0:T(8,128)S(1)} %get-tuple-element.20.first) | copy-start | bytes 6291460
  6.0 25.5 %collective-permute-start.1 = (bf16[2064,128]{1,0:T(8,128)(2,1)S(1)}, bf16[2064,128]{1,0:T(8,128)(2,1)S(1)}, u32[]{:S(2)}, u32[]{:S(2)}) collective-permute-start(bf16[2064,128]{1,0:T(8,128)(2,1)S(1)} %get-tuple-element.22.stack), channel_id=1, source_target_pairs={{0,4},{4,0},{8,12},{12,8},{16,20},{20,16},{24,28},{28,24},{32,36},... | collective-permute-start | bytes 1585160 | tf_op jit(solution)/shard_map/ppermute | solution.py:304
  17.8 18.2 %copy-start.2 = (f32[2,256,1024]{2,1,0:T(8,128)S(1)}, f32[2,256,1024]{2,1,0:T(8,128)}, u32[]{:S(2)}) copy-start(f32[2,256,1024]{2,1,0:T(8,128)} %copy-done.1) | copy-start | bytes 6291460
  32.9 3.1 %collective-permute-start.2 = (f32[2,8,1024]{2,1,0:T(8,128)S(1)}, f32[2,8,1024]{2,1,0:T(8,128)S(1)}, u32[]{:S(2)}, u32[]{:S(2)}) collective-permute-start(f32[2,8,1024]{2,1,0:T(8,128)S(1)} %get-tuple-element.29.mine), channel_id=1, source_target_pairs={{0,4},{4,0},{8,12},{12,8},{16,20},{20,16},{24,28},{28,24},{32,36},... | collective-permute-start | bytes 196616 | tf_op jit(solution)/shard_map/ppermute | solution.py:321
  37.9 29.2 %copy-start = (f32[2,128,1024]{2,1,0:T(8,128)}, f32[2,128,1024]{2,1,0:T(8,128)S(1)}, u32[]{:S(2)}) copy-start(f32[2,128,1024]{2,1,0:T(8,128)S(1)} %get-tuple-element.30.mine) | copy-start | bytes 3145732
  49.9 8.5 %collective-permute-start.4 = (bf16[256,256]{1,0:T(8,128)(2,1)S(1)}, bf16[256,256]{1,0:T(8,128)(2,1)S(1)}, u32[]{:S(2)}, u32[]{:S(2)}) collective-permute-start(bf16[256,256]{1,0:T(8,128)(2,1)S(1)} %reduce_sum.12), channel_id=1, source_target_pairs={{9,1},{15,7},{17,9},{18,2},{22,6},{23,15},{25,17},{26,10},{27,3},{... | collective-permute-start | bytes 393224 | tf_op jit(solution)/shard_map/ppermute | solution.py:343
  50.6 16.5 %collective-permute-start.3 = (f32[128,1024]{1,0:T(8,128)S(1)}, f32[128,1024]{1,0:T(8,128)S(1)}, u32[]{:S(2)}, u32[]{:S(2)}) collective-permute-start(f32[128,1024]{1,0:T(8,128)S(1)} %slice_bitcast_fusion), channel_id=1, source_target_pairs={{0,4},{4,0},{8,12},{12,8},{16,20},{20,16},{24,28},{28,24},{32,36},... | collective-permute-start | bytes 1572872 | tf_op jit(solution)/shard_map/ppermute | solution.py:344
  59.3 18.0 %all-to-all-start.2 = ((bf16[4,256,256]{2,1,0:T(8,128)(2,1)}), bf16[4,256,256]{2,1,0:T(8,128)(2,1)S(1)}, u32[]{:S(2)}, u32[]{:S(2)}) async-start(bf16[4,256,256]{2,1,0:T(8,128)(2,1)} %broadcast_in_dim.7), calls=%async_computation.2 | async-start | bytes 1048576 | tf_op jit(solution)/shard_map/all_to_all | solution.py:352
  67.1 0.8 %copy-start.7 = (f32[128,1024]{1,0:T(8,128)}, f32[128,1024]{1,0:T(8,128)S(1)}, u32[]{:S(2)}) copy-start(f32[128,1024]{1,0:T(8,128)S(1)} %collective-permute-done.3.theirs) | copy-start | bytes 1572868
